TPU v7x, 32 devices: a whole 2x2x4 slice. The times are simulated.
32 devices in a mesh: dp: 16 (over z, x, core), tensor: 2 (over y).
Axes of the slice: x: 2, y: 2, z: 4, core: 2. Of those that a mesh axis runs over, the one named last changes fastest.
Arguments:
- tokens_in: float32 [16384, 1536], P(('dp', 'tensor')), may hold values from -6 to 6
- prefix_len: int32 [16], P('dp'), may hold values from 102 to 512
- attn_gain: float32 [1536], replicated, may hold values from 0.1 to 1.9
- query_weight: bfloat16 [1536, 1536], P(None, 'tensor'), may hold values from -0.15625 to 0.15625
- key_weight: bfloat16 [1536, 1536], P(None, 'tensor'), may hold values from -0.15625 to 0.15625
- value_weight: bfloat16 [1536, 1536], P(None, 'tensor'), may hold values from -0.15625 to 0.15625
- forget_weight: bfloat16 [1536, 24], P(None, 'tensor'), may hold values from -0.15625 to 0.15625
- forget_bias: float32 [24], P('tensor'), may hold values from 1.5 to 7
- outgate_weight: bfloat16 [1536, 1536], P(None, 'tensor'), may hold values from -0.15625 to 0.15625
- output_weight: bfloat16 [1536, 1536], P('tensor'), may hold values from -0.625 to 0.625
- mlp_gain: float32 [1536], replicated, may hold values from 0.1 to 1.9
- gate_weight: bfloat16 [1536, 4096], P(None, 'tensor'), may hold values from -0.15625 to 0.15625
- up_weight: bfloat16 [1536, 4096], P(None, 'tensor'), may hold values from -0.15625 to 0.15625
- down_weight: bfloat16 [4096, 1536], P('tensor'), may hold values from -0.09375 to 0.09375
- out_grad: float32 [16384, 1536], P(('dp', 'tensor')), may hold values from -6 to 6
Outputs:
- layer_out: float32 [16384, 1536], P(('dp', 'tensor'))
- input_grad: float32 [16384, 1536], P(('dp', 'tensor'))
- attn_gain_grad: float32 [1536], replicated
- query_grad: float32 [1536, 1536], P('dp', 'tensor')
- key_grad: float32 [1536, 1536], P('dp', 'tensor')
- value_grad: float32 [1536, 1536], P('dp', 'tensor')
- forget_grad: float32 [1536, 24], P('dp', 'tensor')
- bias_grad: float32 [24], replicated
- outgate_grad: float32 [1536, 1536], P('dp', 'tensor')
- output_grad: float32 [1536, 1536], P('tensor', 'dp')
- mlp_gain_grad: float32 [1536], replicated
- gate_grad: float32 [1536, 4096], P('dp', 'tensor')
- up_grad: float32 [1536, 4096], P('dp', 'tensor')
- down_grad: float32 [4096, 1536], P('tensor', 'dp')
Inputs may be any that keep to these rules, and one draw needn't show every extreme that they name: `prefix_len`: one prefix length for each sequence, drawn independently.
All inputs are finite; a program needn't handle non-finite values.
Results may differ from a plain program's by a relative error of at most 0.025.
Values may be sent and summed in bfloat16 or wider, within the bound.
A program may use at most 320 MiB of HBM per device.

v0:
```python
import jax
import jax.numpy as jnp
from jax import lax
from jax.sharding import PartitionSpec as P

H = 24
HD = 64
LEN = 1024
BLOCK = 1024


epsilon = 1e-06


def dot_trans(left, right):
    return lax.dot_general(
        left, right, (((1,), (1,)), ((), ())), preferred_element_type=jnp.float32
    )


def weight_term(left, right):
    return lax.dot_general(
        left, right, (((0,), (0,)), ((), ())), preferred_element_type=jnp.float32
    )


def rms_rows(rows, gain):
    inverse = lax.rsqrt(jnp.mean(rows * rows, axis=-1, keepdims=True) + epsilon)
    return (inverse, rows * inverse * gain)


def rms_back(rows, inverse, gain, grad):
    scaled = grad * gain
    gain_term = jnp.sum(grad * rows * inverse, axis=0)
    row_term = inverse * scaled - rows * inverse**3 * jnp.mean(
        scaled * rows, axis=-1, keepdims=True
    )
    return (row_term, gain_term)


def key_count(qblock, prefix_size, block_rows):
    prefix_blocks = (prefix_size + block_rows - 1) // block_rows
    return jnp.where(
        qblock * block_rows < prefix_size, jnp.maximum(qblock + 1, prefix_blocks), qblock + 1
    )


def block_scores(query_blk, key_blk, decay_q, decay_k, query_pos, key_pos, prefix_size):
    raw_scores = jnp.einsum(
        "qhd,khd->hqk", query_blk, key_blk, preferred_element_type=jnp.float32
    ) * HD ** (-0.5)
    causal = key_pos[None, :] <= query_pos[:, None]
    allowed = causal | (query_pos[:, None] < prefix_size) & (key_pos[None, :] < prefix_size)
    decay_gap = jnp.transpose(decay_q)[:, :, None] - jnp.transpose(decay_k)[:, None, :]
    scores = jnp.where(
        allowed[None], raw_scores + jnp.where(causal[None], decay_gap, -decay_gap), -1e30
    )
    return (scores, causal)


def attend_sequence(queries, keys_all, values_all, decay, prefix_size):
    block_rows = BLOCK
    heads_here = queries.shape[1]
    outputs, totals = ([], [])
    query_blk = queries
    decay_q = decay
    query_pos = 0 + jnp.arange(block_rows, dtype=jnp.int32)
    amount = key_count(0, prefix_size, block_rows)

    def scores_at(kblock, query_blk=query_blk, decay_q=decay_q, query_pos=query_pos):
        key_off = kblock * block_rows
        key_pos = key_off + jnp.arange(block_rows, dtype=jnp.int32)
        scores, causal = block_scores(
            query_blk, keys_all, decay_q, decay, query_pos, key_pos, prefix_size
        )
        return (scores, key_off)

    def stats_step(kblock, loop_state, scores_at=scores_at):
        running_max, running_sum = loop_state
        scores, key_off = scores_at(kblock)
        new_max = jnp.maximum(running_max, jnp.max(scores, axis=-1))
        running_sum = running_sum * jnp.exp(running_max - new_max) + jnp.sum(
            jnp.exp(scores - new_max[:, :, None]), axis=-1
        )
        return (new_max, running_sum)

    start_state = (
        jnp.full((heads_here, block_rows), -1e30, jnp.float32),
        jnp.zeros((heads_here, block_rows), jnp.float32),
    )
    running_max, running_sum = lax.fori_loop(0, amount, stats_step, start_state)
    log_total = running_max + jnp.log(running_sum)

    def value_step(kblock, weighted, scores_at=scores_at, log_total=log_total):
        scores, key_off = scores_at(kblock)
        attn_probs = jnp.exp(scores - log_total[:, :, None]).astype(jnp.bfloat16)
        return weighted + jnp.einsum(
            "hqk,khd->qhd", attn_probs, values_all, preferred_element_type=jnp.float32
        )

    weighted = lax.fori_loop(
        0, amount, value_step, jnp.zeros((block_rows, heads_here, HD), jnp.float32)
    )
    outputs.append(weighted)
    totals.append(jnp.transpose(log_total))
    return (jnp.concatenate(outputs, axis=0), jnp.concatenate(totals, axis=0))


def attend_back(queries, keys_all, values_all, decay, log_total, grad_out, row_delta, prefix_size):
    block_rows = BLOCK
    heads_here = queries.shape[1]
    score_scale = HD ** (-0.5)
    grad_keys = jnp.zeros((LEN, heads_here, HD), jnp.float32)
    grad_values = jnp.zeros((LEN, heads_here, HD), jnp.float32)
    decay_keys = jnp.zeros((LEN, heads_here), jnp.float32)
    query_parts, decay_parts = ([], [])
    query_blk = queries[0:block_rows]
    decay_q = decay[0:block_rows]
    grad_blk = grad_out[0:block_rows]
    total_q = jnp.transpose(log_total[0:block_rows])
    delta_q = jnp.transpose(row_delta[0:block_rows])
    query_pos = 0 + jnp.arange(block_rows, dtype=jnp.int32)
    amount = key_count(0, prefix_size, block_rows)

    def grad_step(
        kblock,
        loop_state,
        query_blk=query_blk,
        decay_q=decay_q,
        grad_blk=grad_blk,
        total_q=total_q,
        delta_q=delta_q,
        query_pos=query_pos,
    ):
        grad_qblk, decay_qblk, keys_acc, values_acc, decay_acc = loop_state
        key_off = kblock * block_rows
        key_blk = lax.dynamic_slice_in_dim(keys_all, key_off, block_rows, 0)
        value_blk = lax.dynamic_slice_in_dim(values_all, key_off, block_rows, 0)
        decay_k = lax.dynamic_slice_in_dim(decay, key_off, block_rows, 0)
        key_pos = key_off + jnp.arange(block_rows, dtype=jnp.int32)
        scores, causal = block_scores(
            query_blk, key_blk, decay_q, decay_k, query_pos, key_pos, prefix_size
        )
        probs = jnp.exp(scores - total_q[:, :, None])
        grad_probs = jnp.einsum(
            "qhd,khd->hqk", grad_blk, value_blk, preferred_element_type=jnp.float32
        )
        grad_scores = (probs * (grad_probs - delta_q[:, :, None])).astype(jnp.bfloat16)
        grad_qblk = (
            grad_qblk
            + jnp.einsum("hqk,khd->qhd", grad_scores, key_blk, preferred_element_type=jnp.float32)
            * score_scale
        )
        key_part = (
            jnp.einsum("hqk,qhd->khd", grad_scores, query_blk, preferred_element_type=jnp.float32)
            * score_scale
        )
        value_part = jnp.einsum(
            "hqk,qhd->khd", probs.astype(jnp.bfloat16), grad_blk, preferred_element_type=jnp.float32
        )
        signed = jnp.where(
            causal[None], grad_scores.astype(jnp.float32), -grad_scores.astype(jnp.float32)
        )
        decay_qblk = decay_qblk + jnp.transpose(jnp.sum(signed, axis=-1))
        keys_acc = lax.dynamic_update_slice_in_dim(keys_acc, keys_acc + key_part, key_off, 0)
        values_acc = lax.dynamic_update_slice_in_dim(
            values_acc, values_acc + value_part, key_off, 0
        )
        decay_acc = lax.dynamic_update_slice_in_dim(
            decay_acc, decay_acc - jnp.transpose(jnp.sum(signed, axis=1)), key_off, 0
        )
        return (grad_qblk, decay_qblk, keys_acc, values_acc, decay_acc)

    start_state = (
        jnp.zeros((block_rows, heads_here, HD), jnp.float32),
        jnp.zeros((block_rows, heads_here), jnp.float32),
        grad_keys,
        grad_values,
        decay_keys,
    )
    grad_qblk, decay_qblk, grad_keys, grad_values, decay_keys = lax.fori_loop(
        0, amount, grad_step, start_state
    )
    query_parts.append(grad_qblk)
    decay_parts.append(decay_qblk)
    return (
        jnp.concatenate(query_parts, axis=0),
        grad_keys,
        grad_values,
        jnp.concatenate(decay_parts, axis=0) + decay_keys,
    )


def local(
    tokens_in,
    prefix_len,
    attn_gain,
    query_weight,
    key_weight,
    value_weight,
    forget_weight,
    forget_bias,
    outgate_weight,
    output_weight,
    mlp_gain,
    gate_weight,
    up_weight,
    down_weight,
    out_grad,
):
    row_count = tokens_in.shape[0]
    heads_here = forget_weight.shape[1]
    sequences = prefix_len.shape[0]
    tokens = row_count * lax.axis_size("tensor")
    split_shape = (sequences, LEN, heads_here, HD)
    scale_one, normed_rows = rms_rows(tokens_in, attn_gain)
    normed = lax.all_gather(normed_rows.astype(jnp.bfloat16), "tensor", axis=0, tiled=True)
    queries = jnp.dot(normed, query_weight, preferred_element_type=jnp.float32).astype(jnp.bfloat16)
    keys_all = jnp.dot(normed, key_weight, preferred_element_type=jnp.float32).astype(jnp.bfloat16)
    values_all = jnp.dot(normed, value_weight, preferred_element_type=jnp.float32).astype(
        jnp.bfloat16
    )
    forget_logit = jnp.dot(normed, forget_weight, preferred_element_type=jnp.float32) + forget_bias
    decay = jnp.cumsum(jax.nn.log_sigmoid(forget_logit).reshape(sequences, LEN, heads_here), axis=1)
    outgate = jax.nn.sigmoid(jnp.dot(normed, outgate_weight, preferred_element_type=jnp.float32))

    def forward_seq(loop_state, slices):
        attended_seq, total_seq = attend_sequence(
            slices[0], slices[1], slices[2], slices[3], slices[4]
        )
        return (loop_state, (attended_seq, total_seq))

    _, (attended, log_total) = lax.scan(
        forward_seq,
        jnp.zeros((), jnp.float32),
        (
            queries.reshape(split_shape),
            keys_all.reshape(split_shape),
            values_all.reshape(split_shape),
            decay,
            prefix_len,
        ),
    )
    attended = attended.reshape(tokens, heads_here * HD)
    mixed = (outgate * attended).astype(jnp.bfloat16)
    hidden_rows = tokens_in + lax.psum_scatter(
        jnp.dot(
            lax.slice_in_dim(mixed, 0, row_count * lax.axis_size("tensor"), axis=0),
            output_weight,
            preferred_element_type=jnp.float32,
        ).astype(jnp.bfloat16),
        "tensor",
        scatter_dimension=0,
        tiled=True,
    ).astype(jnp.float32)
    scale_two, normed_two_rows = rms_rows(hidden_rows, mlp_gain)
    normed_two = lax.all_gather(normed_two_rows.astype(jnp.bfloat16), "tensor", axis=0, tiled=True)
    gate = jnp.dot(normed_two, gate_weight, preferred_element_type=jnp.float32)
    upward = jnp.dot(normed_two, up_weight, preferred_element_type=jnp.float32)
    active = (jax.nn.silu(gate) * upward).astype(jnp.bfloat16)
    layer_out = hidden_rows + lax.psum_scatter(
        jnp.dot(
            lax.slice_in_dim(active, 0, row_count * lax.axis_size("tensor"), axis=0),
            down_weight,
            preferred_element_type=jnp.float32,
        ).astype(jnp.bfloat16),
        "tensor",
        scatter_dimension=0,
        tiled=True,
    ).astype(jnp.float32)
    grad_branch = lax.all_gather(out_grad.astype(jnp.bfloat16), "tensor", axis=0, tiled=True)
    grad_active = dot_trans(grad_branch, down_weight).astype(jnp.bfloat16)
    down_part = weight_term(active, grad_branch)
    gate_sigmoid = jax.nn.sigmoid(gate)
    grad_act_f = grad_active.astype(jnp.float32)
    grad_gate = (grad_act_f * upward * gate_sigmoid * (1.0 + gate * (1.0 - gate_sigmoid))).astype(
        jnp.bfloat16
    )
    grad_upward = (grad_act_f * gate * gate_sigmoid).astype(jnp.bfloat16)
    gate_part = weight_term(normed_two, grad_gate)
    up_part = weight_term(normed_two, grad_upward)
    grad_normed_two = lax.psum_scatter(
        (
            dot_trans(
                lax.slice_in_dim(grad_gate, 0, row_count * lax.axis_size("tensor"), axis=0),
                gate_weight,
            )
            + dot_trans(
                lax.slice_in_dim(grad_upward, 0, row_count * lax.axis_size("tensor"), axis=0),
                up_weight,
            )
        ).astype(jnp.bfloat16),
        "tensor",
        scatter_dimension=0,
        tiled=True,
    ).astype(jnp.float32)
    grad_hidden, mlp_gain_part = rms_back(hidden_rows, scale_two, mlp_gain, grad_normed_two)
    grad_hidden = grad_hidden + out_grad
    grad_mid = lax.all_gather(grad_hidden.astype(jnp.bfloat16), "tensor", axis=0, tiled=True)
    grad_mixed = dot_trans(grad_mid, output_weight).astype(jnp.bfloat16)
    output_part = weight_term(mixed, grad_mid)
    grad_mixed_f = grad_mixed.astype(jnp.float32)
    grad_attended = (grad_mixed_f * outgate).astype(jnp.bfloat16)
    grad_outlogit = (grad_mixed_f * attended * outgate * (1.0 - outgate)).astype(jnp.bfloat16)
    row_delta = jnp.sum(
        (grad_attended.astype(jnp.float32) * attended).reshape(tokens, heads_here, HD), axis=-1
    )

    def backward_seq(loop_state, slices):
        grads_seq = attend_back(
            slices[0], slices[1], slices[2], slices[3], slices[4], slices[5], slices[6], slices[7]
        )
        return (loop_state, grads_seq)

    _, (grad_query, grad_key, grad_value, grad_decay) = lax.scan(
        backward_seq,
        jnp.zeros((), jnp.float32),
        (
            queries.reshape(split_shape),
            keys_all.reshape(split_shape),
            values_all.reshape(split_shape),
            decay,
            log_total,
            grad_attended.reshape(split_shape),
            row_delta.reshape(sequences, LEN, heads_here),
            prefix_len,
        ),
    )
    grad_query = grad_query.reshape(tokens, heads_here * HD).astype(jnp.bfloat16)
    grad_key = grad_key.reshape(tokens, heads_here * HD).astype(jnp.bfloat16)
    grad_value = grad_value.reshape(tokens, heads_here * HD).astype(jnp.bfloat16)
    later_sum = jnp.flip(jnp.cumsum(jnp.flip(grad_decay, axis=1), axis=1), axis=1).reshape(
        tokens, heads_here
    )
    grad_forget = (later_sum * jax.nn.sigmoid(-forget_logit)).astype(jnp.bfloat16)
    bias_part = jnp.sum(grad_forget.astype(jnp.float32), axis=0)
    query_part = weight_term(normed, grad_query)
    key_part = weight_term(normed, grad_key)
    value_part = weight_term(normed, grad_value)
    forget_part = weight_term(normed, grad_forget)
    outgate_part = weight_term(normed, grad_outlogit)
    total = dot_trans(
        lax.slice_in_dim(grad_query, 0, row_count * lax.axis_size("tensor"), axis=0), query_weight
    )
    total = total + dot_trans(grad_key, key_weight)
    total = total + dot_trans(grad_value, value_weight)
    total = total + dot_trans(grad_forget, forget_weight)
    grad_normed = lax.psum_scatter(
        (
            total
            + dot_trans(
                lax.slice_in_dim(grad_outlogit, 0, row_count * lax.axis_size("tensor"), axis=0),
                outgate_weight,
            )
        ).astype(jnp.bfloat16),
        "tensor",
        scatter_dimension=0,
        tiled=True,
    ).astype(jnp.float32)
    input_part, attn_gain_part = rms_back(tokens_in, scale_one, attn_gain, grad_normed)
    input_grad = grad_hidden + input_part
    all_sums = (
        lax.psum_scatter(
            query_part.astype(jnp.bfloat16), "dp", scatter_dimension=0, tiled=True
        ).astype(jnp.float32),
        lax.psum_scatter(
            key_part.astype(jnp.bfloat16), "dp", scatter_dimension=0, tiled=True
        ).astype(jnp.float32),
        lax.psum_scatter(
            value_part.astype(jnp.bfloat16), "dp", scatter_dimension=0, tiled=True
        ).astype(jnp.float32),
        lax.psum_scatter(
            forget_part.astype(jnp.bfloat16), "dp", scatter_dimension=0, tiled=True
        ).astype(jnp.float32),
        lax.psum_scatter(
            outgate_part.astype(jnp.bfloat16), "dp", scatter_dimension=0, tiled=True
        ).astype(jnp.float32),
        lax.psum_scatter(
            output_part.astype(jnp.bfloat16), "dp", scatter_dimension=1, tiled=True
        ).astype(jnp.float32),
        lax.psum_scatter(
            gate_part.astype(jnp.bfloat16), "dp", scatter_dimension=0, tiled=True
        ).astype(jnp.float32),
        lax.psum_scatter(
            up_part.astype(jnp.bfloat16), "dp", scatter_dimension=0, tiled=True
        ).astype(jnp.float32),
        lax.psum_scatter(
            down_part.astype(jnp.bfloat16), "dp", scatter_dimension=1, tiled=True
        ).astype(jnp.float32),
    )
    (
        query_grad,
        key_grad,
        value_grad,
        forget_grad,
        outgate_grad,
        output_grad,
        gate_grad,
        up_grad,
        down_grad,
    ) = all_sums
    bias_full = lax.dynamic_update_slice_in_dim(
        jnp.zeros((H,), jnp.float32), bias_part, lax.axis_index("tensor") * heads_here, 0
    )
    attn_gain_grad, mlp_gain_grad, bias_grad = lax.psum(
        (attn_gain_part, mlp_gain_part, bias_full), ("dp", "tensor")
    )
    return (
        layer_out,
        input_grad,
        attn_gain_grad,
        query_grad,
        key_grad,
        value_grad,
        forget_grad,
        bias_grad,
        outgate_grad,
        output_grad,
        mlp_gain_grad,
        gate_grad,
        up_grad,
        down_grad,
    )


def solution(mesh):
    in_specs = (
        P(("dp", "tensor"), None),
        P("dp"),
        P(),
        P(None, "tensor"),
        P(None, "tensor"),
        P(None, "tensor"),
        P(None, "tensor"),
        P("tensor"),
        P(None, "tensor"),
        P("tensor", None),
        P(),
        P(None, "tensor"),
        P(None, "tensor"),
        P("tensor", None),
        P(("dp", "tensor"), None),
    )
    out_specs = (
        P(("dp", "tensor"), None),
        P(("dp", "tensor"), None),
        P(),
        P("dp", "tensor"),
        P("dp", "tensor"),
        P("dp", "tensor"),
        P("dp", "tensor"),
        P(),
        P("dp", "tensor"),
        P("tensor", "dp"),
        P(),
        P("dp", "tensor"),
        P("dp", "tensor"),
        P("tensor", "dp"),
    )
    return jax.shard_map(local, mesh=mesh, in_specs=in_specs, out_specs=out_specs, check_vma=False)
```

profile of v0, /device:TPU:0, one launch (start us, length us, event | category | flops | bytes accessed | tf_op | source)
XLA Modules:
  0.0 1273.6 jit_solution(1734301184533579652)
XLA Ops:
  13.0 47.1 %all-gather.5.cloned.1.call-done = bf16[1024,1536]{1,0:T(8,128)(2,1)} async-done(((bf16[512,1536]{1,0:T(8,128)(2,1)}), bf16[1024,1536]{1,0:T(8,128)(2,1)}) %all-gather.5.cloned.1.call-update) | async-done | bytes 3145744 | tf_op jit(solution)/shard_map/all_gather | solution.py:217
  79.1 58.7 %while.72 = (s32[]{:T(128)}, f32[12,1024]{1,0:T(8,128)S(1)}, f32[12,1024]{1,0:T(8,128)}, s32[]{:T(128)}, s32[]{:T(128)}, /*index=5*/bf16[1024,12,64]{0,2,1:T(8,1...) while((s32[]{:T(128)}, f32[12,1024]{1,0:T(8,128)S(1)}, ...), condition=%wide.region_6.7_spmd.clone.clone, body=%wide.region_3.6_spmd.clone.clone.sunk | while | flops 1802530816 | bytes 115044504 | solution.py:91
  81.5 25.9 %fusion.166 = (f32[12,1024]{1,0:T(8,128)S(1)}, f32[12,1024,1024]{1,2,0:T(8,128)}) fusion(f32[12,1024]{1,0:T(8,128)} %bitcast.169, pred[1024,1024]{0,1:T(8,128)(4,1)S(1)} %get-tuple-element.761, pred[1024,1024]{0,1:T(8,128)(4,1)S(1)} %get-tuple-element.762, bf16[1024,12,64]{0,2,1:T(8,128)(2,1)} %get-tuple-element.825, ...), kind=kOutput, calls=%fused_computation.7.clone.1 | convolution fusion | flops 1698680832 | bytes 55672832 | tf_op jit(solution)/shard_map/while/body/eval_jaxpr/while/body/qhd,khd->hqk/dot_general | solution.py:49
  107.4 28.8 %exponential_reduce_fusion.2 = f32[12,1024]{1,0:T(8,128)} fusion(f32[12,1024,1024]{1,2,0:T(8,128)} %get-tuple-element.764, f32[12,1024]{1,0:T(8,128)S(1)} %max.27, f32[12,1024]{1,0:T(8,128)} %bitcast.169, pred[1024,1024]{0,1:T(8,128)(4,1)} %copy-done.4, pred[1024,1024]{0,1:T(8,128)(4,1)S(1)} %get-tuple-element.762), kind=kLoop, calls=%fused_computation.6.clone.1 | loop fusion | flops 100651008 | bytes 52576256 | tf_op jit(solution)/shard_map/while/body/eval_jaxpr/while/body/reduce_sum | solution.py:82
  147.1 33.3 %while.73 = (s32[]{:T(128)}, f32[1024,12,64]{0,2,1:T(8,128)}, s32[]{:T(128)}, s32[]{:T(128)}, bf16[1024,12,64]{0,2,1:T(8,128)(2,1)}, /*index=5*/bf16[1024,12,64]...) while((s32[]{:T(128)}, f32[1024,12,64]{0,2,1:T(8,128)}, ...), condition=%wide.region_8.9_spmd.clone.clone, body=%wide.region_7.8_spmd.clone.clone.sunk | while | flops 3325825024 | bytes 15315077 | solution.py:101
  150.4 30.1 %bitcast_add_fusion.9 = f32[1024,12,64]{0,2,1:T(8,128)} fusion(f32[1024,12,64]{0,2,1:T(8,128)} %get-tuple-element.842, bf16[1024,12,64]{0,2,1:T(8,128)(2,1)} %get-tuple-element.860, f32[12,1024]{1,0:T(8,128)S(1)} %get-tuple-element.859, f32[12,1024]{1,0:T(8,128)} %bitcast.174, pred[1024,1024]{1,0:T(8,128)(4,1)} %get-tuple-element.776, ...), kind=kOutput, calls=%fused_computation.26.clone.1 | convolution fusion | flops 3322675200 | bytes 13205504 | tf_op jit(solution)/shard_map/while/body/eval_jaxpr/while/body/hqk,khd->qhd/dot_general | solution.py:97
  197.8 39.8 %reduce-scatter.16.cloned.1.call-done = bf16[512,1536]{1,0:T(8,128)(2,1)} async-done(((bf16[1024,1536]{1,0:T(8,128)(2,1)}), bf16[512,1536]{1,0:T(8,128)(2,1)}) %reduce-scatter.16.cloned.1.call-update) | async-done | bytes 1572880 | tf_op jit(solution)/shard_map/reduce_scatter | solution.py:246
  243.6 40.5 %all-gather.9.cloned.1.call-done = bf16[1024,1536]{1,0:T(8,128)(2,1)} async-done(((bf16[512,1536]{1,0:T(8,128)(2,1)}), bf16[1024,1536]{1,0:T(8,128)(2,1)}) %all-gather.9.cloned.1.call-update) | async-done | bytes 3145744 | tf_op jit(solution)/shard_map/all_gather | solution.py:271
  295.2 35.2 %all-gather.7.cloned.1.call-done = bf16[1024,1536]{1,0:T(8,128)(2,1)} async-done(((bf16[512,1536]{1,0:T(8,128)(2,1)}), bf16[1024,1536]{1,0:T(8,128)(2,1)}) %all-gather.7.cloned.1.call-update) | async-done | bytes 3145744 | tf_op jit(solution)/shard_map/all_gather | solution.py:257
  390.3 32.2 %reduce-scatter.20.cloned.1.call-done = bf16[512,1536]{1,0:T(8,128)(2,1)} async-done(((bf16[1024,1536]{1,0:T(8,128)(2,1)}), bf16[512,1536]{1,0:T(8,128)(2,1)}) %reduce-scatter.20.cloned.1.call-update) | async-done | bytes 1572880 | tf_op jit(solution)/shard_map/reduce_scatter | solution.py:282
  426.5 41.6 %reduce-scatter.18.cloned.1.call-done = bf16[512,1536]{1,0:T(8,128)(2,1)} async-done(((bf16[1024,1536]{1,0:T(8,128)(2,1)}), bf16[512,1536]{1,0:T(8,128)(2,1)}) %reduce-scatter.18.cloned.1.call-update) | async-done | bytes 1572880 | tf_op jit(solution)/shard_map/reduce_scatter | solution.py:261
  535.5 129.8 %while.74 = (s32[]{:T(128)}, f32[1024,12,64]{0,2,1:T(8,128)}, f32[1024,12]{0,1:T(8,128)S(1)}, f32[1024,12,64]{0,2,1:T(8,128)}, f32[1024,12,64]{0,2,1:T(8,128)}, ...) while((s32[]{:T(128)}, f32[1024,12,64]{0,2,1:T(8,128)}, ...), condition=%wide.region_18.19_spmd.clone.clone, body=%wide.region_15.18_spmd.clone.clone.sunk | while | flops 8349552640 | bytes 286388512 | solution.py:181
  539.3 21.7 %fusion.181 = f32[12,1024,1024]{2,1,0:T(8,128)} fusion(bf16[1024,12,64]{0,2,1:T(8,128)(2,1)} %get-tuple-element.905, bf16[1024,12,64]{0,2,1:T(8,128)(2,1)S(1)} %get-tuple-element.906), kind=kOutput, calls=%fused_computation.140.clone.1 | convolution fusion | flops 1610612736 | bytes 53477376 | tf_op jit(solution)/shard_map/while/body/eval_jaxpr/while/body/qhd,khd->hqk/dot_general | solution.py:49
  561.1 31.4 %bitcast_add_fusion.12 = f32[1024,12,64]{0,2,1:T(8,128)} fusion(f32[1024,12,64]{0,2,1:T(8,128)} %get-tuple-element.884, bf16[1024,12,64]{0,2,1:T(8,128)(2,1)} %get-tuple-element.909, f32[12,1024,1024]{2,1,0:T(8,128)} %fusion.181, f32[12,1024]{1,0:T(8,128)S(1)} %get-tuple-element.908, f32[12,1024]{1,0:T(8,128)} %bitcast.188, ...), kind=kOutput, calls=%fused_computation.47.clone.1 | convolution fusion | flops 1712062464 | bytes 60391424 | tf_op jit(solution)/shard_map/while/body/eval_jaxpr/while/body/hqk,qhd->khd/dot_general | solution.py:158
  592.6 41.1 %fusion.182 = (f32[12,1024]{1,0:T(8,128)S(1)}, f32[12,1024]{1,0:T(8,128)S(1)}, bf16[12,1024,1024]{2,1,0:T(8,128)(2,1)}) fusion(pred[1024,1024]{1,0:T(8,128)(4,1)S(1)} %copy-done.8, f32[12,1024]{1,0:T(8,128)S(1)} %get-tuple-element.911, bf16[1024,12,64]{0,2,1:T(8,128)(2,1)S(1)} %copy-done.10, bf16[1024,12,64]{0,2,1:T(8,128)(2,1)S(1)} %copy-done.34, ...), kind=kOutput, calls=%fused_computation.38.clone.1 | convolution fusion | flops 1799331840 | bytes 80986112 | tf_op jit(solution)/shard_map/while/body/eval_jaxpr/while/body/qhd,khd->hqk/dot_general | solution.py:145
  740.5 44.1 %reduce-scatter.36.cloned.1.call-done = bf16[96,2048]{1,0:T(8,128)(2,1)} async-done(((bf16[1536,2048]{1,0:T(8,128)(2,1)}), bf16[96,2048]{1,0:T(8,128)(2,1)}) %reduce-scatter.36.cloned.1.call-update) | async-done | bytes 393232 | tf_op jit(solution)/shard_map/reduce_scatter | solution.py:384
  786.5 56.6 %reduce-scatter.40.cloned.1.call-done = bf16[96,12]{1,0:T(8,128)(2,1)} async-done(((bf16[1536,12]{1,0:T(8,128)(2,1)}), bf16[96,12]{1,0:T(8,128)(2,1)}) %reduce-scatter.40.cloned.1.call-update) | async-done | bytes 2320
  844.6 64.5 %reduce-scatter.32.cloned.1.call-done = bf16[768,96]{0,1:T(8,128)(2,1)} async-done(((bf16[768,1536]{0,1:T(8,128)(2,1)}), bf16[768,96]{0,1:T(8,128)(2,1)}) %reduce-scatter.32.cloned.1.call-update) | async-done | bytes 147472 | tf_op jit(solution)/shard_map/reduce_scatter | solution.py:378
  910.8 64.3 %reduce-scatter.28.cloned.1.call-done = bf16[96,768]{1,0:T(8,128)(2,1)} async-done(((bf16[1536,768]{1,0:T(8,128)(2,1)}), bf16[96,768]{1,0:T(8,128)(2,1)}) %reduce-scatter.28.cloned.1.call-update) | async-done | bytes 147472 | tf_op jit(solution)/shard_map/reduce_scatter | solution.py:369
  976.7 64.2 %reduce-scatter.26.cloned.1.call-done = bf16[96,768]{1,0:T(8,128)(2,1)} async-done(((bf16[1536,768]{1,0:T(8,128)(2,1)}), bf16[96,768]{1,0:T(8,128)(2,1)}) %reduce-scatter.26.cloned.1.call-update) | async-done | bytes 147472 | tf_op jit(solution)/shard_map/reduce_scatter | solution.py:366
  1042.6 64.2 %reduce-scatter.24.cloned.1.call-done = bf16[96,768]{1,0:T(8,128)(2,1)} async-done(((bf16[1536,768]{1,0:T(8,128)(2,1)}), bf16[96,768]{1,0:T(8,128)(2,1)}) %reduce-scatter.24.cloned.1.call-update) | async-done | bytes 147472 | tf_op jit(solution)/shard_map/reduce_scatter | solution.py:363
  1108.5 64.2 %reduce-scatter.30.cloned.1.call-done = bf16[96,768]{1,0:T(8,128)(2,1)} async-done(((bf16[1536,768]{1,0:T(8,128)(2,1)}), bf16[96,768]{1,0:T(8,128)(2,1)}) %reduce-scatter.30.cloned.1.call-update) | async-done | bytes 147472 | tf_op jit(solution)/shard_map/reduce_scatter | solution.py:375
  1174.3 43.5 %reduce-scatter.22.cloned.1.call-done = bf16[512,1536]{1,0:T(8,128)(2,1)} async-done(((bf16[1024,1536]{1,0:T(8,128)(2,1)}), bf16[512,1536]{1,0:T(8,128)(2,1)}) %reduce-scatter.22.cloned.1.call-update) | async-done | bytes 1572880 | tf_op jit(solution)/shard_map/reduce_scatter | solution.py:348
  1221.2 39.7 %all-reduce = (f32[1536]{0:T(1024)}, f32[24]{0:T(128)}, f32[1536]{0:T(1024)}) all-reduce(f32[1536]{0:T(1024)S(1)} %get-tuple-element.463, f32[24]{0:T(128)S(1)} %dynamic_update_slice.20, f32[1536]{0:T(1024)S(1)} %copy-done.27), channel_id=1, replica_groups=mesh['dp'=16,'tensor'=2] {'dp','tensor'}, use_global_device_ids=true, to_apply=%region_24.25 | all-reduce | flops 3096 | bytes 24768 | tf_op jit(solution)/shard_map/psum | solution.py:405
  (227 shorter events, 336.2 us)
Async XLA Ops:
  7.2 182.7 %copy-start = (bf16[768,1536]{1,0:T(8,128)(2,1)S(1)}, bf16[768,1536]{1,0:T(8,128)(2,1)}, u32[]{:S(2)}) copy-start(bf16[768,1536]{1,0:T(8,128)(2,1)} %param.30) | copy-start | bytes 7077892
  7.2 52.9 %all-gather.5.cloned.1.call-start = ((), (), s32[]{:S(2)}) async-start(), calls=%async_computation.13 | async-start | bytes 4718592 | tf_op jit(solution)/shard_map/all_gather | solution.py:217
  10.8 49.3 %copy-start.29 = (f32[12]{0:T(128)S(1)}, f32[12]{0:T(128)}, u32[]{:S(2)}) copy-start(f32[12]{0:T(128)} %param.28) | copy-start | bytes 148
  12.3 225.3 %reduce-scatter.16.cloned.1.call-start = ((), (), s32[]{:S(2)}) async-start(), calls=%async_computation.14 | async-start | bytes 4718592 | tf_op jit(solution)/shard_map/reduce_scatter | solution.py:246
  194.0 90.1 %all-gather.9.cloned.1.call-start = ((), (), s32[]{:S(2)}) async-start(), calls=%async_computation.17 | async-start | bytes 4718592 | tf_op jit(solution)/shard_map/all_gather | solution.py:271
  197.3 133.1 %all-gather.7.cloned.1.call-start = ((), (), s32[]{:S(2)}) async-start(), calls=%async_computation.15 | async-start | bytes 4718592 | tf_op jit(solution)/shard_map/all_gather | solution.py:257
  243.6 179.0 %reduce-scatter.20.cloned.1.call-start = ((), (), s32[]{:S(2)}) async-start(), calls=%async_computation.18 | async-start | bytes 4718592 | tf_op jit(solution)/shard_map/reduce_scatter | solution.py:282
  379.0 89.2 %reduce-scatter.18.cloned.1.call-start = ((), (), s32[]{:S(2)}) async-start(), calls=%async_computation.16 | async-start | bytes 4718592 | tf_op jit(solution)/shard_map/reduce_scatter | solution.py:261
  390.2 129.1 %all-gather.11.cloned.1.call-start = ((), (), s32[]{:S(2)}) async-start(), calls=%async_computation.19 | async-start | bytes 4718592 | tf_op jit(solution)/shard_map/all_gather | solution.py:299
  474.3 262.3 %reduce-scatter.38.cloned.1.call-start = ((), (), s32[]{:S(2)}) async-start(), calls=%async_computation.28 | async-start | bytes 6684672 | tf_op jit(solution)/shard_map/reduce_scatter | solution.py:387
  485.8 252.8 %reduce-scatter.34.cloned.1.call-start = ((), (), s32[]{:S(2)}) async-start(), calls=%async_computation.26 | async-start | bytes 6684672 | tf_op jit(solution)/shard_map/reduce_scatter | solution.py:381
  497.6 287.0 %reduce-scatter.36.cloned.1.call-start = ((), (), s32[]{:S(2)}) async-start(), calls=%async_computation.27 | async-start | bytes 6684672 | tf_op jit(solution)/shard_map/reduce_scatter | solution.py:384
  509.0 334.2 %reduce-scatter.40.cloned.1.call-start = ((), (), s32[]{:S(2)}) async-start(), calls=%async_computation.29 | async-start | bytes 417792
  535.5 134.9 %copy-start.17 = (f32[1024,12]{0,1:T(8,128)S(1)}, f32[1024,12]{0,1:T(8,128)}, u32[]{:S(2)}) copy-start(f32[1024,12]{0,1:T(8,128)} %get-tuple-element.565) | copy-start | bytes 147460
  674.0 235.1 %reduce-scatter.32.cloned.1.call-start = ((), (), s32[]{:S(2)}) async-start(), calls=%async_computation.25 | async-start | bytes 2506752 | tf_op jit(solution)/shard_map/reduce_scatter | solution.py:378
  680.7 294.4 %reduce-scatter.28.cloned.1.call-start = ((), (), s32[]{:S(2)}) async-start(), calls=%async_computation.23 | async-start | bytes 2506752 | tf_op jit(solution)/shard_map/reduce_scatter | solution.py:369
  689.4 351.5 %reduce-scatter.26.cloned.1.call-start = ((), (), s32[]{:S(2)}) async-start(), calls=%async_computation.22 | async-start | bytes 2506752 | tf_op jit(solution)/shard_map/reduce_scatter | solution.py:366
  698.4 408.4 %reduce-scatter.24.cloned.1.call-start = ((), (), s32[]{:S(2)}) async-start(), calls=%async_computation.21 | async-start | bytes 2506752 | tf_op jit(solution)/shard_map/reduce_scatter | solution.py:363
  707.9 464.8 %reduce-scatter.30.cloned.1.call-start = ((), (), s32[]{:S(2)}) async-start(), calls=%async_computation.24 | async-start | bytes 2506752 | tf_op jit(solution)/shard_map/reduce_scatter | solution.py:375
  714.2 503.7 %reduce-scatter.22.cloned.1.call-start = ((), (), s32[]{:S(2)}) async-start(), calls=%async_computation.20 | async-start | bytes 4718592 | tf_op jit(solution)/shard_map/reduce_scatter | solution.py:348
  736.3 481.5 %copy-start.22 = (f32[1536]{0:T(1024)S(1)}, f32[1536]{0:T(1024)}, u32[]{:S(2)}) copy-start(f32[1536]{0:T(1024)} %param.23) | copy-start | bytes 18436
  736.3 481.5 %copy-start.26 = (f32[512]{0:T(512)S(1)}, f32[512]{0:T(512)}, u32[]{:S(2)}) copy-start(f32[512]{0:T(512)} %copy-done.25) | copy-start | bytes 6148
  976.7 244.4 %copy-start.27 = (f32[1536]{0:T(1024)S(1)}, f32[1536]{0:T(1024)}, u32[]{:S(2)}) copy-start(f32[1536]{0:T(1024)} %get-tuple-element.461) | copy-start | bytes 18436
  976.7 284.2 %copy-start.28 = (f32[512]{0:T(512)S(1)}, f32[512]{0:T(512)}, u32[]{:S(2)}) copy-start(f32[512]{0:T(512)} %get-tuple-element.560) | copy-start | bytes 6148
  (33 other events, 460.5 us)
Sparse Core Ops, SparseCore 0:
  12.4 47.6 all-gather.4
  194.1 43.4 reduce-scatter.15
  239.2 44.8 all-gather.8
  285.5 44.8 all-gather.6
  379.1 43.4 reduce-scatter.19
  424.6 43.4 reduce-scatter.17
  474.4 44.8 all-gather.10
  523.3 85.0 reduce-scatter.37
  612.4 84.1 reduce-scatter.33
  700.3 84.2 reduce-scatter.35
  788.1 55.0 reduce-scatter.39
  846.8 62.2 reduce-scatter.31
  912.9 62.1 reduce-scatter.27
  978.7 62.2 reduce-scatter.25
  1044.6 62.2 reduce-scatter.23
  1110.4 62.2 reduce-scatter.29
  1175.3 42.4 reduce-scatter.21
where the time goes:
time: 1280 us; the launch traced here: 1270 us
  waiting for transfers between devices  713 us (56%)
  matrix products  383 us (30%)
  other arithmetic  102 us (8%)
  blocking collectives  39.7 us (3%)
  local copies, waits for them, and re-layouts  18.2 us (1%)
  between operations  15.3 us (1%)
    dot_general x9, matrix products, weight_term(): lax.dot_general(left, right, (((0,), (0,)), ((), ())), preferred_element_...  69 us
    reduce_scatter x1, waiting for transfers between devices, local(): lax.psum_scatter(output_part.astype(jnp.bfloat16), 'dp', scatter_dimensio...  64.5 us
    reduce_scatter x1, waiting for transfers between devices, local(): lax.psum_scatter(value_part.astype(jnp.bfloat16), 'dp', scatter_dimension...  64.3 us
    reduce_scatter x1, waiting for transfers between devices, local(): lax.psum_scatter(outgate_part.astype(jnp.bfloat16), 'dp', scatter_dimensi...  64.2 us
    reduce_scatter x1, waiting for transfers between devices, local(): lax.psum_scatter(key_part.astype(jnp.bfloat16), 'dp', scatter_dimension=0...  64.2 us
    reduce_scatter x1, waiting for transfers between devices, local(): lax.psum_scatter(query_part.astype(jnp.bfloat16), 'dp', scatter_dimension...  64.2 us
    dot_general x9, matrix products, dot_trans(): lax.dot_general(left, right, (((1,), (1,)), ((), ())), preferred_element_...  58.9 us
    unnamed x18, waiting for transfers between devices  56.9 us
  transfers between devices with their start and end apart: 17, of which 15 were waited for; matrix products, arithmetic and copies ran while one was open for 23% of the time, Pallas kernels for 0%

commit v1 on v0

v1 whole, which is shorter than its diff:
```python
import jax
import jax.numpy as jnp
from jax import lax
from jax.experimental import pallas as pl
from jax.experimental.pallas import tpu as pltpu
from jax.sharding import PartitionSpec as P

H = 24
HD = 64
LEN = 1024
LANES = 128
FAR = -1e30


epsilon = 1e-06


def dot_nn(left, right):
    return lax.dot_general(
        left, right, (((1,), (0,)), ((), ())), preferred_element_type=jnp.float32
    )


def dot_nt(left, right):
    return lax.dot_general(
        left, right, (((1,), (1,)), ((), ())), preferred_element_type=jnp.float32
    )


def dot_tn(left, right):
    return lax.dot_general(
        left, right, (((0,), (0,)), ((), ())), preferred_element_type=jnp.float32
    )


def lane_of(shape, head):
    lane = lax.broadcasted_iota(jnp.int32, shape, 1)
    return lane - (1 - head) * HD, (lane // HD) == head


def three_lanes(relative, first, column, otherwise):
    high = column.astype(jnp.bfloat16).astype(jnp.float32)
    rest = column - high
    middle = rest.astype(jnp.bfloat16).astype(jnp.float32)
    low = rest - middle
    placed = jnp.where(relative == first + 2, low, otherwise)
    placed = jnp.where(relative == first + 1, middle, placed)
    return jnp.where(relative == first, high, placed)


def lanes_at(relative, first, value, otherwise):
    return jnp.where((relative >= first) & (relative < first + 3), value, otherwise)


def quarters(ref):
    return [ref.at[:, part * LANES : (part + 1) * LANES] for part in range(4)]


def forward_kernel(where_ref, qkvz_ref, d_ref, mixed_ref, att_ref, total_ref, qa, qu, ka):
    q_ref, k_ref, v_ref, z_ref = quarters(qkvz_ref)
    length = q_ref.shape[0]
    half, quarter = length // 2, length // 4
    prefix, first, second = where_ref[0], where_ref[1], where_ref[2]
    first = pl.multiple_of(first, half)
    second = pl.multiple_of(second, half)
    early = pl.ds(first, half)
    for head in range(2):
        relative, own = lane_of((length, LANES), head)
        decay = jnp.broadcast_to(d_ref[0, :, head : head + 1], (length, LANES))
        plus = three_lanes(relative, 0, decay, lanes_at(relative, 3, 1.0, 0.0))
        minus = three_lanes(relative, 3, -decay, lanes_at(relative, 0, 1.0, 0.0))
        scaled = q_ref[...].astype(jnp.float32) * HD**-0.5
        qa[...] = jnp.where(own, scaled, plus).astype(jnp.bfloat16)
        qu[...] = jnp.where(own, scaled, -plus).astype(jnp.bfloat16)
        ka[...] = jnp.where(own, k_ref[...].astype(jnp.float32), minus).astype(jnp.bfloat16)
        lanes = slice(head * HD, head * HD + HD)

        def finish(rows, parts, lanes=lanes, head=head):
            top = parts[0][0].max(axis=1, keepdims=True)
            for scores, _ in parts[1:]:
                top = jnp.maximum(top, scores.max(axis=1, keepdims=True))
            norm, out = 0.0, 0.0
            for scores, keys in parts:
                weight = jnp.exp(scores - top)
                norm = norm + weight.sum(axis=1, keepdims=True)
                out = out + dot_nn(weight.astype(jnp.bfloat16), v_ref[keys, :])
            att_ref[rows, lanes] = (out / norm)[:, lanes]
            total_ref[0, rows, head : head + 1] = top + jnp.log(norm)

        for part in range(2):
            rows = pl.ds(first + part * quarter, quarter)
            i = lax.broadcasted_iota(jnp.int32, (quarter, half), 0) + part * quarter
            j = lax.broadcasted_iota(jnp.int32, (quarter, half), 1)
            both = (i < prefix) & (j < prefix)
            below = dot_nt(qa[rows, :], ka[early, :])
            above = dot_nt(qu[rows, :], ka[early, :])
            scores = jnp.where(j <= i, below, jnp.where(both, above, FAR))
            finish(rows, [(scores, early)])
        for part in range(2):
            rows = pl.ds(second + part * quarter, quarter)
            width = (part + 1) * quarter
            late = pl.ds(second, width)
            i = lax.broadcasted_iota(jnp.int32, (quarter, width), 0) + part * quarter
            j = lax.broadcasted_iota(jnp.int32, (quarter, width), 1)
            finish(
                rows,
                [
                    (dot_nt(qa[rows, :], ka[early, :]), early),
                    (jnp.where(j <= i, dot_nt(qa[rows, :], ka[late, :]), FAR), late),
                ],
            )
    mixed_ref[...] = (jax.nn.sigmoid(z_ref[...].astype(jnp.float32)) * att_ref[...]).astype(
        jnp.bfloat16
    )


def backward_kernel(
    where_ref,
    qkvz_ref,
    gm_ref,
    att_ref,
    d_ref,
    total_ref,
    grads_ref,
    gd_ref,
    qa,
    qu,
    ka,
    va,
    ga,
    acc_q,
    acc_k,
    acc_v,
):
    q_ref, k_ref, v_ref, z_ref = quarters(qkvz_ref)
    dq_ref, dk_ref, dv_ref, dz_ref = quarters(grads_ref)
    length = q_ref.shape[0]
    half, quarter = length // 2, length // 4
    prefix, first, second = where_ref[0], where_ref[1], where_ref[2]
    first = pl.multiple_of(first, half)
    second = pl.multiple_of(second, half)
    outgate = jax.nn.sigmoid(z_ref[...].astype(jnp.float32))
    grad_mixed = gm_ref[...].astype(jnp.float32)
    attended = att_ref[...]
    grad_att = (grad_mixed * outgate).astype(jnp.bfloat16).astype(jnp.float32)
    dz_ref[...] = (grad_mixed * attended * outgate * (1.0 - outgate)).astype(jnp.bfloat16)
    product = grad_att * attended
    for head in range(2):
        relative, own = lane_of((length, LANES), head)
        delta = jnp.sum(jnp.where(own, product, 0.0), axis=1, keepdims=True)
        delta = jnp.broadcast_to(delta, (length, LANES))
        decay = jnp.broadcast_to(d_ref[0, :, head : head + 1], (length, LANES))
        total = jnp.broadcast_to(total_ref[0, :, head : head + 1], (length, LANES))
        ones = lanes_at(relative, 3, 1.0, 0.0)
        ones_front = lanes_at(relative, 0, 1.0, 0.0)
        scaled = q_ref[...].astype(jnp.float32) * HD**-0.5
        qa[...] = jnp.where(own, scaled, three_lanes(relative, 0, decay - total, ones)).astype(
            jnp.bfloat16
        )
        qu[...] = jnp.where(own, scaled, three_lanes(relative, 0, -decay - total, -ones)).astype(
            jnp.bfloat16
        )
        ka[...] = jnp.where(
            own, k_ref[...].astype(jnp.float32), three_lanes(relative, 3, -decay, ones_front)
        ).astype(jnp.bfloat16)
        va[...] = jnp.where(own, v_ref[...].astype(jnp.float32), ones_front).astype(jnp.bfloat16)
        ga[...] = jnp.where(own, grad_att, three_lanes(relative, 0, -delta, 0.0)).astype(
            jnp.bfloat16
        )
        lanes = slice(head * HD, head * HD + HD)
        free = (1 - head) * HD

        def unit(keys, queries, shape, key_start, query_start, prefixed, masked, fresh_k, fresh_q,
                 head=head):
            score = dot_nt(ka[keys, :], qa[queries, :])
            if prefixed or masked:
                j = lax.broadcasted_iota(jnp.int32, shape, 0) + key_start
                i = lax.broadcasted_iota(jnp.int32, shape, 1) + query_start
                causal = j <= i
                other = FAR
                if prefixed:
                    above = dot_nt(ka[keys, :], qu[queries, :])
                    other = jnp.where((i < prefix) & (j < prefix), above, FAR)
                score = jnp.where(causal, score, other)
            probs = jnp.exp(score)
            grad = (probs * dot_nt(va[keys, :], ga[queries, :])).astype(jnp.bfloat16)
            part_v = dot_nn(probs.astype(jnp.bfloat16), ga[queries, :])
            part_k = dot_nn(grad, qa[queries, :])
            part_q = dot_tn(grad, ka[keys, :])
            if prefixed:
                turned = jnp.where(causal, 0.0, -2.0 * grad.astype(jnp.float32)).astype(
                    jnp.bfloat16
                )
                back_k, _ = lane_of((shape[1], LANES), head)
                back_q, _ = lane_of((shape[0], LANES), head)
                part_k = part_k + dot_nn(turned, jnp.where(back_k == 3, 1.0, 0.0).astype(jnp.bfloat16))
                part_q = part_q + dot_tn(turned, jnp.where(back_q == 0, 1.0, 0.0).astype(jnp.bfloat16))
            if fresh_k:
                acc_k[keys, :] = part_k
                acc_v[keys, :] = part_v
            else:
                acc_k[keys, :] += part_k
                acc_v[keys, :] += part_v
            if fresh_q:
                acc_q[queries, :] = part_q
            else:
                acc_q[queries, :] += part_q

        early = pl.ds(first, half)
        for part in range(2):
            queries = pl.ds(first + part * quarter, quarter)
            unit(early, queries, (half, quarter), 0, part * quarter, True, False, part == 0, True)
        for part in range(2):
            queries = pl.ds(second + part * quarter, quarter)
            unit(early, queries, (half, quarter), 0, 0, False, False, False, True)
        unit(pl.ds(second, half), pl.ds(second + quarter, quarter), (half, quarter), 0, quarter,
             False, True, True, False)
        unit(pl.ds(second, quarter), pl.ds(second, quarter), (quarter, quarter), 0, 0,
             False, True, False, False)
        dq_ref[:, lanes] = (acc_q[:, lanes] * HD**-0.5).astype(jnp.bfloat16)
        dk_ref[:, lanes] = acc_k[:, lanes].astype(jnp.bfloat16)
        dv_ref[:, lanes] = acc_v[:, lanes].astype(jnp.bfloat16)
        gd_ref[0, :, head : head + 1] = acc_q[:, free : free + 1] - acc_k[:, free + 3 : free + 4]


def wide(length, columns, offset=0):
    return pl.BlockSpec((length, columns), lambda pair, where: (0, pair + offset))


def narrow(length, offset=0):
    return pl.BlockSpec((1, length, 2), lambda pair, where: (pair + offset, 0, 0))


def attention_forward(places, qkvz, decay):
    length = qkvz.shape[0]
    pairs = decay.shape[0]
    return pl.pallas_call(
        forward_kernel,
        grid_spec=pltpu.PrefetchScalarGridSpec(
            num_scalar_prefetch=1,
            grid=(pairs,),
            in_specs=[wide(length, 4 * LANES), narrow(length)],
            out_specs=[wide(length, LANES)] * 2 + [narrow(length)],
            scratch_shapes=[pltpu.VMEM((length, LANES), jnp.bfloat16)] * 3,
        ),
        out_shape=[
            jax.ShapeDtypeStruct((length, pairs * LANES), jnp.bfloat16),
            jax.ShapeDtypeStruct((length, pairs * LANES), jnp.float32),
            jax.ShapeDtypeStruct((pairs, length, 2), jnp.float32),
        ],
        compiler_params=pltpu.CompilerParams(vmem_limit_bytes=56 << 20),
        cost_estimate=pl.CostEstimate(
            flops=pairs * 5_000_000_000, bytes_accessed=15_000_000, transcendentals=0
        ),
        name="attention_forward",
    )(places, qkvz, decay)


def attention_backward(places, qkvz, grad_mixed, attended, decay, log_total, start, count):
    length = qkvz.shape[0]
    return pl.pallas_call(
        backward_kernel,
        grid_spec=pltpu.PrefetchScalarGridSpec(
            num_scalar_prefetch=1,
            grid=(count,),
            in_specs=[wide(length, 4 * LANES, start)]
            + [wide(length, LANES, start)] * 2
            + [narrow(length, start)] * 2,
            out_specs=[wide(length, 4 * LANES), narrow(length)],
            scratch_shapes=[pltpu.VMEM((length, LANES), jnp.bfloat16)] * 5
            + [pltpu.VMEM((length, LANES), jnp.float32)] * 3,
        ),
        out_shape=[
            jax.ShapeDtypeStruct((length, count * 4 * LANES), jnp.bfloat16),
            jax.ShapeDtypeStruct((count, length, 2), jnp.float32),
        ],
        compiler_params=pltpu.CompilerParams(vmem_limit_bytes=56 << 20),
        cost_estimate=pl.CostEstimate(
            flops=count * 8_000_000_000, bytes_accessed=15_000_000, transcendentals=0
        ),
        name="attention_backward",
    )(places, qkvz, grad_mixed, attended, decay, log_total)


def weight_term(left, right):
    return lax.dot_general(
        left, right, (((0,), (0,)), ((), ())), preferred_element_type=jnp.float32
    )


def rms_rows(rows, gain):
    inverse = lax.rsqrt(jnp.mean(rows * rows, axis=-1, keepdims=True) + epsilon)
    return (inverse, rows * inverse * gain)


def rms_back(rows, inverse, gain, grad):
    scaled = grad * gain
    gain_term = jnp.sum(grad * rows * inverse, axis=0)
    row_term = inverse * scaled - rows * inverse**3 * jnp.mean(
        scaled * rows, axis=-1, keepdims=True
    )
    return (row_term, gain_term)


def tie(*values):
    return lax.optimization_barrier(values)


def swap(rows):
    return lax.ppermute(rows, "tensor", [(0, 1), (1, 0)])


def two_devices():
    return lax.axis_size("tensor") == 2


def gather_rows(rows, other=None):
    if not two_devices():
        return lax.all_gather(rows, "tensor", axis=0, tiled=True)
    return jnp.concatenate([rows, swap(rows) if other is None else other], axis=0)


def half_starts(length):
    if not two_devices():
        return jnp.array(0, jnp.int32), jnp.array(length // 2, jnp.int32)
    first = lax.axis_index("tensor") * (length // 2)
    return first, length // 2 - first


def scatter_rows(product, length):
    if not two_devices():
        return lax.psum_scatter(
            product(0, length).astype(jnp.bfloat16), "tensor", scatter_dimension=0, tiled=True
        ).astype(jnp.float32), 0.0
    sent = product(length // 2, length).astype(jnp.bfloat16)
    arrived = swap(sent)
    _, start = tie(sent, jnp.zeros((), jnp.float32))
    return product(0, length // 2), arrived


class WeightSum:
    def __init__(self, partial, masks):
        self.size = lax.axis_size("dp")
        bits = self.size.bit_length() - 1
        rows, columns = partial.shape
        self.terms = [
            partial.astype(jnp.bfloat16).reshape((2,) * bits + (rows // self.size, columns))
        ]
        self.left = list(range(bits - 1, -1, -1))
        self.masks = list(masks)

    def send(self, critical):
        if not self.masks:
            return critical
        mask = self.masks.pop(0)
        bit = mask.bit_length() - 1
        axis = self.left.index(bit)
        self.left.remove(bit)
        mine = (lax.axis_index("dp") // mask) % 2
        sent = sum(
            lax.dynamic_index_in_dim(term, 1 - mine, axis, False).astype(jnp.float32)
            for term in self.terms
        ).astype(jnp.bfloat16)
        critical, sent = tie(critical, sent)
        arrived = lax.ppermute(sent, "dp", [(i, i ^ mask) for i in range(self.size)])
        self.terms = [
            lax.dynamic_index_in_dim(term, mine, axis, False) for term in self.terms
        ] + [arrived]
        return critical

    def arrive(self, critical):
        critical, self.terms[-1] = tie(critical, self.terms[-1])
        return critical

    def result(self):
        while self.masks:
            self.send(jnp.zeros((), jnp.float32))
        return sum(term.astype(jnp.float32) for term in self.terms)


def all_sum(value):
    size = lax.axis_size("dp")
    mask = 1
    while mask < size:
        value = value + lax.ppermute(value, "dp", [(i, i ^ mask) for i in range(size)])
        mask *= 2
    if not two_devices():
        return lax.psum(value, "tensor")
    return value + swap(value)


def pair_columns(weights, pairs):
    width = pairs * LANES
    padded = [jnp.pad(w, ((0, 0), (0, width - w.shape[1]))) for w in weights]
    parts = [w[:, p * LANES : (p + 1) * LANES] for p in range(pairs) for w in padded]
    return jnp.concatenate(parts, axis=1)


def running_sum(order, values):
    high = lax.reduce_precision(values, 8, 7)
    middle = lax.reduce_precision(values - high, 8, 7)
    terms = jnp.concatenate([high, middle, values - high - middle], axis=1).astype(jnp.bfloat16)
    sums = dot_nn(order, terms)
    return sum(jnp.split(sums, 3, axis=1))


def by_pairs(columns):
    length, heads = columns.shape
    columns = jnp.pad(columns, ((0, 0), (0, heads % 2)))
    return columns.reshape(length, -1, 2).transpose(1, 0, 2)


def from_pairs(pairs, heads):
    return pairs.transpose(1, 0, 2).reshape(pairs.shape[1], -1)[:, :heads]


def local(
    tokens_in,
    prefix_len,
    attn_gain,
    query_weight,
    key_weight,
    value_weight,
    forget_weight,
    forget_bias,
    outgate_weight,
    output_weight,
    mlp_gain,
    gate_weight,
    up_weight,
    down_weight,
    out_grad,
):
    heads_here = forget_weight.shape[1]
    assert prefix_len.shape[0] == 1
    pairs = (heads_here + 1) // 2
    width = heads_here * HD
    first, second = half_starts(LEN)
    places = jnp.stack([prefix_len[0], first, second])
    index = jnp.arange(LEN, dtype=jnp.int32)
    position = (index + first) % LEN
    earlier = (position[None, :] <= position[:, None]).astype(jnp.bfloat16)
    later = (position[None, :] >= position[:, None]).astype(jnp.bfloat16)
    bits = lax.axis_size("dp").bit_length() - 1
    near = [1 << bit for bit in range(bits)]
    far = near[:1] + near[2:] + near[1:2]

    scale_one, normed_rows = rms_rows(tokens_in, attn_gain)
    normed = gather_rows(normed_rows.astype(jnp.bfloat16))
    projection = pair_columns((query_weight, key_weight, value_weight, outgate_weight), pairs)
    output_padded = jnp.pad(output_weight, ((0, pairs * LANES - width), (0, 0)))
    normed, branch_rows = tie(normed, out_grad.astype(jnp.bfloat16))
    grad_branch = gather_rows(branch_rows)
    qkvz = dot_nn(normed, projection).astype(jnp.bfloat16)
    forget_logit = dot_nn(normed, forget_weight) + forget_bias
    decay = by_pairs(running_sum(earlier, jax.nn.log_sigmoid(forget_logit)))
    mixed, attended, log_total = attention_forward(places, qkvz, decay)
    mixed, grad_branch = tie(mixed, grad_branch)
    own, arrived = scatter_rows(lambda a, b: dot_nn(mixed[a:b], output_padded), LEN)
    grad_active = dot_nt(grad_branch, down_weight).astype(jnp.bfloat16)
    own, grad_active = tie(own, grad_active)
    hidden_rows = tokens_in + (own + arrived)

    scale_two, normed_two_rows = rms_rows(hidden_rows, mlp_gain)
    normed_two = gather_rows(normed_two_rows.astype(jnp.bfloat16))
    gate = dot_nn(normed_two, gate_weight)
    upward = dot_nn(normed_two, up_weight)
    active = (jax.nn.silu(gate) * upward).astype(jnp.bfloat16)
    gate_sigmoid = jax.nn.sigmoid(gate)
    grad_act_f = grad_active.astype(jnp.float32)
    grad_gate = (grad_act_f * upward * gate_sigmoid * (1.0 + gate * (1.0 - gate_sigmoid))).astype(
        jnp.bfloat16
    )
    grad_upward = (grad_act_f * gate * gate_sigmoid).astype(jnp.bfloat16)
    own, arrived = scatter_rows(
        lambda a, b: dot_nt(grad_gate[a:b], gate_weight) + dot_nt(grad_upward[a:b], up_weight), LEN
    )
    own, grad_branch, active = tie(own, grad_branch, active)
    down = WeightSum(weight_term(grad_branch, active), near)
    own = down.send(own)
    own, normed_two = tie(own, normed_two)
    gate_sum = WeightSum(weight_term(normed_two, grad_gate), near)
    own = gate_sum.send(own)
    own = down.arrive(own)
    own = down.send(own)
    grad_normed_two = own + arrived
    grad_hidden, mlp_gain_part = rms_back(hidden_rows, scale_two, mlp_gain, grad_normed_two)
    grad_hidden = grad_hidden + out_grad
    mid_rows = grad_hidden.astype(jnp.bfloat16)
    mid_rows, normed_two, active = tie(mid_rows, normed_two, active)
    other = swap(mid_rows) if two_devices() else jnp.zeros((), jnp.float32)
    up_sum = WeightSum(weight_term(normed_two, grad_upward), near)
    other = up_sum.send(other)
    other = gate_sum.arrive(other)
    other = gate_sum.send(other)
    last_own, last_arrived = scatter_rows(lambda a, b: dot_nn(active[a:b], down_weight), LEN)
    other, last_own = tie(other, last_own)
    other = up_sum.arrive(other)
    other = up_sum.send(other)
    grad_mid = gather_rows(mid_rows, other)

    grad_mixed = dot_nt(grad_mid, output_padded).astype(jnp.bfloat16)
    grad_mixed = down.arrive(grad_mixed)
    grad_mixed = down.send(grad_mixed)
    cut = pairs // 2
    saved = (attended, decay, log_total)
    grads_a, decay_a = attention_backward(places, qkvz, grad_mixed, *saved, 0, cut)
    grads_a, mixed, grad_mid = tie(grads_a, mixed, grad_mid)
    output_sum = WeightSum(weight_term(grad_mid, mixed)[:, :width], far)
    grads_a = output_sum.send(grads_a)
    grads_a = down.arrive(grads_a)
    grads_a = down.send(grads_a)
    grads_a = gate_sum.arrive(grads_a)
    grads_a = gate_sum.send(grads_a)
    grads_a, grad_mixed = tie(grads_a, grad_mixed)
    sum_a = WeightSum(weight_term(normed, grads_a), far)
    grad_mixed = sum_a.send(grad_mixed)
    grad_mixed = output_sum.arrive(grad_mixed)
    grad_mixed = output_sum.send(grad_mixed)
    grad_mixed, last_arrived = tie(grad_mixed, last_arrived)
    layer_out = hidden_rows + (last_own + last_arrived)
    grads_b, decay_b = attention_backward(places, qkvz, grad_mixed, *saved, cut, pairs - cut)
    for each in (down, gate_sum, up_sum, sum_a, output_sum):
        grads_b = each.arrive(grads_b)
        grads_b = each.send(grads_b)
    grad_decay = from_pairs(jnp.concatenate([decay_a, decay_b], axis=0), heads_here)
    grad_forget = (running_sum(later, grad_decay) * jax.nn.sigmoid(-forget_logit)).astype(
        jnp.bfloat16
    )
    bias_part = jnp.sum(grad_forget.astype(jnp.float32), axis=0)
    middle = cut * 4 * LANES

    def normed_term(a, b):
        term = dot_nt(grads_a[a:b], projection[:, :middle])
        term = term + dot_nt(grads_b[a:b], projection[:, middle:])
        return term + dot_nt(grad_forget[a:b], forget_weight)

    own, arrived = scatter_rows(normed_term, LEN)
    own, normed = tie(own, normed)
    sum_b = WeightSum(weight_term(normed, grads_b), near)
    own = sum_b.send(own)
    forget_sum = WeightSum(weight_term(normed, grad_forget), far)
    own = forget_sum.send(own)
    own = sum_b.arrive(own)
    own = sum_b.send(own)
    grad_normed = own + arrived
    input_part, attn_gain_part = rms_back(tokens_in, scale_one, attn_gain, grad_normed)
    input_grad = grad_hidden + input_part

    down_grad = down.result().T
    gate_grad = gate_sum.result()
    up_grad = up_sum.result()
    output_grad = output_sum.result().T
    forget_grad = forget_sum.result()
    block = jnp.concatenate([sum_a.result(), sum_b.result()], axis=1)
    block = block.reshape(block.shape[0], pairs, 4, LANES)
    query_grad, key_grad, value_grad, outgate_grad = [
        block[:, :, part].reshape(block.shape[0], pairs * LANES)[:, :width] for part in range(4)
    ]
    bias_full = lax.dynamic_update_slice_in_dim(
        jnp.zeros((H,), jnp.float32), bias_part, lax.axis_index("tensor") * heads_here, 0
    )
    summed = all_sum(jnp.concatenate([attn_gain_part, mlp_gain_part, bias_full]))
    width = attn_gain_part.shape[0]
    attn_gain_grad, mlp_gain_grad, bias_grad = jnp.split(summed, [width, 2 * width])
    return (
        layer_out,
        input_grad,
        attn_gain_grad,
        query_grad,
        key_grad,
        value_grad,
        forget_grad,
        bias_grad,
        outgate_grad,
        output_grad,
        mlp_gain_grad,
        gate_grad,
        up_grad,
        down_grad,
    )


def solution(mesh):
    in_specs = (
        P(("dp", "tensor"), None),
        P("dp"),
        P(),
        P(None, "tensor"),
        P(None, "tensor"),
        P(None, "tensor"),
        P(None, "tensor"),
        P("tensor"),
        P(None, "tensor"),
        P("tensor", None),
        P(),
        P(None, "tensor"),
        P(None, "tensor"),
        P("tensor", None),
        P(("dp", "tensor"), None),
    )
    out_specs = (
        P(("dp", "tensor"), None),
        P(("dp", "tensor"), None),
        P(),
        P("dp", "tensor"),
        P("dp", "tensor"),
        P("dp", "tensor"),
        P("dp", "tensor"),
        P(),
        P("dp", "tensor"),
        P("tensor", "dp"),
        P(),
        P("dp", "tensor"),
        P("dp", "tensor"),
        P("tensor", "dp"),
    )
    return jax.shard_map(local, mesh=mesh, in_specs=in_specs, out_specs=out_specs, check_vma=False)
```

time: 1280 us -> 682 us (0.53)
  waiting for transfers between devices: 713 us -> 238 us
  matrix products: 383 us -> 181 us
  Pallas kernels: 0 us -> 83.9 us
  blocking collectives: 39.7 us -> 0 us
  local copies, waits for them, and re-layouts: 18.2 us -> 56 us
  starting transfers between devices: 1.28 us -> 34.1 us
  other arithmetic: 102 us -> 85 us
    reduce_scatter x12 -> x0, waiting for transfers between devices: 523 us -> none  [the longest x1 64.5 us: local(): lax.psum_scatter(output_part.astype(jnp.bfloat16), 'dp', scatter_dimensio...]
    ppermute x0 -> x41, waiting for transfers between devices: none -> 238 us  [the longest x9 133 us: swap(): return lax.ppermute(rows, 'tensor', [(0, 1), (1, 0)])]
    dot_general x25 -> x22, matrix products: 314 us -> 135 us  [the longest x10 77.8 us: dot_nn(): lax.dot_general(left, right, (((1,), (0,)), ((), ())), preferred_element_...]
    all_gather x4 -> x0, waiting for transfers between devices: 133 us -> none  [the longest x1 47.1 us: local(): lax.all_gather(normed_rows.astype(jnp.bfloat16), 'tensor', axis=0, tiled=...]
    pallas_call x0 -> x3, Pallas kernels: none -> 83.9 us  [the longest x2 53.2 us: attention_backward(): pl.pallas_call(backward_kernel, grid_spec=pltpu.PrefetchScalarGridSpec(nu...]
    unnamed x18 -> x0, waiting for transfers between devices: 56.9 us -> none
    psum x1 -> x0, blocking collectives: 39.7 us -> none  [local(): lax.psum((attn_gain_part, mlp_gain_part, bias_full), ('dp', 'tensor'))]
    ppermute x0 -> x41, starting transfers between devices: none -> 34.1 us  [the longest x28 19.4 us: send(): lax.ppermute(sent, 'dp', [(i, i ^ mask) for i in range(self.size)])]
  transfers between devices with their start and end apart: 17 -> 41, of which waited for: 15 -> 18; matrix products, arithmetic and copies ran while one was open for 23% -> 28% of each run, Pallas kernels for 0% -> 12%
where the time goes in v1:
time: 682 us; the launch traced here: 680 us
  waiting for transfers between devices  238 us (35%)
  matrix products  181 us (27%)
  other arithmetic  85 us (12%)
  Pallas kernels  83.9 us (12%)
  local copies, waits for them, and re-layouts  56 us (8%)
  starting transfers between devices  34.1 us (5%)
    ppermute x9, waiting for transfers between devices, swap(): return lax.ppermute(rows, 'tensor', [(0, 1), (1, 0)])  133 us
    ppermute x28, waiting for transfers between devices, send(): lax.ppermute(sent, 'dp', [(i, i ^ mask) for i in range(self.size)])  95.2 us
    dot_general x10, matrix products, dot_nn(): lax.dot_general(left, right, (((1,), (0,)), ((), ())), preferred_element_...  77.8 us
    dot_general x12, matrix products, dot_nt(): lax.dot_general(left, right, (((1,), (1,)), ((), ())), preferred_element_...  56.7 us
    pallas_call x2, Pallas kernels, attention_backward(): pl.pallas_call(backward_kernel, grid_spec=pltpu.PrefetchScalarGridSpec(nu...  53.2 us
    dot_general x7, matrix products, weight_term(): lax.dot_general(left, right, (((0,), (0,)), ((), ())), preferred_element_...  45.9 us
    convert_element_type x20, other arithmetic, send(): sent = sum((lax.dynamic_index_in_dim(term, 1 - mine, axis, False).astype(...  39.2 us
    pallas_call x1, Pallas kernels, attention_forward(): pl.pallas_call(forward_kernel, grid_spec=pltpu.PrefetchScalarGridSpec(num...  30.8 us
  transfers between devices with their start and end apart: 41, of which 18 were waited for; matrix products, arithmetic and copies ran while one was open for 28% of the time, Pallas kernels for 12%

profile of v1, /device:TPU:0, one launch (start us, length us, event | category | flops | bytes accessed | tf_op | source)
XLA Modules:
  0.0 680.2 jit_solution(12507801185727912932)
XLA Ops:
  23.8 19.0 %collective-permute-done = bf16[512,1536]{1,0:T(8,128)(2,1)} collective-permute-done((bf16[512,1536]{1,0:T(8,128)(2,1)}, bf16[512,1536]{1,0:T(8,128)(2,1)}, u32[]{:S(2)}, u32[]{:S(2)}) %collective-permute-start) | collective-permute-done | bytes 1572896 | tf_op jit(solution)/shard_map/ppermute | solution.py:310
  51.8 15.1 %convolution_convert_fusion.5.qkvz_ref = bf16[1024,3072]{1,0:T(8,128)(2,1)} fusion(bf16[1024,1536]{1,0:T(8,128)(2,1)} %copy-done.6, bf16[1536,3072]{1,0:T(8,128)(2,1)} %copy-done.49), kind=kOutput, calls=%fused_computation.14 | convolution fusion | flops 9666822144 | bytes 18874368 | tf_op jit(solution)/shard_map/dot_general | solution.py:19
  66.9 30.8 %attention_forward.1 = (bf16[1024,768]{1,0:T(8,128)(2,1)}, f32[1024,768]{1,0:T(8,128)}, f32[6,1024,2]{2,1,0:T(8,128)}) custom-call(s32[3]{0:T(128)} %pad_add_fusion.where_ref, bf16[1024,3072]{1,0:T(8,128)(2,1)} %convolution_convert_fusion.5.qkvz_ref, f32[6,1024,2]{2,1,0:T(8,128)} %bitcast.422), custom_call_target="tpu_custom_call" | custom-call | flops 30000001024 | bytes 15000000 | tf_op jit(solution)/shard_map/attention_forward/pallas_call | solution.py:237
  102.7 8.3 %convolution_convert_fusion.6 = bf16[1024,2048]{1,0:T(8,128)(2,1)} fusion(bf16[1024,1536]{1,0:T(8,128)(2,1)S(1)} %pad_maximum_fusion.1, bf16[2048,1536]{1,0:T(8,128)(2,1)S(1)} %bitcast.446), kind=kOutput, calls=%fused_computation.19 | convolution fusion | flops 6444548096 | bytes 13631488 | tf_op jit(solution)/shard_map/dot_general | solution.py:25
  111.1 26.4 %collective-permute-done.2 = bf16[512,1536]{1,0:T(8,128)(2,1)S(1)} collective-permute-done((bf16[512,1536]{1,0:T(8,128)(2,1)S(1)}, bf16[512,1536]{1,0:T(8,128)(2,1)S(1)}, u32[]{:S(2)}, u32[]{:S(2)}) %collective-permute-start.2) | collective-permute-done | bytes 1572896 | tf_op jit(solution)/shard_map/ppermute | solution.py:310
  141.8 33.9 %collective-permute-done.3 = bf16[512,1536]{1,0:T(8,128)(2,1)} collective-permute-done((bf16[512,1536]{1,0:T(8,128)(2,1)}, bf16[512,1536]{1,0:T(8,128)(2,1)}, u32[]{:S(2)}, u32[]{:S(2)}) %collective-permute-start.3) | collective-permute-done | bytes 1572896 | tf_op jit(solution)/shard_map/ppermute | solution.py:310
  175.7 23.1 %fusion.95 = f32[1024,2048]{1,0:T(8,128)} fusion(bf16[1536,2048]{1,0:T(8,128)(2,1)} %param.26, bf16[512,1536]{1,0:T(8,128)(2,1)} %collective-permute-done.3, bf16[512,1536]{1,0:T(8,128)(2,1)} %multiply_convert_fusion.1), kind=kOutput, calls=%fused_computation.308 | convolution fusion | flops 6448742400 | bytes 17825792 | tf_op jit(solution)/shard_map/dot_general | solution.py:19
  198.8 17.5 %multiply_convert_fusion = (bf16[1024,2048]{1,0:T(8,128)(2,1)}, bf16[1024,2048]{1,0:T(8,128)(2,1)}, bf16[1024,2048]{1,0:T(8,128)(2,1)}) fusion(f32[1024,2048]{1,0:T(8,128)} %fusion.95, bf16[1024,2048]{1,0:T(8,128)(2,1)} %convolution_convert_fusion.6, bf16[1536,2048]{1,0:T(8,128)(2,1)} %param.27, bf16[512,1536]{1,0:T(8,128)(2,1)} %collective-permute-done.3, ...), kind=kOutput, calls=%fused_computation.7 | convolution fusion | flops 6484393984 | bytes 34603008 | tf_op jit(solution)/shard_map/dot_general | solution.py:19
  216.3 6.8 %fusion.17 = f32[512,1536]{1,0:T(8,128)} fusion(bf16[1536,2048]{1,0:T(8,128)(2,1)S(1)} %bitcast.442, bf16[1024,2048]{1,0:T(8,128)(2,1)} %get-tuple-element.239), kind=kOutput, calls=%fused_computation.65 | convolution fusion | flops 3221225472 | bytes 11534336 | tf_op jit(solution)/shard_map/dot_general | solution.py:25
  232.0 9.7 %convolution_convert_fusion.4 = bf16[1536,2048]{1,0:T(8,128)(2,1)S(1)} fusion(bf16[1024,1536]{1,0:T(8,128)(2,1)S(1)} %copy-done.25, bf16[1024,2048]{1,0:T(8,128)(2,1)} %get-tuple-element.144), kind=kOutput, calls=%fused_computation.13 | convolution fusion | flops 6445596672 | bytes 13631488 | tf_op jit(solution)/shard_map/dot_general | solution.py:286
  255.4 9.5 %convolution_convert_fusion.3 = bf16[1536,2048]{1,0:T(8,128)(2,1)S(1)} fusion(bf16[1024,1536]{1,0:T(8,128)(2,1)S(1)} %pad_maximum_fusion.2, bf16[1024,2048]{1,0:T(8,128)(2,1)} %get-tuple-element.239), kind=kOutput, calls=%fused_computation.12 | convolution fusion | flops 6445596672 | bytes 13631488 | tf_op jit(solution)/shard_map/dot_general | solution.py:286
  271.3 14.5 %collective-permute-done.5 = bf16[512,1536]{1,0:T(8,128)(2,1)S(1)} collective-permute-done((bf16[512,1536]{1,0:T(8,128)(2,1)S(1)}, bf16[512,1536]{1,0:T(8,128)(2,1)S(1)}, u32[]{:S(2)}, u32[]{:S(2)}) %collective-permute-start.5) | collective-permute-done | bytes 1572896 | tf_op jit(solution)/shard_map/ppermute | solution.py:310
  291.2 9.9 %convolution_convert_fusion.2 = bf16[1536,2048]{1,0:T(8,128)(2,1)S(1)} fusion(bf16[1024,1536]{1,0:T(8,128)(2,1)S(1)} %pad_maximum_fusion.2, bf16[1024,2048]{1,0:T(8,128)(2,1)} %get-tuple-element.240), kind=kOutput, calls=%fused_computation.11 | convolution fusion | flops 6445596672 | bytes 13631488 | tf_op jit(solution)/shard_map/dot_general | solution.py:286
  304.9 17.7 %collective-permute-done.6 = bf16[512,1536]{1,0:T(8,128)(2,1)S(1)} collective-permute-done((bf16[512,1536]{1,0:T(8,128)(2,1)S(1)}, bf16[512,1536]{1,0:T(8,128)(2,1)S(1)}, u32[]{:S(2)}, u32[]{:S(2)}) %collective-permute-start.6) | collective-permute-done | bytes 1572896 | tf_op jit(solution)/shard_map/ppermute | solution.py:310
  323.8 8.1 %convolution_convert_fusion.8 = bf16[512,1536]{1,0:T(8,128)(2,1)} fusion(bf16[2048,1536]{1,0:T(8,128)(2,1)} %param.28, bf16[1024,2048]{1,0:T(8,128)(2,1)} %get-tuple-element.144), kind=kOutput, calls=%fused_computation.54 | convolution fusion | flops 3222011904 | bytes 9961472 | tf_op jit(solution)/shard_map/dot_general | solution.py:19
  334.0 7.9 %fusion.23 = f32[512,1536]{1,0:T(8,128)} fusion(bf16[2048,1536]{1,0:T(8,128)(2,1)} %param.28, bf16[1024,2048]{1,0:T(8,128)(2,1)S(1)} %copy-done.61), kind=kOutput, calls=%fused_computation.71 | convolution fusion | flops 3221225472 | bytes 11534336 | tf_op jit(solution)/shard_map/dot_general | solution.py:19
  354.6 15.9 %collective-permute-done.9 = bf16[2,2,96,2048]{3,2,1,0:T(8,128)(2,1)S(1)} collective-permute-done((bf16[2,2,96,2048]{3,2,1,0:T(8,128)(2,1)S(1)}, bf16[2,2,96,2048]{3,2,1,0:T(8,128)(2,1)S(1)}, u32[]{:S(2)}, u32[]{:S(2)}) %collective-permute-start.9) | collective-permute-done | bytes 1572896 | tf_op jit(solution)/shard_map/ppermute | solution.py:365
  376.5 26.7 %attention_backward.2 = (bf16[1024,1536]{1,0:T(8,128)(2,1)}, f32[3,1024,2]{2,1,0:T(8,128)}) custom-call(s32[3]{0:T(128)} %pad_add_fusion.where_ref, bf16[1024,3072]{1,0:T(8,128)(2,1)} %convolution_convert_fusion.5.qkvz_ref, bf16[1024,768]{1,0:T(8,128)(2,1)} %convolution_convert_fusion.11.gm_ref, f32[1024,768]{1,0:T(8,128)} %get-tuple-element.155.att_ref, ...), custom_call_target="tpu_custom_call" | custom-call | flops 24000000000 | bytes 15000000 | tf_op jit(solution)/shard_map/attention_backward/pallas_call | solution.py:261
  439.1 26.5 %attention_backward.3 = (bf16[1024,1536]{1,0:T(8,128)(2,1)}, f32[3,1024,2]{2,1,0:T(8,128)}) custom-call(s32[3]{0:T(128)} %pad_add_fusion.where_ref, bf16[1024,3072]{1,0:T(8,128)(2,1)} %convolution_convert_fusion.5.qkvz_ref, bf16[1024,768]{1,0:T(8,128)(2,1)} %convolution_convert_fusion.11.gm_ref, f32[1024,768]{1,0:T(8,128)} %get-tuple-element.155.att_ref, ...), custom_call_target="tpu_custom_call" | custom-call | flops 24000000000 | bytes 15000000 | tf_op jit(solution)/shard_map/attention_backward/pallas_call | solution.py:261
  490.5 22.9 %collective-permute-done.39 = bf16[2,96,2048]{2,1,0:T(8,128)(2,1)} collective-permute-done((bf16[2,96,2048]{2,1,0:T(8,128)(2,1)}, bf16[2,96,2048]{2,1,0:T(8,128)(2,1)}, u32[]{:S(2)}, u32[]{:S(2)}) %collective-permute-start.39) | collective-permute-done | bytes 786464 | tf_op jit(solution)/shard_map/ppermute | solution.py:365
  517.7 15.9 %collective-permute-done.40 = bf16[96,2048]{1,0:T(8,128)(2,1)S(1)} collective-permute-done((bf16[96,2048]{1,0:T(8,128)(2,1)S(1)}, bf16[96,2048]{1,0:T(8,128)(2,1)S(1)}, u32[]{:S(2)}, u32[]{:S(2)}) %collective-permute-start.40) | collective-permute-done | bytes 393248 | tf_op jit(solution)/shard_map/ppermute | solution.py:365
  580.7 21.7 %collective-permute-done.20 = bf16[512,1536]{1,0:T(8,128)(2,1)S(1)} collective-permute-done((bf16[512,1536]{1,0:T(8,128)(2,1)S(1)}, bf16[512,1536]{1,0:T(8,128)(2,1)S(1)}, u32[]{:S(2)}, u32[]{:S(2)}) %collective-permute-start.20) | collective-permute-done | bytes 1572896 | tf_op jit(solution)/shard_map/ppermute | solution.py:310
  628.4 20.6 %collective-permute-done.27 = bf16[2,96,1536]{2,1,0:T(8,128)(2,1)S(1)} collective-permute-done((bf16[2,96,1536]{2,1,0:T(8,128)(2,1)S(1)}, bf16[2,96,1536]{2,1,0:T(8,128)(2,1)S(1)}, u32[]{:S(2)}, u32[]{:S(2)}) %collective-permute-start.27) | collective-permute-done | bytes 589856 | tf_op jit(solution)/shard_map/ppermute | solution.py:365
  659.8 8.0 %collective-permute-done.31 = bf16[96,1536]{1,0:T(8,128)(2,1)S(1)} collective-permute-done((bf16[96,1536]{1,0:T(8,128)(2,1)S(1)}, bf16[96,1536]{1,0:T(8,128)(2,1)S(1)}, u32[]{:S(2)}, u32[]{:S(2)}) %collective-permute-start.31) | collective-permute-done | bytes 294944 | tf_op jit(solution)/shard_map/ppermute | solution.py:365
  (349 shorter events, 261.1 us)
Async XLA Ops:
  5.1 37.7 %collective-permute-start = (bf16[512,1536]{1,0:T(8,128)(2,1)}, bf16[512,1536]{1,0:T(8,128)(2,1)}, u32[]{:S(2)}, u32[]{:S(2)}) collective-permute-start(bf16[512,1536]{1,0:T(8,128)(2,1)} %multiply_convert_fusion.2), channel_id=1, source_target_pairs={{0,1},{1,0},{2,3},{3,2},{4,5},{5,4},{6,7},{7,6},{8,9},{9,8},{10,11... | collective-permute-start | bytes 4718600 | tf_op jit(solution)/shard_map/ppermute | solution.py:310
  47.6 50.1 %collective-permute-start.1 = (bf16[512,1536]{1,0:T(8,128)(2,1)}, bf16[512,1536]{1,0:T(8,128)(2,1)}, u32[]{:S(2)}, u32[]{:S(2)}) collective-permute-start(bf16[512,1536]{1,0:T(8,128)(2,1)} %convert_element_type.733), channel_id=1, source_target_pairs={{0,1},{1,0},{2,3},{3,2},{4,5},{5,4},{6,7},{7,6},{8,9},{9,8},{10,11... | collective-permute-start | bytes 4718600 | tf_op jit(solution)/shard_map/ppermute | solution.py:310
  102.4 35.1 %collective-permute-start.2 = (bf16[512,1536]{1,0:T(8,128)(2,1)S(1)}, bf16[512,1536]{1,0:T(8,128)(2,1)S(1)}, u32[]{:S(2)}, u32[]{:S(2)}) collective-permute-start(bf16[512,1536]{1,0:T(8,128)(2,1)S(1)} %convolution_convert_fusion.9), channel_id=1, source_target_pairs={{0,1},{1,0},{2,3},{3,2},{4,5},{5,4},{6,7},{7,6},{8,9},{9,8},{10,11... | collective-permute-start | bytes 4718600 | tf_op jit(solution)/shard_map/ppermute | solution.py:310
  141.2 34.5 %collective-permute-start.3 = (bf16[512,1536]{1,0:T(8,128)(2,1)}, bf16[512,1536]{1,0:T(8,128)(2,1)}, u32[]{:S(2)}, u32[]{:S(2)}) collective-permute-start(bf16[512,1536]{1,0:T(8,128)(2,1)} %multiply_convert_fusion.1), channel_id=1, source_target_pairs={{0,1},{1,0},{2,3},{3,2},{4,5},{5,4},{6,7},{7,6},{8,9},{9,8},{10,11... | collective-permute-start | bytes 4718600 | tf_op jit(solution)/shard_map/ppermute | solution.py:310
  252.5 33.4 %collective-permute-start.5 = (bf16[512,1536]{1,0:T(8,128)(2,1)S(1)}, bf16[512,1536]{1,0:T(8,128)(2,1)S(1)}, u32[]{:S(2)}, u32[]{:S(2)}) collective-permute-start(bf16[512,1536]{1,0:T(8,128)(2,1)S(1)} %fusion.13), channel_id=1, source_target_pairs={{0,1},{1,0},{2,3},{3,2},{4,5},{5,4},{6,7},{7,6},{8,9},{9,8},{10,11... | collective-permute-start | bytes 4718600 | tf_op jit(solution)/shard_map/ppermute | solution.py:310
  267.4 74.5 %collective-permute-start.7 = (bf16[2,2,2,96,2048]{4,3,2,1,0:T(8,128)(2,1)}, bf16[2,2,2,96,2048]{4,3,2,1,0:T(8,128)(2,1)}, u32[]{:S(2)}, u32[]{:S(2)}) collective-permute-start(bf16[2,2,2,96,2048]{4,3,2,1,0:T(8,128)(2,1)} %dynamic-slice_bitcast_fusion.1), channel_id=1, source_target_pairs={{0,2},{2,0},{4,6},{6,4},{8,10},{10,8},{12,14},{14,12},{16,18},{18,... | collective-permute-start | bytes 9437192 | tf_op jit(solution)/shard_map/ppermute | solution.py:365
  290.1 32.4 %collective-permute-start.6 = (bf16[512,1536]{1,0:T(8,128)(2,1)S(1)}, bf16[512,1536]{1,0:T(8,128)(2,1)S(1)}, u32[]{:S(2)}, u32[]{:S(2)}) collective-permute-start(bf16[512,1536]{1,0:T(8,128)(2,1)S(1)} %get-tuple-element.137), channel_id=1, source_target_pairs={{0,1},{1,0},{2,3},{3,2},{4,5},{5,4},{6,7},{7,6},{8,9},{9,8},{10,11... | collective-permute-start | bytes 4718600 | tf_op jit(solution)/shard_map/ppermute | solution.py:310
  331.9 107.2 %collective-permute-start.13 = (bf16[512,1536]{1,0:T(8,128)(2,1)}, bf16[512,1536]{1,0:T(8,128)(2,1)}, u32[]{:S(2)}, u32[]{:S(2)}) collective-permute-start(bf16[512,1536]{1,0:T(8,128)(2,1)} %convolution_convert_fusion.8), channel_id=1, source_target_pairs={{0,1},{1,0},{2,3},{3,2},{4,5},{5,4},{6,7},{7,6},{8,9},{9,8},{10,11... | collective-permute-start | bytes 4718600 | tf_op jit(solution)/shard_map/ppermute | solution.py:310
  333.2 37.3 %collective-permute-start.9 = (bf16[2,2,96,2048]{3,2,1,0:T(8,128)(2,1)S(1)}, bf16[2,2,96,2048]{3,2,1,0:T(8,128)(2,1)S(1)}, u32[]{:S(2)}, u32[]{:S(2)}) collective-permute-start(bf16[2,2,96,2048]{3,2,1,0:T(8,128)(2,1)S(1)} %copy-done.29), channel_id=1, source_target_pairs={{0,4},{2,6},{4,0},{6,2},{8,12},{10,14},{12,8},{14,10},{16,20},{18,... | collective-permute-start | bytes 4718600 | tf_op jit(solution)/shard_map/ppermute | solution.py:365
  345.6 68.1 %collective-permute-start.11 = (bf16[2,2,96,2048]{3,2,1,0:T(8,128)(2,1)}, bf16[2,2,96,2048]{3,2,1,0:T(8,128)(2,1)}, u32[]{:S(2)}, u32[]{:S(2)}) collective-permute-start(bf16[2,2,96,2048]{3,2,1,0:T(8,128)(2,1)} %fusion.10), channel_id=1, source_target_pairs={{0,4},{2,6},{4,0},{6,2},{8,12},{10,14},{12,8},{14,10},{16,20},{18,... | collective-permute-start | bytes 4718600 | tf_op jit(solution)/shard_map/ppermute | solution.py:365
  374.3 36.8 %collective-permute-start.10 = (bf16[2,96,2048]{2,1,0:T(8,128)(2,1)}, bf16[2,96,2048]{2,1,0:T(8,128)(2,1)}, u32[]{:S(2)}, u32[]{:S(2)}) collective-permute-start(bf16[2,96,2048]{2,1,0:T(8,128)(2,1)} %fusion.31), channel_id=1, source_target_pairs={{0,8},{2,10},{4,12},{6,14},{8,0},{10,2},{12,4},{14,6},{16,24},{18,... | collective-permute-start | bytes 2359304 | tf_op jit(solution)/shard_map/ppermute | solution.py:365
  375.0 107.2 %collective-permute-start.16 = (bf16[2,2,96,2048]{3,2,1,0:T(8,128)(2,1)}, bf16[2,2,96,2048]{3,2,1,0:T(8,128)(2,1)}, u32[]{:S(2)}, u32[]{:S(2)}) collective-permute-start(bf16[2,2,96,2048]{3,2,1,0:T(8,128)(2,1)} %fusion.9), channel_id=1, source_target_pairs={{0,4},{2,6},{4,0},{6,2},{8,12},{10,14},{12,8},{14,10},{16,20},{18,... | collective-permute-start | bytes 4718600 | tf_op jit(solution)/shard_map/ppermute | solution.py:365
  411.0 26.9 %collective-permute-start.12 = (bf16[2,2,2,96,768]{4,3,2,1,0:T(8,128)(2,1)S(1)}, bf16[2,2,2,96,768]{4,3,2,1,0:T(8,128)(2,1)S(1)}, u32[]{:S(2)}, u32[]{:S(2)}) collective-permute-start(bf16[2,2,2,96,768]{4,3,2,1,0:T(8,128)(2,1)S(1)} %dynamic-slice_bitcast_fusion.5), channel_id=1, source_target_pairs={{0,2},{2,0},{4,6},{6,4},{8,10},{10,8},{12,14},{14,12},{16,18},{18,... | collective-permute-start | bytes 3538952 | tf_op jit(solution)/shard_map/ppermute | solution.py:365
  413.6 51.9 %collective-permute-start.14 = (bf16[96,2048]{1,0:T(8,128)(2,1)S(1)}, bf16[96,2048]{1,0:T(8,128)(2,1)S(1)}, u32[]{:S(2)}, u32[]{:S(2)}) collective-permute-start(bf16[96,2048]{1,0:T(8,128)(2,1)S(1)} %fusion.47), channel_id=1, source_target_pairs={{0,16},{2,18},{4,20},{6,22},{8,24},{10,26},{12,28},{14,30},{16,0},... | collective-permute-start | bytes 1179656 | tf_op jit(solution)/shard_map/ppermute | solution.py:365
  419.1 60.7 %collective-permute-start.15 = (bf16[2,96,2048]{2,1,0:T(8,128)(2,1)}, bf16[2,96,2048]{2,1,0:T(8,128)(2,1)}, u32[]{:S(2)}, u32[]{:S(2)}) collective-permute-start(bf16[2,96,2048]{2,1,0:T(8,128)(2,1)} %fusion.30), channel_id=1, source_target_pairs={{0,8},{2,10},{4,12},{6,14},{8,0},{10,2},{12,4},{14,6},{16,24},{18,... | collective-permute-start | bytes 2359304 | tf_op jit(solution)/shard_map/ppermute | solution.py:365
  437.9 98.2 %collective-permute-start.17 = (bf16[2,2,2,96,1536]{4,3,2,1,0:T(8,128)(2,1)}, bf16[2,2,2,96,1536]{4,3,2,1,0:T(8,128)(2,1)}, u32[]{:S(2)}, u32[]{:S(2)}) collective-permute-start(bf16[2,2,2,96,1536]{4,3,2,1,0:T(8,128)(2,1)} %dynamic-slice_bitcast_fusion.4), channel_id=1, source_target_pairs={{0,2},{2,0},{4,6},{6,4},{8,10},{10,8},{12,14},{14,12},{16,18},{18,... | collective-permute-start | bytes 7077896 | tf_op jit(solution)/shard_map/ppermute | solution.py:365
  471.7 67.4 %collective-permute-start.18 = (bf16[2,2,96,768]{3,2,1,0:T(8,128)(2,1)}, bf16[2,2,96,768]{3,2,1,0:T(8,128)(2,1)}, u32[]{:S(2)}, u32[]{:S(2)}) collective-permute-start(bf16[2,2,96,768]{3,2,1,0:T(8,128)(2,1)} %fusion.40), channel_id=1, source_target_pairs={{0,8},{2,10},{4,12},{6,14},{8,0},{10,2},{12,4},{14,6},{16,24},{18,... | collective-permute-start | bytes 1769480 | tf_op jit(solution)/shard_map/ppermute | solution.py:365
  485.1 28.3 %collective-permute-start.39 = (bf16[2,96,2048]{2,1,0:T(8,128)(2,1)}, bf16[2,96,2048]{2,1,0:T(8,128)(2,1)}, u32[]{:S(2)}, u32[]{:S(2)}) collective-permute-start(bf16[2,96,2048]{2,1,0:T(8,128)(2,1)} %fusion.29), channel_id=1, source_target_pairs={{0,8},{2,10},{4,12},{6,14},{8,0},{10,2},{12,4},{14,6},{16,24},{18,... | collective-permute-start | bytes 2359304 | tf_op jit(solution)/shard_map/ppermute | solution.py:365
  565.5 36.9 %collective-permute-start.20 = (bf16[512,1536]{1,0:T(8,128)(2,1)S(1)}, bf16[512,1536]{1,0:T(8,128)(2,1)S(1)}, u32[]{:S(2)}, u32[]{:S(2)}) collective-permute-start(bf16[512,1536]{1,0:T(8,128)(2,1)S(1)} %fusion.12), channel_id=1, source_target_pairs={{0,1},{1,0},{2,3},{3,2},{4,5},{5,4},{6,7},{7,6},{8,9},{9,8},{10,11... | collective-permute-start | bytes 4718600 | tf_op jit(solution)/shard_map/ppermute | solution.py:310
  573.0 30.4 %collective-permute-start.36 = (bf16[2,96,768]{2,1,0:T(8,128)(2,1)S(1)}, bf16[2,96,768]{2,1,0:T(8,128)(2,1)S(1)}, u32[]{:S(2)}, u32[]{:S(2)}) collective-permute-start(bf16[2,96,768]{2,1,0:T(8,128)(2,1)S(1)} %copy-done.40), channel_id=1, source_target_pairs={{0,16},{2,18},{4,20},{6,22},{8,24},{10,26},{12,28},{14,30},{16,0},... | collective-permute-start | bytes 884744 | tf_op jit(solution)/shard_map/ppermute | solution.py:365
  575.4 45.8 %collective-permute-start.26 = (bf16[2,2,96,1536]{3,2,1,0:T(8,128)(2,1)S(1)}, bf16[2,2,96,1536]{3,2,1,0:T(8,128)(2,1)S(1)}, u32[]{:S(2)}, u32[]{:S(2)}) collective-permute-start(bf16[2,2,96,1536]{3,2,1,0:T(8,128)(2,1)S(1)} %copy-done.32), channel_id=1, source_target_pairs={{0,8},{2,10},{4,12},{6,14},{8,0},{10,2},{12,4},{14,6},{16,24},{18,... | collective-permute-start | bytes 3538952 | tf_op jit(solution)/shard_map/ppermute | solution.py:365
  577.0 29.8 %collective-permute-start.35 = (bf16[96,12]{0,1:T(8,128)(2,1)S(1)}, bf16[96,12]{0,1:T(8,128)(2,1)S(1)}, u32[]{:S(2)}, u32[]{:S(2)}) collective-permute-start(bf16[96,12]{0,1:T(8,128)(2,1)S(1)} %fusion.81), channel_id=1, source_target_pairs={{0,4},{2,6},{4,0},{6,2},{8,12},{10,14},{12,8},{14,10},{16,20},{18,... | collective-permute-start | bytes 6920 | tf_op jit(solution)/shard_map/ppermute | solution.py:365
  579.1 42.1 %collective-permute-start.29 = (bf16[2,2,96,1536]{3,2,1,0:T(8,128)(2,1)S(1)}, bf16[2,2,96,1536]{3,2,1,0:T(8,128)(2,1)S(1)}, u32[]{:S(2)}, u32[]{:S(2)}) collective-permute-start(bf16[2,2,96,1536]{3,2,1,0:T(8,128)(2,1)S(1)} %fusion.14), channel_id=1, source_target_pairs={{0,4},{2,6},{4,0},{6,2},{8,12},{10,14},{12,8},{14,10},{16,20},{18,... | collective-permute-start | bytes 3538952 | tf_op jit(solution)/shard_map/ppermute | solution.py:365
  624.0 27.8 %collective-permute-start.30 = (bf16[2,96,1536]{2,1,0:T(8,128)(2,1)S(1)}, bf16[2,96,1536]{2,1,0:T(8,128)(2,1)S(1)}, u32[]{:S(2)}, u32[]{:S(2)}) collective-permute-start(bf16[2,96,1536]{2,1,0:T(8,128)(2,1)S(1)} %get-tuple-element.212), channel_id=1, source_target_pairs={{0,8},{2,10},{4,12},{6,14},{8,0},{10,2},{12,4},{14,6},{16,24},{18,... | collective-permute-start | bytes 1769480 | tf_op jit(solution)/shard_map/ppermute | solution.py:365
  (89 other events, 1319.5 us)

commit v2 on v1

--- a/solution.py
+++ b/solution.py
@@ -250,7 +250,7 @@
         ],
         compiler_params=pltpu.CompilerParams(vmem_limit_bytes=56 << 20),
         cost_estimate=pl.CostEstimate(
-            flops=pairs * 5_000_000_000, bytes_accessed=15_000_000, transcendentals=0
+            flops=7_000_000_000, bytes_accessed=10_000_000, transcendentals=0
         ),
         name="attention_forward",
     )(places, qkvz, decay)
@@ -276,7 +276,7 @@
         ],
         compiler_params=pltpu.CompilerParams(vmem_limit_bytes=56 << 20),
         cost_estimate=pl.CostEstimate(
-            flops=count * 8_000_000_000, bytes_accessed=15_000_000, transcendentals=0
+            flops=7_000_000_000, bytes_accessed=10_000_000, transcendentals=0
         ),
         name="attention_backward",
     )(places, qkvz, grad_mixed, attended, decay, log_total)
@@ -327,66 +327,133 @@
     return first, length // 2 - first
 
 
-def scatter_rows(product, length):
+class Line:
+    def __init__(self):
+        self.token = jnp.zeros((), jnp.float32)
+
+    def start(self, values):
+        self.token, values = tie(self.token, values)
+        return values
+
+    def run(self, step, *values):
+        return self.start(step(*self.start(values)))
+
+
+def scatter_rows(line, product, values, length):
     if not two_devices():
-        return lax.psum_scatter(
-            product(0, length).astype(jnp.bfloat16), "tensor", scatter_dimension=0, tiled=True
-        ).astype(jnp.float32), 0.0
-    sent = product(length // 2, length).astype(jnp.bfloat16)
+        term = line.run(lambda *v: product(0, length, *v).astype(jnp.bfloat16), *values)
+        return lax.psum_scatter(term, "tensor", scatter_dimension=0, tiled=True), jnp.zeros(
+            (), jnp.bfloat16
+        )
+    sent = line.run(lambda *v: product(length // 2, length, *v).astype(jnp.bfloat16), *values)
     arrived = swap(sent)
-    _, start = tie(sent, jnp.zeros((), jnp.float32))
-    return product(0, length // 2), arrived
+    return line.run(lambda *v: product(0, length // 2, *v), *values), arrived
+
+
+def halves_kernel(mine_ref, left_ref, right_ref, kept_ref, sent_ref, total):
+    total[...] = dot_tn(left_ref[...], right_ref[...])
+    count, rows, _ = kept_ref.shape
+    mine = mine_ref[0]
+    for pair in range(count):
+        for ref, place in ((kept_ref, mine), (sent_ref, 1 - mine)):
+            start = pl.multiple_of((2 * pair + place) * rows, 8)
+            ref[pair] = total[pl.ds(start, rows), :].astype(ref.dtype)
+
+
+def weight_halves(left, right, size):
+    length, rows = left.shape
+    columns = right.shape[1]
+    step = 384
+    block = rows // size
+    assert rows % step == 0 and step % (2 * block) == 0
+    count = step // (2 * block)
+    mine = (lax.axis_index("dp") % 2).reshape(1)
+    half = pl.BlockSpec((count, block, columns), lambda i, mine: (i, 0, 0))
+    return pl.pallas_call(
+        halves_kernel,
+        grid_spec=pltpu.PrefetchScalarGridSpec(
+            num_scalar_prefetch=1,
+            grid=(rows // step,),
+            in_specs=[
+                pl.BlockSpec((length, step), lambda i, mine: (0, i)),
+                pl.BlockSpec((length, columns), lambda i, mine: (0, 0)),
+            ],
+            out_specs=[half, half],
+            scratch_shapes=[pltpu.VMEM((step, columns), jnp.float32)],
+        ),
+        out_shape=[jax.ShapeDtypeStruct((size // 2, block, columns), jnp.bfloat16)] * 2,
+        compiler_params=pltpu.CompilerParams(vmem_limit_bytes=40 << 20),
+        cost_estimate=pl.CostEstimate(flops=7_000_000_000, bytes_accessed=10_000_000, transcendentals=0),
+        name="weight_halves",
+    )(mine, left, right)
 
 
 class WeightSum:
-    def __init__(self, partial, masks):
+    def __init__(self, line, left, right, masks):
+        self.line = line
         self.size = lax.axis_size("dp")
-        bits = self.size.bit_length() - 1
-        rows, columns = partial.shape
-        self.terms = [
-            partial.astype(jnp.bfloat16).reshape((2,) * bits + (rows // self.size, columns))
-        ]
-        self.left = list(range(bits - 1, -1, -1))
-        self.masks = list(masks)
-
-    def send(self, critical):
+        self.bits = self.size.bit_length() - 1
+        kept, sent = line.run(lambda *v: weight_halves(*v, self.size), left, right)
+        shape = (2,) * (self.bits - 1) + kept.shape[1:]
+        assert masks[0] == 1
+        self.masks = list(masks[1:])
+        self.left = list(range(self.bits - 1, 0, -1))
+        self.terms = [kept.reshape(shape), self.exchange(sent.reshape(shape), 1)]
+
+    def exchange(self, sent, mask):
+        return lax.ppermute(sent, "dp", [(i, i ^ mask) for i in range(self.size)])
+
+    def arrive(self):
+        self.terms[-1] = self.line.start(self.terms[-1])
+
+    def step(self):
         if not self.masks:
-            return critical
+            return
         mask = self.masks.pop(0)
-        bit = mask.bit_length() - 1
-        axis = self.left.index(bit)
-        self.left.remove(bit)
+        axis = self.left.index(mask.bit_length() - 1)
+        self.left.remove(mask.bit_length() - 1)
         mine = (lax.axis_index("dp") // mask) % 2
+        self.arrive()
         sent = sum(
             lax.dynamic_index_in_dim(term, 1 - mine, axis, False).astype(jnp.float32)
             for term in self.terms
         ).astype(jnp.bfloat16)
-        critical, sent = tie(critical, sent)
-        arrived = lax.ppermute(sent, "dp", [(i, i ^ mask) for i in range(self.size)])
+        sent = self.line.start(sent)
+        arrived = self.exchange(sent, mask)
         self.terms = [
             lax.dynamic_index_in_dim(term, mine, axis, False) for term in self.terms
         ] + [arrived]
-        return critical
-
-    def arrive(self, critical):
-        critical, self.terms[-1] = tie(critical, self.terms[-1])
-        return critical
+
+    def result(self, finish=lambda total: total):
+        while self.masks:
+            self.step()
+        return self.line.run(
+            lambda *terms: finish(sum(term.astype(jnp.float32) for term in terms)), *self.terms
+        )
+
+
+class AllSum:
+    def __init__(self, line, value, rows):
+        self.line, self.value, self.rows, self.mask = line, value, rows, 1
+        self.arrived = jnp.zeros((), value.dtype)
+        self.step()
+
+    def step(self):
+        size = lax.axis_size("dp")
+        if self.mask < size:
+            mask = self.mask
+            self.value = self.line.run(lambda a, b: a + b, self.value, self.arrived)
+            self.arrived = lax.ppermute(self.value, "dp", [(i, i ^ mask) for i in range(size)])
+            self.mask *= 2
 
     def result(self):
-        while self.masks:
-            self.send(jnp.zeros((), jnp.float32))
-        return sum(term.astype(jnp.float32) for term in self.terms)
-
-
-def all_sum(value):
-    size = lax.axis_size("dp")
-    mask = 1
-    while mask < size:
-        value = value + lax.ppermute(value, "dp", [(i, i ^ mask) for i in range(size)])
-        mask *= 2
-    if not two_devices():
-        return lax.psum(value, "tensor")
-    return value + swap(value)
+        while self.mask < lax.axis_size("dp"):
+            self.step()
+        value = self.line.run(lambda a, b: a + b, self.value, self.arrived)
+        top = value[: self.rows]
+        if not two_devices():
+            return lax.psum(top, "tensor"), value[self.rows :]
+        return self.line.run(lambda a, b: a + b, top, swap(top)), value[self.rows :]
 
 
 def pair_columns(weights, pairs):
@@ -455,114 +522,150 @@
     forget_logit = dot_nn(normed, forget_weight) + forget_bias
     decay = by_pairs(running_sum(earlier, jax.nn.log_sigmoid(forget_logit)))
     mixed, attended, log_total = attention_forward(places, qkvz, decay)
-    mixed, grad_branch = tie(mixed, grad_branch)
-    own, arrived = scatter_rows(lambda a, b: dot_nn(mixed[a:b], output_padded), LEN)
-    grad_active = dot_nt(grad_branch, down_weight).astype(jnp.bfloat16)
-    own, grad_active = tie(own, grad_active)
-    hidden_rows = tokens_in + (own + arrived)
+    line = Line()
+    own, arrived = scatter_rows(
+        line, lambda a, b, m, w: dot_nn(m[a:b], w), (mixed, output_padded), LEN
+    )
+    grad_active = line.run(
+        lambda g, w: dot_nt(g, w).astype(jnp.bfloat16), grad_branch, down_weight
+    )
+    hidden_rows = tokens_in + line.run(lambda a, b: a + b, own, arrived)
 
     scale_two, normed_two_rows = rms_rows(hidden_rows, mlp_gain)
     normed_two = gather_rows(normed_two_rows.astype(jnp.bfloat16))
-    gate = dot_nn(normed_two, gate_weight)
-    upward = dot_nn(normed_two, up_weight)
-    active = (jax.nn.silu(gate) * upward).astype(jnp.bfloat16)
-    gate_sigmoid = jax.nn.sigmoid(gate)
-    grad_act_f = grad_active.astype(jnp.float32)
-    grad_gate = (grad_act_f * upward * gate_sigmoid * (1.0 + gate * (1.0 - gate_sigmoid))).astype(
-        jnp.bfloat16
-    )
-    grad_upward = (grad_act_f * gate * gate_sigmoid).astype(jnp.bfloat16)
+
+    def gated(normed_two, grad_active):
+        gate = dot_nn(normed_two, gate_weight)
+        upward = dot_nn(normed_two, up_weight)
+        active = (jax.nn.silu(gate) * upward).astype(jnp.bfloat16)
+        gate_sigmoid = jax.nn.sigmoid(gate)
+        grad_act_f = grad_active.astype(jnp.float32)
+        grad_gate = (
+            grad_act_f * upward * gate_sigmoid * (1.0 + gate * (1.0 - gate_sigmoid))
+        ).astype(jnp.bfloat16)
+        grad_upward = (grad_act_f * gate * gate_sigmoid).astype(jnp.bfloat16)
+        return active, grad_gate, grad_upward
+
+    active, grad_gate, grad_upward = line.run(gated, normed_two, grad_active)
     own, arrived = scatter_rows(
-        lambda a, b: dot_nt(grad_gate[a:b], gate_weight) + dot_nt(grad_upward[a:b], up_weight), LEN
-    )
-    own, grad_branch, active = tie(own, grad_branch, active)
-    down = WeightSum(weight_term(grad_branch, active), near)
-    own = down.send(own)
-    own, normed_two = tie(own, normed_two)
-    gate_sum = WeightSum(weight_term(normed_two, grad_gate), near)
-    own = gate_sum.send(own)
-    own = down.arrive(own)
-    own = down.send(own)
-    grad_normed_two = own + arrived
-    grad_hidden, mlp_gain_part = rms_back(hidden_rows, scale_two, mlp_gain, grad_normed_two)
-    grad_hidden = grad_hidden + out_grad
-    mid_rows = grad_hidden.astype(jnp.bfloat16)
-    mid_rows, normed_two, active = tie(mid_rows, normed_two, active)
-    other = swap(mid_rows) if two_devices() else jnp.zeros((), jnp.float32)
-    up_sum = WeightSum(weight_term(normed_two, grad_upward), near)
-    other = up_sum.send(other)
-    other = gate_sum.arrive(other)
-    other = gate_sum.send(other)
-    last_own, last_arrived = scatter_rows(lambda a, b: dot_nn(active[a:b], down_weight), LEN)
-    other, last_own = tie(other, last_own)
-    other = up_sum.arrive(other)
-    other = up_sum.send(other)
-    grad_mid = gather_rows(mid_rows, other)
-
-    grad_mixed = dot_nt(grad_mid, output_padded).astype(jnp.bfloat16)
-    grad_mixed = down.arrive(grad_mixed)
-    grad_mixed = down.send(grad_mixed)
+        line,
+        lambda a, b, g, u: dot_nt(g[a:b], gate_weight) + dot_nt(u[a:b], up_weight),
+        (grad_gate, grad_upward),
+        LEN,
+    )
+    down = WeightSum(line, grad_branch, active, near)
+    gate_sum = WeightSum(line, normed_two, grad_gate, near)
+    up_sum = WeightSum(line, normed_two, grad_upward, near)
+
+    def middle_grads(own, arrived):
+        grad_hidden, mlp_gain_part = rms_back(hidden_rows, scale_two, mlp_gain, own + arrived)
+        grad_hidden = grad_hidden + out_grad
+        return grad_hidden, mlp_gain_part, grad_hidden.astype(jnp.bfloat16)
+
+    grad_hidden, mlp_gain_part, mid_rows = line.run(middle_grads, own, arrived)
+    grad_mid = gather_rows(mid_rows)
+    down.step()
+    gate_sum.step()
+    last_own, last_arrived = scatter_rows(
+        line, lambda a, b, m, w: dot_nn(m[a:b], w), (active, down_weight), LEN
+    )
+    up_sum.step()
+
+    grad_mid, grad_mixed = line.run(
+        lambda m, w: (m, dot_nt(m, w).astype(jnp.bfloat16)), grad_mid, output_padded
+    )
+    down.step()
     cut = pairs // 2
     saved = (attended, decay, log_total)
-    grads_a, decay_a = attention_backward(places, qkvz, grad_mixed, *saved, 0, cut)
-    grads_a, mixed, grad_mid = tie(grads_a, mixed, grad_mid)
-    output_sum = WeightSum(weight_term(grad_mid, mixed)[:, :width], far)
-    grads_a = output_sum.send(grads_a)
-    grads_a = down.arrive(grads_a)
-    grads_a = down.send(grads_a)
-    grads_a = gate_sum.arrive(grads_a)
-    grads_a = gate_sum.send(grads_a)
-    grads_a, grad_mixed = tie(grads_a, grad_mixed)
-    sum_a = WeightSum(weight_term(normed, grads_a), far)
-    grad_mixed = sum_a.send(grad_mixed)
-    grad_mixed = output_sum.arrive(grad_mixed)
-    grad_mixed = output_sum.send(grad_mixed)
-    grad_mixed, last_arrived = tie(grad_mixed, last_arrived)
-    layer_out = hidden_rows + (last_own + last_arrived)
-    grads_b, decay_b = attention_backward(places, qkvz, grad_mixed, *saved, cut, pairs - cut)
-    for each in (down, gate_sum, up_sum, sum_a, output_sum):
-        grads_b = each.arrive(grads_b)
-        grads_b = each.send(grads_b)
-    grad_decay = from_pairs(jnp.concatenate([decay_a, decay_b], axis=0), heads_here)
-    grad_forget = (running_sum(later, grad_decay) * jax.nn.sigmoid(-forget_logit)).astype(
-        jnp.bfloat16
-    )
-    bias_part = jnp.sum(grad_forget.astype(jnp.float32), axis=0)
+    output_sum = WeightSum(line, grad_mid, mixed[:, :width], far)
+    grads_a, decay_a = line.run(
+        lambda g: attention_backward(places, qkvz, g, *saved, 0, cut), grad_mixed
+    )
+    last_arrived = line.start(last_arrived)
+    gate_sum.step()
+    down.step()
+    output_sum.step()
+    sum_a = WeightSum(line, normed, grads_a, near)
+    grads_b, decay_b = line.run(
+        lambda g: attention_backward(places, qkvz, g, *saved, cut, pairs - cut), grad_mixed
+    )
+    sum_a.step()
+    sum_b = WeightSum(line, normed, grads_b, near)
+    up_sum.step()
+    down.arrive()
+    gate_sum.step()
+    output_sum.step()
     middle = cut * 4 * LANES
 
-    def normed_term(a, b):
+    def forget_term(decay_a, decay_b):
+        grad_decay = from_pairs(jnp.concatenate([decay_a, decay_b], axis=0), heads_here)
+        return (running_sum(later, grad_decay) * jax.nn.sigmoid(-forget_logit)).astype(
+            jnp.bfloat16
+        )
+
+    def normed_term(a, b, grads_a, grads_b, grad_forget):
         term = dot_nt(grads_a[a:b], projection[:, :middle])
         term = term + dot_nt(grads_b[a:b], projection[:, middle:])
         return term + dot_nt(grad_forget[a:b], forget_weight)
 
-    own, arrived = scatter_rows(normed_term, LEN)
-    own, normed = tie(own, normed)
-    sum_b = WeightSum(weight_term(normed, grads_b), near)
-    own = sum_b.send(own)
-    forget_sum = WeightSum(weight_term(normed, grad_forget), far)
-    own = forget_sum.send(own)
-    own = sum_b.arrive(own)
-    own = sum_b.send(own)
-    grad_normed = own + arrived
-    input_part, attn_gain_part = rms_back(tokens_in, scale_one, attn_gain, grad_normed)
-    input_grad = grad_hidden + input_part
-
-    down_grad = down.result().T
+    grad_forget = line.run(forget_term, decay_a, decay_b)
+    values = (grads_a, grads_b, grad_forget)
+    half = LEN // 2
+    if two_devices():
+        sent = line.run(lambda *v: normed_term(half, LEN, *v).astype(jnp.bfloat16), *values)
+        arrived = swap(sent)
+    sum_b.step()
+    if two_devices():
+        own = line.run(lambda *v: normed_term(0, half, *v), *values)
+    else:
+        own, arrived = scatter_rows(line, normed_term, values, LEN)
+
+    def small_terms(grad_forget, normed):
+        bias_part = jnp.sum(grad_forget.astype(jnp.float32), axis=0)
+        bias_row = lax.dynamic_update_slice_in_dim(
+            jnp.zeros((normed.shape[1],), jnp.float32),
+            bias_part,
+            lax.axis_index("tensor") * heads_here,
+            0,
+        )
+        return bias_row, weight_term(grad_forget, normed)
+
+    bias_row, forget_part = line.run(small_terms, grad_forget, normed)
+    sum_a.step()
+    up_sum.step()
+
+    def input_grads(own, arrived):
+        input_part, attn_gain_part = rms_back(tokens_in, scale_one, attn_gain, own + arrived)
+        return grad_hidden + input_part, attn_gain_part
+
+    input_grad, attn_gain_part = line.run(input_grads, own, arrived)
+    small = jnp.concatenate(
+        [jnp.stack([attn_gain_part, mlp_gain_part, bias_row]), forget_part], axis=0
+    )
+    gains = AllSum(line, small, 3)
+    sum_b.step()
+    gains.step()
+    output_sum.step()
+    sum_a.step()
+    gains.step()
+    down_grad = down.result(jnp.transpose)
     gate_grad = gate_sum.result()
+    layer_out = line.run(lambda a, b: hidden_rows + (a + b), last_own, last_arrived)
+    sum_b.step()
+    gains.step()
+    output_grad = output_sum.result(jnp.transpose)
     up_grad = up_sum.result()
-    output_grad = output_sum.result().T
-    forget_grad = forget_sum.result()
+    top, forget_full = gains.result()
+    block_rows = forget_full.shape[1] // lax.axis_size("dp")
+    forget_grad = lax.dynamic_slice_in_dim(
+        forget_full, lax.axis_index("dp") * block_rows, block_rows, 1
+    ).T
     block = jnp.concatenate([sum_a.result(), sum_b.result()], axis=1)
     block = block.reshape(block.shape[0], pairs, 4, LANES)
     query_grad, key_grad, value_grad, outgate_grad = [
         block[:, :, part].reshape(block.shape[0], pairs * LANES)[:, :width] for part in range(4)
     ]
-    bias_full = lax.dynamic_update_slice_in_dim(
-        jnp.zeros((H,), jnp.float32), bias_part, lax.axis_index("tensor") * heads_here, 0
-    )
-    summed = all_sum(jnp.concatenate([attn_gain_part, mlp_gain_part, bias_full]))
-    width = attn_gain_part.shape[0]
-    attn_gain_grad, mlp_gain_grad, bias_grad = jnp.split(summed, [width, 2 * width])
+    attn_gain_grad, mlp_gain_grad, bias_grad = top[0] + line.token, top[1], top[2, :H]
     return (
         layer_out,
         input_grad,

time: 682 us -> 615 us (0.902)
  waiting for transfers between devices: 238 us -> 154 us
  matrix products: 181 us -> 128 us
  Pallas kernels: 83.9 us -> 130 us
  local copies, waits for them, and re-layouts: 56 us -> 77.4 us
    ppermute x32 -> x28, waiting for transfers between devices: 105 us -> 48.2 us  [the longest x24 34.1 us: exchange(): return lax.ppermute(sent, 'dp', [(i, i ^ mask) for i in range(self.size)])]
    pallas_call x0 -> x6, Pallas kernels: none -> 45.4 us  [weight_halves(): pl.pallas_call(halves_kernel, grid_spec=pltpu.PrefetchScalarGridSpec(num_...]
    dot_general x7 -> x1, matrix products: 45.9 us -> 2.57 us  [weight_term(): lax.dot_general(left, right, (((0,), (0,)), ((), ())), preferred_element_...]
    ppermute x9, waiting for transfers between devices: 133 us -> 105 us  [swap(): return lax.ppermute(rows, 'tensor', [(0, 1), (1, 0)])]
    squeeze x6 -> x19, local copies, waits for them, and re-layouts: 8.51 us -> 23.3 us  [the longest x18 22.8 us: step(): lax.dynamic_index_in_dim(term, mine, axis, False)]
    dot_general x10, matrix products: 77.8 us -> 65 us  [dot_nn(): lax.dot_general(left, right, (((1,), (0,)), ((), ())), preferred_element_...]
    optimization_barrier x0 -> x7, local copies, waits for them, and re-layouts: none -> 11.5 us  [tie(): return lax.optimization_barrier(values)]
    ppermute x32 -> x28, starting transfers between devices: 21.9 us -> 26.4 us  [the longest x24 23.4 us: exchange(): return lax.ppermute(sent, 'dp', [(i, i ^ mask) for i in range(self.size)])]
  transfers between devices with their start and end apart: 41 -> 37, of which waited for: 18 -> 14; matrix products, arithmetic and copies ran while one was open for 28% -> 32% of each run, Pallas kernels for 12% -> 20%
where the time goes in v2:
time: 615 us; the launch traced here: 608 us
  waiting for transfers between devices  154 us (25%)
  Pallas kernels  130 us (21%)
  matrix products  128 us (21%)
  other arithmetic  79.1 us (13%)
  local copies, waits for them, and re-layouts  77.4 us (13%)
  starting transfers between devices  36.9 us (6%)
    ppermute x9, waiting for transfers between devices, swap(): return lax.ppermute(rows, 'tensor', [(0, 1), (1, 0)])  105 us
    dot_general x10, matrix products, dot_nn(): lax.dot_general(left, right, (((1,), (0,)), ((), ())), preferred_element_...  65 us
    dot_general x12, matrix products, dot_nt(): lax.dot_general(left, right, (((1,), (1,)), ((), ())), preferred_element_...  60.7 us
    pallas_call x2, Pallas kernels, attention_backward(): pl.pallas_call(backward_kernel, grid_spec=pltpu.PrefetchScalarGridSpec(nu...  53.6 us
    pallas_call x6, Pallas kernels, weight_halves(): pl.pallas_call(halves_kernel, grid_spec=pltpu.PrefetchScalarGridSpec(num_...  45.4 us
    ppermute x24, waiting for transfers between devices, exchange(): return lax.ppermute(sent, 'dp', [(i, i ^ mask) for i in range(self.size)])  34.1 us
    convert_element_type x18, other arithmetic, step(): sent = sum((lax.dynamic_index_in_dim(term, 1 - mine, axis, False).astype(...  33.7 us
    pallas_call x1, Pallas kernels, attention_forward(): pl.pallas_call(forward_kernel, grid_spec=pltpu.PrefetchScalarGridSpec(num...  30.7 us
  transfers between devices with their start and end apart: 37, of which 14 were waited for; matrix products, arithmetic and copies ran while one was open for 32% of the time, Pallas kernels for 20%

profile of v2, /device:TPU:0, one launch (start us, length us, event | category | flops | bytes accessed | tf_op | source)
XLA Modules:
  0.0 608.0 jit_solution(10415341890987006513)
XLA Ops:
  23.8 19.0 %collective-permute-done = bf16[512,1536]{1,0:T(8,128)(2,1)} collective-permute-done((bf16[512,1536]{1,0:T(8,128)(2,1)}, bf16[512,1536]{1,0:T(8,128)(2,1)}, u32[]{:S(2)}, u32[]{:S(2)}) %collective-permute-start) | collective-permute-done | bytes 1572896 | tf_op jit(solution)/shard_map/ppermute | solution.py:310
  51.8 15.1 %convolution_convert_fusion.qkvz_ref = bf16[1024,3072]{1,0:T(8,128)(2,1)} fusion(bf16[1024,1536]{1,0:T(8,128)(2,1)} %copy-done.1, bf16[1536,3072]{1,0:T(8,128)(2,1)} %copy-done.79), kind=kOutput, calls=%fused_computation.9 | convolution fusion | flops 9666822144 | bytes 18874368 | tf_op jit(solution)/shard_map/dot_general | solution.py:19
  66.9 30.7 %attention_forward.1 = (bf16[1024,768]{1,0:T(8,128)(2,1)}, f32[1024,768]{1,0:T(8,128)}, f32[6,1024,2]{2,1,0:T(8,128)}) custom-call(s32[3]{0:T(128)} %pad_add_fusion.where_ref, bf16[1024,3072]{1,0:T(8,128)(2,1)} %convolution_convert_fusion.qkvz_ref, f32[6,1024,2]{2,1,0:T(8,128)} %bitcast.238), custom_call_target="tpu_custom_call" | custom-call | flops 7000000000 | bytes 10000000 | tf_op jit(solution)/shard_map/attention_forward/pallas_call | solution.py:237
  103.7 8.6 %convolution_convert_fusion.1 = bf16[1024,2048]{1,0:T(8,128)(2,1)} fusion(bf16[1024,1536]{1,0:T(8,128)(2,1)S(1)} %constant_dynamic-update-slice_fusion.left_ref, bf16[2048,1536]{1,0:T(8,128)(2,1)S(1)} %bitcast.256), kind=kOutput, calls=%fused_computation.14 | convolution fusion | flops 6444548096 | bytes 13631488 | tf_op jit(solution)/shard_map/dot_general | solution.py:25
  112.4 23.0 %collective-permute-done.2 = bf16[512,1536]{1,0:T(8,128)(2,1)S(1)} collective-permute-done((bf16[512,1536]{1,0:T(8,128)(2,1)S(1)}, bf16[512,1536]{1,0:T(8,128)(2,1)S(1)}, u32[]{:S(2)}, u32[]{:S(2)}) %collective-permute-start.2) | collective-permute-done | bytes 1572896 | tf_op jit(solution)/shard_map/ppermute | solution.py:310
  140.1 33.9 %collective-permute-done.3 = bf16[512,1536]{1,0:T(8,128)(2,1)} collective-permute-done((bf16[512,1536]{1,0:T(8,128)(2,1)}, bf16[512,1536]{1,0:T(8,128)(2,1)}, u32[]{:S(2)}, u32[]{:S(2)}) %collective-permute-start.3) | collective-permute-done | bytes 1572896 | tf_op jit(solution)/shard_map/ppermute | solution.py:310
  176.1 12.0 %fusion.76 = f32[1024,2048]{1,0:T(8,128)} fusion(bf16[1024,1536]{1,0:T(8,128)(2,1)S(1)} %pad_maximum_fusion.1.left_ref, bf16[1536,2048]{1,0:T(8,128)(2,1)} %param.26), kind=kOutput, calls=%fused_computation.253 | convolution fusion | flops 6442450944 | bytes 17825792 | tf_op jit(solution)/shard_map/dot_general | solution.py:19
  188.1 15.2 %fusion.2 = (bf16[1024,2048]{1,0:T(8,128)(2,1)S(1)}, bf16[1024,2048]{1,0:T(8,128)(2,1)}, bf16[1024,2048]{1,0:T(8,128)(2,1)S(1)}) fusion(bf16[1024,2048]{1,0:T(8,128)(2,1)} %convolution_convert_fusion.1, f32[1024,2048]{1,0:T(8,128)} %fusion.76, bf16[1024,1536]{1,0:T(8,128)(2,1)S(1)} %pad_maximum_fusion.1.left_ref, bf16[1536,2048]{1,0:T(8,128)(2,1)} %param.27), kind=kOutput, calls=%fused_computation.4 | convolution fusion | flops 6478102528 | bytes 34603008 | tf_op jit(solution)/shard_map/dot_general | solution.py:19
  203.3 7.3 %fusion.18 = f32[512,1536]{1,0:T(8,128)S(1)} fusion(bf16[1536,2048]{1,0:T(8,128)(2,1)} %param.26, bf16[1024,2048]{1,0:T(8,128)(2,1)S(1)} %get-tuple-element.375.right_ref), kind=kOutput, calls=%fused_computation.54 | convolution fusion | flops 3221225472 | bytes 11534336 | tf_op jit(solution)/shard_map/dot_general | solution.py:25
  210.7 7.9 %fusion.10 = bf16[512,1536]{1,0:T(8,128)(2,1)} fusion(f32[512,1536]{1,0:T(8,128)S(1)} %fusion.18, bf16[1536,2048]{1,0:T(8,128)(2,1)} %param.27, bf16[1024,2048]{1,0:T(8,128)(2,1)S(1)} %get-tuple-element.381.right_ref), kind=kOutput, calls=%fused_computation.44 | convolution fusion | flops 3222798336 | bytes 13107200 | tf_op jit(solution)/shard_map/dot_general | solution.py:25
  224.7 8.5 %convolution_add_fusion.4 = f32[512,1536]{1,0:T(8,128)} fusion(f32[512,1536]{1,0:T(8,128)} %fusion.15, bf16[1536,2048]{1,0:T(8,128)(2,1)} %param.27, bf16[1024,2048]{1,0:T(8,128)(2,1)S(1)} %get-tuple-element.381.right_ref), kind=kOutput, calls=%fused_computation.19 | convolution fusion | flops 3222011904 | bytes 14680064 | tf_op jit(solution)/shard_map/dot_general | solution.py:25
  233.2 9.1 %weight_halves.6 = (bf16[8,96,2048]{2,1,0:T(8,128)(2,1)S(1)}, bf16[8,96,2048]{2,1,0:T(8,128)(2,1)}) custom-call(s32[1]{0:T(128)} %bitcast.3.mine_ref, bf16[1024,1536]{1,0:T(8,128)(2,1)S(1)} %copy-done.17, bf16[1024,2048]{1,0:T(8,128)(2,1)S(1)} %copy-done.27), custom_call_target="tpu_custom_call" | custom-call | flops 7000000000 | bytes 10000000 | tf_op jit(solution)/shard_map/weight_halves/pallas_call | solution.py:372
  244.1 9.3 %weight_halves.7 = (bf16[8,96,2048]{2,1,0:T(8,128)(2,1)S(1)}, bf16[8,96,2048]{2,1,0:T(8,128)(2,1)}) custom-call(s32[1]{0:T(128)} %bitcast.3.mine_ref, bf16[1024,1536]{1,0:T(8,128)(2,1)S(1)} %pad_maximum_fusion.1.left_ref, bf16[1024,2048]{1,0:T(8,128)(2,1)S(1)} %get-tuple-element.375.right_ref), custom_call_target="tpu_custom_call" | custom-call | flops 7000000000 | bytes 10000000 | tf_op jit(solution)/shard_map/weight_halves/pallas_call | solution.py:372
  259.6 8.6 %weight_halves.8 = (bf16[8,96,2048]{2,1,0:T(8,128)(2,1)S(1)}, bf16[8,96,2048]{2,1,0:T(8,128)(2,1)S(1)}) custom-call(s32[1]{0:T(128)} %bitcast.3.mine_ref, bf16[1024,1536]{1,0:T(8,128)(2,1)S(1)} %copy-done.10, bf16[1024,2048]{1,0:T(8,128)(2,1)S(1)} %copy-done.26), custom_call_target="tpu_custom_call" | custom-call | flops 7000000000 | bytes 10000000 | tf_op jit(solution)/shard_map/weight_halves/pallas_call | solution.py:372
  282.2 7.3 %convolution_convert_fusion.2 = bf16[512,1536]{1,0:T(8,128)(2,1)} fusion(bf16[2048,1536]{1,0:T(8,128)(2,1)} %param.28, bf16[1024,2048]{1,0:T(8,128)(2,1)S(1)} %copy-done.28), kind=kOutput, calls=%fused_computation.42 | convolution fusion | flops 3222011904 | bytes 9961472 | tf_op jit(solution)/shard_map/dot_general | solution.py:19
  291.2 7.8 %fusion.11 = f32[512,1536]{1,0:T(8,128)} fusion(bf16[2048,1536]{1,0:T(8,128)(2,1)} %param.28, bf16[1024,2048]{1,0:T(8,128)(2,1)S(1)} %copy-done.28), kind=kOutput, calls=%fused_computation.47 | convolution fusion | flops 3221225472 | bytes 11534336 | tf_op jit(solution)/shard_map/dot_general | solution.py:19
  303.5 9.8 %collective-permute-done.8 = bf16[512,1536]{1,0:T(8,128)(2,1)S(1)} collective-permute-done((bf16[512,1536]{1,0:T(8,128)(2,1)S(1)}, bf16[512,1536]{1,0:T(8,128)(2,1)S(1)}, u32[]{:S(2)}, u32[]{:S(2)}) %collective-permute-start.8) | collective-permute-done | bytes 1572896 | tf_op jit(solution)/shard_map/ppermute | solution.py:310
  336.1 26.9 %attention_backward.2 = (bf16[1024,1536]{1,0:T(8,128)(2,1)}, f32[3,1024,2]{2,1,0:T(8,128)}) custom-call(s32[3]{0:T(128)} %pad_add_fusion.where_ref, bf16[1024,3072]{1,0:T(8,128)(2,1)} %convolution_convert_fusion.qkvz_ref, bf16[1024,768]{1,0:T(8,128)(2,1)} %convolution_convert_fusion.4.gm_ref, f32[1024,768]{1,0:T(8,128)} %get-tuple-element.433.att_ref, ...), custom_call_target="tpu_custom_call" | custom-call | flops 7000000000 | bytes 10000000 | tf_op jit(solution)/shard_map/attention_backward/pallas_call | solution.py:261
  370.6 7.3 %weight_halves.10 = (bf16[8,96,1536]{2,1,0:T(8,128)(2,1)S(1)}, bf16[8,96,1536]{2,1,0:T(8,128)(2,1)}) custom-call(s32[1]{0:T(128)} %bitcast.3.mine_ref, bf16[1024,1536]{1,0:T(8,128)(2,1)S(1)} %copy-done.2, bf16[1024,1536]{1,0:T(8,128)(2,1)S(1)} %copy-done.23), custom_call_target="tpu_custom_call" | custom-call | flops 7000000000 | bytes 10000000 | tf_op jit(solution)/shard_map/weight_halves/pallas_call | solution.py:372
  399.1 26.7 %attention_backward.3 = (bf16[1024,1536]{1,0:T(8,128)(2,1)}, f32[3,1024,2]{2,1,0:T(8,128)}) custom-call(s32[3]{0:T(128)} %pad_add_fusion.where_ref, bf16[1024,3072]{1,0:T(8,128)(2,1)} %convolution_convert_fusion.qkvz_ref, bf16[1024,768]{1,0:T(8,128)(2,1)} %convolution_convert_fusion.4.gm_ref, f32[1024,768]{1,0:T(8,128)} %get-tuple-element.433.att_ref, ...), custom_call_target="tpu_custom_call" | custom-call | flops 7000000000 | bytes 10000000 | tf_op jit(solution)/shard_map/attention_backward/pallas_call | solution.py:261
  500.7 17.2 %collective-permute-done.22 = bf16[512,1536]{1,0:T(8,128)(2,1)} collective-permute-done((bf16[512,1536]{1,0:T(8,128)(2,1)}, bf16[512,1536]{1,0:T(8,128)(2,1)}, u32[]{:S(2)}, u32[]{:S(2)}) %collective-permute-start.22) | collective-permute-done | bytes 1572896 | tf_op jit(solution)/shard_map/ppermute | solution.py:310
  528.2 17.3 %collective-permute-done.23 = bf16[2,2,96,1536]{3,2,0,1:T(8,128)(2,1)S(1)} collective-permute-done((bf16[2,2,96,1536]{3,2,0,1:T(8,128)(2,1)S(1)}, bf16[2,2,96,1536]{3,2,0,1:T(8,128)(2,1)S(1)}, u32[]{:S(2)}, u32[]{:S(2)}) %collective-permute-start.23) | collective-permute-done | bytes 1179680 | tf_op jit(solution)/shard_map/ppermute | solution.py:404
  565.7 9.6 %collective-permute-done.29 = bf16[2,96,1536]{2,1,0:T(8,128)(2,1)S(1)} collective-permute-done((bf16[2,96,1536]{2,1,0:T(8,128)(2,1)S(1)}, bf16[2,96,1536]{2,1,0:T(8,128)(2,1)S(1)}, u32[]{:S(2)}, u32[]{:S(2)}) %collective-permute-start.29) | collective-permute-done | bytes 589856 | tf_op jit(solution)/shard_map/ppermute | solution.py:404
  581.5 9.7 %collective-permute-done.33 = f32[15,1536]{1,0:T(8,128)S(1)} collective-permute-done((f32[15,1536]{1,0:T(8,128)S(1)}, f32[15,1536]{1,0:T(8,128)S(1)}, u32[]{:S(2)}, u32[]{:S(2)}) %collective-permute-start.33) | collective-permute-done | bytes 92192 | tf_op jit(solution)/shard_map/ppermute | solution.py:446
  (397 shorter events, 256.9 us)
Async XLA Ops:
  5.1 37.7 %collective-permute-start = (bf16[512,1536]{1,0:T(8,128)(2,1)}, bf16[512,1536]{1,0:T(8,128)(2,1)}, u32[]{:S(2)}, u32[]{:S(2)}) collective-permute-start(bf16[512,1536]{1,0:T(8,128)(2,1)} %multiply_convert_fusion.2), channel_id=1, source_target_pairs={{0,1},{1,0},{2,3},{3,2},{4,5},{5,4},{6,7},{7,6},{8,9},{9,8},{10,11... | collective-permute-start | bytes 4718600 | tf_op jit(solution)/shard_map/ppermute | solution.py:310
  47.6 54.6 %collective-permute-start.1 = (bf16[512,1536]{1,0:T(8,128)(2,1)}, bf16[512,1536]{1,0:T(8,128)(2,1)}, u32[]{:S(2)}, u32[]{:S(2)}) collective-permute-start(bf16[512,1536]{1,0:T(8,128)(2,1)} %convert_element_type.482), channel_id=1, source_target_pairs={{0,1},{1,0},{2,3},{3,2},{4,5},{5,4},{6,7},{7,6},{8,9},{9,8},{10,11... | collective-permute-start | bytes 4718600 | tf_op jit(solution)/shard_map/ppermute | solution.py:310
  100.3 35.1 %collective-permute-start.2 = (bf16[512,1536]{1,0:T(8,128)(2,1)S(1)}, bf16[512,1536]{1,0:T(8,128)(2,1)S(1)}, u32[]{:S(2)}, u32[]{:S(2)}) collective-permute-start(bf16[512,1536]{1,0:T(8,128)(2,1)S(1)} %convolution_convert_fusion.3), channel_id=1, source_target_pairs={{0,1},{1,0},{2,3},{3,2},{4,5},{5,4},{6,7},{7,6},{8,9},{9,8},{10,11... | collective-permute-start | bytes 4718600 | tf_op jit(solution)/shard_map/ppermute | solution.py:310
  139.5 34.5 %collective-permute-start.3 = (bf16[512,1536]{1,0:T(8,128)(2,1)}, bf16[512,1536]{1,0:T(8,128)(2,1)}, u32[]{:S(2)}, u32[]{:S(2)}) collective-permute-start(bf16[512,1536]{1,0:T(8,128)(2,1)} %multiply_convert_fusion.1), channel_id=1, source_target_pairs={{0,1},{1,0},{2,3},{3,2},{4,5},{5,4},{6,7},{7,6},{8,9},{9,8},{10,11... | collective-permute-start | bytes 4718600 | tf_op jit(solution)/shard_map/ppermute | solution.py:310
  218.6 49.7 %collective-permute-start.4 = (bf16[512,1536]{1,0:T(8,128)(2,1)}, bf16[512,1536]{1,0:T(8,128)(2,1)}, u32[]{:S(2)}, u32[]{:S(2)}) collective-permute-start(bf16[512,1536]{1,0:T(8,128)(2,1)} %fusion.10), channel_id=1, source_target_pairs={{0,1},{1,0},{2,3},{3,2},{4,5},{5,4},{6,7},{7,6},{8,9},{9,8},{10,11... | collective-permute-start | bytes 4718600 | tf_op jit(solution)/shard_map/ppermute | solution.py:310
  244.1 33.4 %collective-permute-start.5 = (bf16[2,2,2,96,2048]{4,3,2,1,0:T(8,128)(2,1)}, bf16[2,2,2,96,2048]{4,3,2,1,0:T(8,128)(2,1)}, u32[]{:S(2)}, u32[]{:S(2)}) collective-permute-start(bf16[2,2,2,96,2048]{4,3,2,1,0:T(8,128)(2,1)} %bitcast.4), channel_id=1, source_target_pairs={{0,2},{2,0},{4,6},{6,4},{8,10},{10,8},{12,14},{14,12},{16,18},{18,... | collective-permute-start | bytes 9437192 | tf_op jit(solution)/shard_map/ppermute | solution.py:404
  276.3 37.0 %collective-permute-start.8 = (bf16[512,1536]{1,0:T(8,128)(2,1)S(1)}, bf16[512,1536]{1,0:T(8,128)(2,1)S(1)}, u32[]{:S(2)}, u32[]{:S(2)}) collective-permute-start(bf16[512,1536]{1,0:T(8,128)(2,1)S(1)} %get-tuple-element.414), channel_id=1, source_target_pairs={{0,1},{1,0},{2,3},{3,2},{4,5},{5,4},{6,7},{7,6},{8,9},{9,8},{10,11... | collective-permute-start | bytes 4718600 | tf_op jit(solution)/shard_map/ppermute | solution.py:310
  289.6 37.3 %collective-permute-start.9 = (bf16[2,2,96,2048]{3,2,0,1:T(8,128)(2,1)S(1)}, bf16[2,2,96,2048]{3,2,0,1:T(8,128)(2,1)S(1)}, u32[]{:S(2)}, u32[]{:S(2)}) collective-permute-start(bf16[2,2,96,2048]{3,2,0,1:T(8,128)(2,1)S(1)} %copy.59), channel_id=1, source_target_pairs={{0,4},{2,6},{4,0},{6,2},{8,12},{10,14},{12,8},{14,10},{16,20},{18,... | collective-permute-start | bytes 4718600 | tf_op jit(solution)/shard_map/ppermute | solution.py:404
  317.3 45.8 %collective-permute-start.10 = (bf16[512,1536]{1,0:T(8,128)(2,1)}, bf16[512,1536]{1,0:T(8,128)(2,1)}, u32[]{:S(2)}, u32[]{:S(2)}) collective-permute-start(bf16[512,1536]{1,0:T(8,128)(2,1)} %convolution_convert_fusion.2), channel_id=1, source_target_pairs={{0,1},{1,0},{2,3},{3,2},{4,5},{5,4},{6,7},{7,6},{8,9},{9,8},{10,11... | collective-permute-start | bytes 4718600 | tf_op jit(solution)/shard_map/ppermute | solution.py:310
  318.4 44.6 %collective-permute-start.11 = (bf16[2,2,96,2048]{3,2,0,1:T(8,128)(2,1)}, bf16[2,2,96,2048]{3,2,0,1:T(8,128)(2,1)}, u32[]{:S(2)}, u32[]{:S(2)}) collective-permute-start(bf16[2,2,96,2048]{3,2,0,1:T(8,128)(2,1)} %copy.60), channel_id=1, source_target_pairs={{0,4},{2,6},{4,0},{6,2},{8,12},{10,14},{12,8},{14,10},{16,20},{18,... | collective-permute-start | bytes 4718600 | tf_op jit(solution)/shard_map/ppermute | solution.py:404
  334.6 34.0 %collective-permute-start.13 = (bf16[2,2,2,96,768]{4,3,2,1,0:T(8,128)(2,1)}, bf16[2,2,2,96,768]{4,3,2,1,0:T(8,128)(2,1)}, u32[]{:S(2)}, u32[]{:S(2)}) collective-permute-start(bf16[2,2,2,96,768]{4,3,2,1,0:T(8,128)(2,1)} %bitcast.20), channel_id=1, source_target_pairs={{0,2},{2,0},{4,6},{6,4},{8,10},{10,8},{12,14},{14,12},{16,18},{18,... | collective-permute-start | bytes 3538952 | tf_op jit(solution)/shard_map/ppermute | solution.py:404
  379.4 48.3 %collective-permute-start.14 = (bf16[2,2,2,96,1536]{4,3,2,1,0:T(8,128)(2,1)}, bf16[2,2,2,96,1536]{4,3,2,1,0:T(8,128)(2,1)}, u32[]{:S(2)}, u32[]{:S(2)}) collective-permute-start(bf16[2,2,2,96,1536]{4,3,2,1,0:T(8,128)(2,1)} %bitcast.23), channel_id=1, source_target_pairs={{0,2},{2,0},{4,6},{6,4},{8,10},{10,8},{12,14},{14,12},{16,18},{18,... | collective-permute-start | bytes 7077896 | tf_op jit(solution)/shard_map/ppermute | solution.py:404
  382.3 58.1 %collective-permute-start.15 = (bf16[2,2,96,2048]{3,2,0,1:T(8,128)(2,1)}, bf16[2,2,96,2048]{3,2,0,1:T(8,128)(2,1)}, u32[]{:S(2)}, u32[]{:S(2)}) collective-permute-start(bf16[2,2,96,2048]{3,2,0,1:T(8,128)(2,1)} %copy.61), channel_id=1, source_target_pairs={{0,4},{2,6},{4,0},{6,2},{8,12},{10,14},{12,8},{14,10},{16,20},{18,... | collective-permute-start | bytes 4718600 | tf_op jit(solution)/shard_map/ppermute | solution.py:404
  390.2 53.2 %collective-permute-start.17 = (bf16[2,96,2048]{2,1,0:T(8,128)(2,1)S(1)}, bf16[2,96,2048]{2,1,0:T(8,128)(2,1)}, u32[]{:S(2)}, u32[]{:S(2)}) collective-permute-start(bf16[2,96,2048]{2,1,0:T(8,128)(2,1)S(1)} %copy-done.62), channel_id=1, source_target_pairs={{0,8},{2,10},{4,12},{6,14},{8,0},{10,2},{12,4},{14,6},{16,24},{18,... | collective-permute-start | bytes 2359304 | tf_op jit(solution)/shard_map/ppermute | solution.py:404
  394.2 49.2 %collective-permute-start.16 = (bf16[96,2048]{1,0:T(8,128)(2,1)S(1)}, bf16[96,2048]{1,0:T(8,128)(2,1)}, u32[]{:S(2)}, u32[]{:S(2)}) collective-permute-start(bf16[96,2048]{1,0:T(8,128)(2,1)S(1)} %copy-done.71), channel_id=1, source_target_pairs={{0,16},{2,18},{4,20},{6,22},{8,24},{10,26},{12,28},{14,30},{16,0},... | collective-permute-start | bytes 1179656 | tf_op jit(solution)/shard_map/ppermute | solution.py:404
  397.6 48.1 %collective-permute-start.18 = (bf16[2,2,96,768]{3,2,1,0:T(8,128)(2,1)}, bf16[2,2,96,768]{3,2,1,0:T(8,128)(2,1)}, u32[]{:S(2)}, u32[]{:S(2)}) collective-permute-start(bf16[2,2,96,768]{3,2,1,0:T(8,128)(2,1)} %fusion.46), channel_id=1, source_target_pairs={{0,8},{2,10},{4,12},{6,14},{8,0},{10,2},{12,4},{14,6},{16,24},{18,... | collective-permute-start | bytes 1769480 | tf_op jit(solution)/shard_map/ppermute | solution.py:404
  430.5 64.5 %collective-permute-start.20 = (bf16[2,2,96,1536]{3,2,0,1:T(8,128)(2,1)}, bf16[2,2,96,1536]{3,2,0,1:T(8,128)(2,1)}, u32[]{:S(2)}, u32[]{:S(2)}) collective-permute-start(bf16[2,2,96,1536]{3,2,0,1:T(8,128)(2,1)} %copy.64), channel_id=1, source_target_pairs={{0,4},{2,6},{4,0},{6,2},{8,12},{10,14},{12,8},{14,10},{16,20},{18,... | collective-permute-start | bytes 3538952 | tf_op jit(solution)/shard_map/ppermute | solution.py:404
  458.0 88.7 %collective-permute-start.25 = (bf16[2,96,768]{2,1,0:T(8,128)(2,1)}, bf16[2,96,768]{2,1,0:T(8,128)(2,1)}, u32[]{:S(2)}, u32[]{:S(2)}) collective-permute-start(bf16[2,96,768]{2,1,0:T(8,128)(2,1)} %fusion.49), channel_id=1, source_target_pairs={{0,16},{2,18},{4,20},{6,22},{8,24},{10,26},{12,28},{14,30},{16,0},... | collective-permute-start | bytes 884744 | tf_op jit(solution)/shard_map/ppermute | solution.py:404
  458.4 100.4 %collective-permute-start.28 = (bf16[96,2048]{1,0:T(8,128)(2,1)}, bf16[96,2048]{1,0:T(8,128)(2,1)}, u32[]{:S(2)}, u32[]{:S(2)}) collective-permute-start(bf16[96,2048]{1,0:T(8,128)(2,1)} %fusion.41), channel_id=1, source_target_pairs={{0,16},{2,18},{4,20},{6,22},{8,24},{10,26},{12,28},{14,30},{16,0},... | collective-permute-start | bytes 1179656 | tf_op jit(solution)/shard_map/ppermute | solution.py:404
  461.0 36.2 %collective-permute-start.21 = (bf16[2,96,2048]{2,1,0:T(8,128)(2,1)}, bf16[2,96,2048]{2,1,0:T(8,128)(2,1)}, u32[]{:S(2)}, u32[]{:S(2)}) collective-permute-start(bf16[2,96,2048]{2,1,0:T(8,128)(2,1)} %fusion.27), channel_id=1, source_target_pairs={{0,8},{2,10},{4,12},{6,14},{8,0},{10,2},{12,4},{14,6},{16,24},{18,... | collective-permute-start | bytes 2359304 | tf_op jit(solution)/shard_map/ppermute | solution.py:404
  480.8 37.1 %collective-permute-start.22 = (bf16[512,1536]{1,0:T(8,128)(2,1)}, bf16[512,1536]{1,0:T(8,128)(2,1)}, u32[]{:S(2)}, u32[]{:S(2)}) collective-permute-start(bf16[512,1536]{1,0:T(8,128)(2,1)} %fusion.9), channel_id=1, source_target_pairs={{0,1},{1,0},{2,3},{3,2},{4,5},{5,4},{6,7},{7,6},{8,9},{9,8},{10,11... | collective-permute-start | bytes 4718600 | tf_op jit(solution)/shard_map/ppermute | solution.py:310
  498.9 78.4 %collective-permute-start.32 = (bf16[96,2048]{1,0:T(8,128)(2,1)S(1)}, bf16[96,2048]{1,0:T(8,128)(2,1)S(1)}, u32[]{:S(2)}, u32[]{:S(2)}) collective-permute-start(bf16[96,2048]{1,0:T(8,128)(2,1)S(1)} %fusion.40), channel_id=1, source_target_pairs={{0,16},{2,18},{4,20},{6,22},{8,24},{10,26},{12,28},{14,30},{16,0},... | collective-permute-start | bytes 1179656 | tf_op jit(solution)/shard_map/ppermute | solution.py:404
  499.2 48.7 %collective-permute-start.26 = (bf16[2,96,1536]{2,1,0:T(8,128)(2,1)S(1)}, bf16[2,96,1536]{2,1,0:T(8,128)(2,1)S(1)}, u32[]{:S(2)}, u32[]{:S(2)}) collective-permute-start(bf16[2,96,1536]{2,1,0:T(8,128)(2,1)S(1)} %fusion.39), channel_id=1, source_target_pairs={{0,8},{2,10},{4,12},{6,14},{8,0},{10,2},{12,4},{14,6},{16,24},{18,... | collective-permute-start | bytes 1769480 | tf_op jit(solution)/shard_map/ppermute | solution.py:404
  551.5 43.5 %collective-permute-start.35 = (bf16[96,1536]{1,0:T(8,128)(2,1)S(1)}, bf16[96,1536]{1,0:T(8,128)(2,1)S(1)}, u32[]{:S(2)}, u32[]{:S(2)}) collective-permute-start(bf16[96,1536]{1,0:T(8,128)(2,1)S(1)} %fusion.48), channel_id=1, source_target_pairs={{0,16},{2,18},{4,20},{6,22},{8,24},{10,26},{12,28},{14,30},{16,0},... | collective-permute-start | bytes 884744 | tf_op jit(solution)/shard_map/ppermute | solution.py:404
  (105 other events, 1491.0 us)

commit v3 on v2

--- a/solution.py
+++ b/solution.py
@@ -56,23 +56,26 @@
     return [ref.at[:, part * LANES : (part + 1) * LANES] for part in range(4)]
 
 
-def forward_kernel(where_ref, qkvz_ref, d_ref, mixed_ref, att_ref, total_ref, qa, qu, ka):
+def forward_kernel(slot, where_ref, qkvz_ref, d_ref, *refs):
+    mixed_ref, att_ref, total_ref, qa, qu, ka = refs[-6:]
     q_ref, k_ref, v_ref, z_ref = quarters(qkvz_ref)
     length = q_ref.shape[0]
     half, quarter = length // 2, length // 4
-    prefix, first, second = where_ref[0], where_ref[1], where_ref[2]
-    first = pl.multiple_of(first, half)
-    second = pl.multiple_of(second, half)
-    early = pl.ds(first, half)
+    prefix = where_ref[0]
+    here, there = slot * half, (1 - slot) * half
+    is_first = where_ref[1] == here
+    here_rows = pl.ds(here, half)
     for head in range(2):
         relative, own = lane_of((length, LANES), head)
         decay = jnp.broadcast_to(d_ref[0, :, head : head + 1], (length, LANES))
+        minus = three_lanes(relative, 3, -decay, lanes_at(relative, 0, 1.0, 0.0))
+        ka[...] = jnp.where(own, k_ref[...].astype(jnp.float32), minus).astype(jnp.bfloat16)
+        relative, own = lane_of((half, LANES), head)
+        decay = jnp.broadcast_to(d_ref[0, here_rows, head : head + 1], (half, LANES))
         plus = three_lanes(relative, 0, decay, lanes_at(relative, 3, 1.0, 0.0))
-        minus = three_lanes(relative, 3, -decay, lanes_at(relative, 0, 1.0, 0.0))
-        scaled = q_ref[...].astype(jnp.float32) * HD**-0.5
+        scaled = q_ref[here_rows, :].astype(jnp.float32) * HD**-0.5
         qa[...] = jnp.where(own, scaled, plus).astype(jnp.bfloat16)
         qu[...] = jnp.where(own, scaled, -plus).astype(jnp.bfloat16)
-        ka[...] = jnp.where(own, k_ref[...].astype(jnp.float32), minus).astype(jnp.bfloat16)
         lanes = slice(head * HD, head * HD + HD)
 
         def finish(rows, parts, lanes=lanes, head=head):
@@ -87,31 +90,37 @@
             att_ref[rows, lanes] = (out / norm)[:, lanes]
             total_ref[0, rows, head : head + 1] = top + jnp.log(norm)
 
-        for part in range(2):
-            rows = pl.ds(first + part * quarter, quarter)
-            i = lax.broadcasted_iota(jnp.int32, (quarter, half), 0) + part * quarter
-            j = lax.broadcasted_iota(jnp.int32, (quarter, half), 1)
-            both = (i < prefix) & (j < prefix)
-            below = dot_nt(qa[rows, :], ka[early, :])
-            above = dot_nt(qu[rows, :], ka[early, :])
-            scores = jnp.where(j <= i, below, jnp.where(both, above, FAR))
-            finish(rows, [(scores, early)])
-        for part in range(2):
-            rows = pl.ds(second + part * quarter, quarter)
-            width = (part + 1) * quarter
-            late = pl.ds(second, width)
-            i = lax.broadcasted_iota(jnp.int32, (quarter, width), 0) + part * quarter
-            j = lax.broadcasted_iota(jnp.int32, (quarter, width), 1)
-            finish(
-                rows,
-                [
-                    (dot_nt(qa[rows, :], ka[early, :]), early),
-                    (jnp.where(j <= i, dot_nt(qa[rows, :], ka[late, :]), FAR), late),
-                ],
-            )
-    mixed_ref[...] = (jax.nn.sigmoid(z_ref[...].astype(jnp.float32)) * att_ref[...]).astype(
-        jnp.bfloat16
-    )
+        @pl.when(is_first)
+        def _(finish=finish):
+            for part in range(2):
+                rows = pl.ds(part * quarter, quarter)
+                i = lax.broadcasted_iota(jnp.int32, (quarter, half), 0) + part * quarter
+                j = lax.broadcasted_iota(jnp.int32, (quarter, half), 1)
+                both = (i < prefix) & (j < prefix)
+                below = dot_nt(qa[rows, :], ka[here_rows, :])
+                above = dot_nt(qu[rows, :], ka[here_rows, :])
+                scores = jnp.where(j <= i, below, jnp.where(both, above, FAR))
+                finish(rows, [(scores, here_rows)])
+
+        @pl.when(jnp.logical_not(is_first))
+        def _(finish=finish):
+            early = pl.ds(there, half)
+            for part in range(2):
+                rows = pl.ds(part * quarter, quarter)
+                width = (part + 1) * quarter
+                late = pl.ds(here, width)
+                i = lax.broadcasted_iota(jnp.int32, (quarter, width), 0) + part * quarter
+                j = lax.broadcasted_iota(jnp.int32, (quarter, width), 1)
+                finish(
+                    rows,
+                    [
+                        (dot_nt(qa[rows, :], ka[early, :]), early),
+                        (jnp.where(j <= i, dot_nt(qa[rows, :], ka[late, :]), FAR), late),
+                    ],
+                )
+
+    outgate = jax.nn.sigmoid(z_ref[here_rows, :].astype(jnp.float32))
+    mixed_ref[...] = (outgate * att_ref[...]).astype(jnp.bfloat16)
 
 
 def backward_kernel(
@@ -231,29 +240,36 @@
     return pl.BlockSpec((1, length, 2), lambda pair, where: (pair + offset, 0, 0))
 
 
-def attention_forward(places, qkvz, decay):
+def attention_forward(places, qkvz, decay, slot, before=None):
     length = qkvz.shape[0]
+    half = length // 2
     pairs = decay.shape[0]
+    rows = pl.BlockSpec((half, LANES), lambda pair, where: (slot, pair))
+    column = pl.BlockSpec((1, half, 2), lambda pair, where: (pair, slot, 0))
+    held = () if before is None else tuple(before)
     return pl.pallas_call(
-        forward_kernel,
+        lambda *refs: forward_kernel(slot, *refs),
         grid_spec=pltpu.PrefetchScalarGridSpec(
             num_scalar_prefetch=1,
             grid=(pairs,),
-            in_specs=[wide(length, 4 * LANES), narrow(length)],
-            out_specs=[wide(length, LANES)] * 2 + [narrow(length)],
-            scratch_shapes=[pltpu.VMEM((length, LANES), jnp.bfloat16)] * 3,
+            in_specs=[wide(length, 4 * LANES), narrow(length)]
+            + [pl.BlockSpec(memory_space=pl.ANY)] * len(held),
+            out_specs=[rows, rows, column],
+            scratch_shapes=[pltpu.VMEM((half, LANES), jnp.bfloat16)] * 2
+            + [pltpu.VMEM((length, LANES), jnp.bfloat16)],
         ),
         out_shape=[
             jax.ShapeDtypeStruct((length, pairs * LANES), jnp.bfloat16),
             jax.ShapeDtypeStruct((length, pairs * LANES), jnp.float32),
             jax.ShapeDtypeStruct((pairs, length, 2), jnp.float32),
         ],
+        input_output_aliases={3 + k: k for k in range(len(held))},
         compiler_params=pltpu.CompilerParams(vmem_limit_bytes=56 << 20),
         cost_estimate=pl.CostEstimate(
-            flops=7_000_000_000, bytes_accessed=10_000_000, transcendentals=0
+            flops=1_000_000, bytes_accessed=1_000_000, transcendentals=0
         ),
         name="attention_forward",
-    )(places, qkvz, decay)
+    )(places, qkvz, decay, *held)
 
 
 def attention_backward(places, qkvz, grad_mixed, attended, decay, log_total, start, count):
@@ -345,9 +361,9 @@
         return lax.psum_scatter(term, "tensor", scatter_dimension=0, tiled=True), jnp.zeros(
             (), jnp.bfloat16
         )
-    sent = line.run(lambda *v: product(length // 2, length, *v).astype(jnp.bfloat16), *values)
-    arrived = swap(sent)
-    return line.run(lambda *v: product(0, length // 2, *v), *values), arrived
+    terms = line.run(lambda *v: product(0, length, *v), *values)
+    sent = line.run(lambda t: t[length // 2 :].astype(jnp.bfloat16), terms)
+    return terms[: length // 2], swap(sent)
 
 
 def halves_kernel(mine_ref, left_ref, right_ref, kept_ref, sent_ref, total):
@@ -383,9 +399,43 @@
         ),
         out_shape=[jax.ShapeDtypeStruct((size // 2, block, columns), jnp.bfloat16)] * 2,
         compiler_params=pltpu.CompilerParams(vmem_limit_bytes=40 << 20),
-        cost_estimate=pl.CostEstimate(flops=7_000_000_000, bytes_accessed=10_000_000, transcendentals=0),
+        cost_estimate=pl.CostEstimate(flops=1_000_000, bytes_accessed=1_000_000, transcendentals=0),
         name="weight_halves",
     )(mine, left, right)
+
+
+def halve_kernel(mine_ref, kept_a, sent_a, kept_b, sent_b, kept_ref, sent_ref):
+    kept = kept_a[...].astype(jnp.float32) + kept_b[...].astype(jnp.float32)
+    sent = sent_a[...].astype(jnp.float32) + sent_b[...].astype(jnp.float32)
+    kept_ref[...] = kept.astype(kept_ref.dtype)
+    sent_ref[...] = sent.astype(sent_ref.dtype)
+
+
+def halve(one, two, axis, mine):
+    lead, (rows, columns) = one.shape[:-2], one.shape[-2:]
+    before = 2**axis
+    after = 2 ** (len(lead) - axis - 1)
+    cut = (before, 2, after, rows, columns)
+    block = (1, pl.squeezed, 1, rows, columns)
+    kept = pl.BlockSpec(block, lambda p, q, mine: (p, mine[0], q, 0, 0))
+    sent = pl.BlockSpec(block, lambda p, q, mine: (p, 1 - mine[0], q, 0, 0))
+    out = pl.BlockSpec((1, 1, rows, columns), lambda p, q, mine: (p, q, 0, 0))
+    one, two = one.reshape(cut), two.reshape(cut)
+    parts = pl.pallas_call(
+        halve_kernel,
+        grid_spec=pltpu.PrefetchScalarGridSpec(
+            num_scalar_prefetch=1,
+            grid=(before, after),
+            in_specs=[kept, sent, kept, sent],
+            out_specs=[out, out],
+        ),
+        out_shape=[jax.ShapeDtypeStruct((before, after, rows, columns), one.dtype)] * 2,
+        compiler_params=pltpu.CompilerParams(vmem_limit_bytes=40 << 20),
+        cost_estimate=pl.CostEstimate(flops=1_000_000, bytes_accessed=1_000_000, transcendentals=0),
+        name="halve",
+    )(mine.reshape(1), one, one, two, two)
+    shape = lead[:axis] + lead[axis + 1 :] + (rows, columns)
+    return [part.reshape(shape) for part in parts]
 
 
 class WeightSum:
@@ -413,16 +463,8 @@
         axis = self.left.index(mask.bit_length() - 1)
         self.left.remove(mask.bit_length() - 1)
         mine = (lax.axis_index("dp") // mask) % 2
-        self.arrive()
-        sent = sum(
-            lax.dynamic_index_in_dim(term, 1 - mine, axis, False).astype(jnp.float32)
-            for term in self.terms
-        ).astype(jnp.bfloat16)
-        sent = self.line.start(sent)
-        arrived = self.exchange(sent, mask)
-        self.terms = [
-            lax.dynamic_index_in_dim(term, mine, axis, False) for term in self.terms
-        ] + [arrived]
+        kept, sent = self.line.run(lambda *t: halve(*t, axis, mine), *self.terms)
+        self.terms = [kept, self.exchange(sent, mask)]
 
     def result(self, finish=lambda total: total):
         while self.masks:
@@ -521,18 +563,30 @@
     qkvz = dot_nn(normed, projection).astype(jnp.bfloat16)
     forget_logit = dot_nn(normed, forget_weight) + forget_bias
     decay = by_pairs(running_sum(earlier, jax.nn.log_sigmoid(forget_logit)))
-    mixed, attended, log_total = attention_forward(places, qkvz, decay)
     line = Line()
-    own, arrived = scatter_rows(
-        line, lambda a, b, m, w: dot_nn(m[a:b], w), (mixed, output_padded), LEN
-    )
+    saved = line.run(lambda d, q: attention_forward(places, q, d, 1), decay, qkvz)
+    grad_branch = line.start(grad_branch)
+    half = LEN // 2
+    if two_devices():
+        sent = line.run(
+            lambda m: dot_nn(m[half:], output_padded).astype(jnp.bfloat16), saved[0]
+        )
+        arrived = swap(sent)
+    saved = line.run(lambda d, q, *b: attention_forward(places, q, d, 0, b), decay, qkvz, *saved)
+    mixed, attended, log_total = saved
+    if two_devices():
+        own = line.run(lambda m: dot_nn(m[:half], output_padded), mixed)
+    else:
+        own, arrived = scatter_rows(
+            line, lambda a, b, m, w: dot_nn(m[a:b], w), (mixed, output_padded), LEN
+        )
+    hidden_rows = tokens_in + line.run(lambda a, b: a + b, own, arrived)
+
+    scale_two, normed_two_rows = rms_rows(hidden_rows, mlp_gain)
+    normed_two = gather_rows(line.start(normed_two_rows.astype(jnp.bfloat16)))
     grad_active = line.run(
         lambda g, w: dot_nt(g, w).astype(jnp.bfloat16), grad_branch, down_weight
     )
-    hidden_rows = tokens_in + line.run(lambda a, b: a + b, own, arrived)
-
-    scale_two, normed_two_rows = rms_rows(hidden_rows, mlp_gain)
-    normed_two = gather_rows(normed_two_rows.astype(jnp.bfloat16))
 
     def gated(normed_two, grad_active):
         gate = dot_nn(normed_two, gate_weight)
@@ -609,16 +663,21 @@
         return term + dot_nt(grad_forget[a:b], forget_weight)
 
     grad_forget = line.run(forget_term, decay_a, decay_b)
+    sum_a.step()
     values = (grads_a, grads_b, grad_forget)
-    half = LEN // 2
     if two_devices():
         sent = line.run(lambda *v: normed_term(half, LEN, *v).astype(jnp.bfloat16), *values)
         arrived = swap(sent)
+    up_sum.arrive()
+    gate_sum.arrive()
     sum_b.step()
     if two_devices():
         own = line.run(lambda *v: normed_term(0, half, *v), *values)
     else:
         own, arrived = scatter_rows(line, normed_term, values, LEN)
+
+    up_sum.step()
+    output_sum.arrive()
 
     def small_terms(grad_forget, normed):
         bias_part = jnp.sum(grad_forget.astype(jnp.float32), axis=0)
@@ -632,12 +691,12 @@
 
     bias_row, forget_part = line.run(small_terms, grad_forget, normed)
     sum_a.step()
-    up_sum.step()
 
     def input_grads(own, arrived):
         input_part, attn_gain_part = rms_back(tokens_in, scale_one, attn_gain, own + arrived)
         return grad_hidden + input_part, attn_gain_part
 
+    sum_b.arrive()
     input_grad, attn_gain_part = line.run(input_grads, own, arrived)
     small = jnp.concatenate(
         [jnp.stack([attn_gain_part, mlp_gain_part, bias_row]), forget_part], axis=0
@@ -645,12 +704,13 @@
     gains = AllSum(line, small, 3)
     sum_b.step()
     gains.step()
+    up_sum.arrive()
     output_sum.step()
-    sum_a.step()
-    gains.step()
+    sum_a.arrive()
     down_grad = down.result(jnp.transpose)
     gate_grad = gate_sum.result()
     layer_out = line.run(lambda a, b: hidden_rows + (a + b), last_own, last_arrived)
+    gains.step()
     sum_b.step()
     gains.step()
     output_grad = output_sum.result(jnp.transpose)

time: 615 us -> 605 us (0.984)
  Pallas kernels: 130 us -> 174 us
  other arithmetic: 79.1 us -> 47.6 us
  matrix products: 128 us -> 116 us
  local copies, waits for them, and re-layouts: 77.4 us -> 66.8 us
    pallas_call x1 -> x20, Pallas kernels: 30.7 us -> 74.9 us  [the longest x2 40.3 us: attention_forward(): pl.pallas_call(lambda *refs: forward_kernel(slot, *refs), grid_spec=pltpu...]
    ppermute x24, waiting for transfers between devices: 34.1 us -> 72.7 us  [exchange(): return lax.ppermute(sent, 'dp', [(i, i ^ mask) for i in range(self.size)])]
    convert_element_type x19 -> x1, other arithmetic: 35.2 us -> 0.32 us  [local(): normed_two = gather_rows(line.start(normed_two_rows.astype(jnp.bfloat16)))]
    ppermute x9, waiting for transfers between devices: 105 us -> 72.4 us  [swap(): return lax.ppermute(rows, 'tensor', [(0, 1), (1, 0)])]
    squeeze x18 -> x0, local copies, waits for them, and re-layouts: 22.8 us -> none  [step(): lax.dynamic_index_in_dim(term, mine, axis, False)]
    unnamed x211 -> x233, local copies, waits for them, and re-layouts: 27.3 us -> 39.8 us
    dot_general x10 -> x9, matrix products: 65 us -> 56.7 us  [dot_nn(): lax.dot_general(left, right, (((1,), (0,)), ((), ())), preferred_element_...]
    optimization_barrier x7 -> x2, local copies, waits for them, and re-layouts: 11.5 us -> 4.97 us  [tie(): return lax.optimization_barrier(values)]
  transfers between devices with their start and end apart: 37 -> 37, of which waited for: 14 -> 14; matrix products, arithmetic and copies ran while one was open for 32% -> 20% of each run, Pallas kernels for 20% -> 27%
where the time goes in v3:
time: 605 us; the launch traced here: 599 us
  Pallas kernels  174 us (29%)
  waiting for transfers between devices  155 us (26%)
  matrix products  116 us (19%)
  local copies, waits for them, and re-layouts  66.8 us (11%)
  other arithmetic  47.6 us (8%)
  starting transfers between devices  36 us (6%)
    ppermute x24, waiting for transfers between devices, exchange(): return lax.ppermute(sent, 'dp', [(i, i ^ mask) for i in range(self.size)])  72.7 us
    ppermute x9, waiting for transfers between devices, swap(): return lax.ppermute(rows, 'tensor', [(0, 1), (1, 0)])  72.4 us
    dot_general x9, matrix products, dot_nn(): lax.dot_general(left, right, (((1,), (0,)), ((), ())), preferred_element_...  56.7 us
    dot_general x10, matrix products, dot_nt(): lax.dot_general(left, right, (((1,), (1,)), ((), ())), preferred_element_...  56.4 us
    pallas_call x2, Pallas kernels, attention_backward(): pl.pallas_call(backward_kernel, grid_spec=pltpu.PrefetchScalarGridSpec(nu...  53.3 us
    pallas_call x6, Pallas kernels, weight_halves(): pl.pallas_call(halves_kernel, grid_spec=pltpu.PrefetchScalarGridSpec(num_...  46 us
    pallas_call x2, Pallas kernels, attention_forward(): pl.pallas_call(lambda *refs: forward_kernel(slot, *refs), grid_spec=pltpu...  40.3 us
    unnamed x233, local copies, waits for them, and re-layouts  39.8 us
  transfers between devices with their start and end apart: 37, of which 14 were waited for; matrix products, arithmetic and copies ran while one was open for 20% of the time, Pallas kernels for 27%

profile of v3, /device:TPU:0, one launch (start us, length us, event | category | flops | bytes accessed | tf_op | source)
XLA Modules:
  0.0 598.6 jit_solution(3046901429860708695)
XLA Ops:
  23.8 19.0 %collective-permute-done = bf16[512,1536]{1,0:T(8,128)(2,1)} collective-permute-done((bf16[512,1536]{1,0:T(8,128)(2,1)}, bf16[512,1536]{1,0:T(8,128)(2,1)}, u32[]{:S(2)}, u32[]{:S(2)}) %collective-permute-start) | collective-permute-done | bytes 1572896 | tf_op jit(solution)/shard_map/ppermute | solution.py:326
  52.0 15.1 %convolution_convert_fusion.refs_1_.qkvz_ref = bf16[1024,3072]{1,0:T(8,128)(2,1)} fusion(bf16[1024,1536]{1,0:T(8,128)(2,1)} %copy-done.1, bf16[1536,3072]{1,0:T(8,128)(2,1)} %copy-done.94), kind=kOutput, calls=%fused_computation.9 | convolution fusion | flops 9666822144 | bytes 18874368 | tf_op jit(solution)/shard_map/dot_general | solution.py:19
  67.1 21.3 %attention_forward.2 = (bf16[1024,768]{1,0:T(8,128)(2,1)}, f32[1024,768]{1,0:T(8,128)}, f32[6,1024,2]{2,1,0:T(8,128)}) custom-call(s32[3]{0:T(128)} %pad_add_fusion.refs_0_.where_ref, bf16[1024,3072]{1,0:T(8,128)(2,1)} %convolution_convert_fusion.refs_1_.qkvz_ref, f32[6,1024,2]{2,1,0:T(8,128)} %bitcast.205), custom_call_target="tpu_custom_call" | custom-call | flops 1000000 | bytes 1000000 | tf_op jit(solution)/shard_map/attention_forward/pallas_call | solution.py:250
  92.8 19.0 %attention_forward.3 = (bf16[1024,768]{1,0:T(8,128)(2,1)}, f32[1024,768]{1,0:T(8,128)}, f32[6,1024,2]{2,1,0:T(8,128)}) custom-call(s32[3]{0:T(128)} %pad_add_fusion.refs_0_.where_ref, bf16[1024,3072]{1,0:T(8,128)(2,1)} %convolution_convert_fusion.refs_1_.qkvz_ref, ...), custom_call_target="tpu_custom_call", output_to_operand_aliasing={{0}: (3, {}), {1}: (4, {}), {2}: (5, {})} | custom-call | flops 1000000 | bytes 1000000 | tf_op jit(solution)/shard_map/attention_forward/pallas_call | solution.py:250
  114.4 13.6 %collective-permute-done.2 = bf16[512,1536]{1,0:T(8,128)(2,1)S(1)} collective-permute-done((bf16[512,1536]{1,0:T(8,128)(2,1)}, bf16[512,1536]{1,0:T(8,128)(2,1)S(1)}, u32[]{:S(2)}, u32[]{:S(2)}) %collective-permute-start.2) | collective-permute-done | bytes 1572896 | tf_op jit(solution)/shard_map/ppermute | solution.py:326
  132.2 8.3 %convolution_convert_fusion.1 = bf16[1024,2048]{1,0:T(8,128)(2,1)} fusion(bf16[1024,1536]{1,0:T(8,128)(2,1)S(1)} %pad_maximum_fusion.1.left_ref, bf16[2048,1536]{1,0:T(8,128)(2,1)S(1)} %bitcast.218), kind=kOutput, calls=%fused_computation.15 | convolution fusion | flops 6444548096 | bytes 13631488 | tf_op jit(solution)/shard_map/dot_general | solution.py:25
  140.5 24.7 %collective-permute-done.3 = bf16[512,1536]{1,0:T(8,128)(2,1)S(1)} collective-permute-done((bf16[512,1536]{1,0:T(8,128)(2,1)S(1)}, bf16[512,1536]{1,0:T(8,128)(2,1)S(1)}, u32[]{:S(2)}, u32[]{:S(2)}) %collective-permute-start.3) | collective-permute-done | bytes 1572896 | tf_op jit(solution)/shard_map/ppermute | solution.py:326
  165.4 9.0 %fusion.47 = f32[1024,2048]{1,0:T(8,128)} fusion(bf16[1024,1536]{1,0:T(8,128)(2,1)S(1)} %constant_dynamic-update-slice_fusion.left_ref, bf16[1536,2048]{1,0:T(8,128)(2,1)S(1)} %bitcast.216), kind=kOutput, calls=%fused_computation.176 | convolution fusion | flops 6442450944 | bytes 17825792 | tf_op jit(solution)/shard_map/dot_general | solution.py:19
  174.3 15.2 %fusion.2 = (bf16[1024,2048]{1,0:T(8,128)(2,1)S(1)}, bf16[1024,2048]{1,0:T(8,128)(2,1)}, bf16[1024,2048]{1,0:T(8,128)(2,1)S(1)}) fusion(bf16[1024,2048]{1,0:T(8,128)(2,1)} %convolution_convert_fusion.1, f32[1024,2048]{1,0:T(8,128)} %fusion.47, bf16[1024,1536]{1,0:T(8,128)(2,1)S(1)} %constant_dynamic-update-slice_fusion.left_ref, bf16[1536,2048]{1,0:T(8,128)(2,1)} %param.27), kind=kOutput, calls=%fused_computation.4 | convolution fusion | flops 6478102528 | bytes 34603008 | tf_op jit(solution)/shard_map/dot_general | solution.py:19
  189.6 13.1 %fusion.48 = f32[1024,1536]{1,0:T(8,128)} fusion(bf16[1024,2048]{1,0:T(8,128)(2,1)S(1)} %get-tuple-element.479.right_ref, bf16[1536,2048]{1,0:T(8,128)(2,1)} %param.26), kind=kOutput, calls=%fused_computation.177 | convolution fusion | flops 6442450944 | bytes 16777216 | tf_op jit(solution)/shard_map/dot_general | solution.py:25
  202.7 10.4 %convolution_add_fusion = f32[1024,1536]{1,0:T(8,128)S(1)} fusion(f32[1024,1536]{1,0:T(8,128)} %fusion.48, bf16[1024,2048]{1,0:T(8,128)(2,1)S(1)} %get-tuple-element.485.right_ref, bf16[1536,2048]{1,0:T(8,128)(2,1)} %param.27), kind=kOutput, calls=%fused_computation.10 | convolution fusion | flops 6444023808 | bytes 23068672 | tf_op jit(solution)/shard_map/dot_general | solution.py:25
  221.7 9.1 %weight_halves.6 = (bf16[8,96,2048]{2,1,0:T(8,128)(2,1)S(1)}, bf16[8,96,2048]{2,1,0:T(8,128)(2,1)}) custom-call(s32[1]{0:T(128)} %bitcast.3.mine_ref, bf16[1024,1536]{1,0:T(8,128)(2,1)S(1)} %copy-done.8, bf16[1024,2048]{1,0:T(8,128)(2,1)S(1)} %copy-done.21), custom_call_target="tpu_custom_call" | custom-call | flops 1000000 | bytes 1000000 | tf_op jit(solution)/shard_map/weight_halves/pallas_call | solution.py:388
  230.9 9.2 %weight_halves.7 = (bf16[8,96,2048]{2,1,0:T(8,128)(2,1)S(1)}, bf16[8,96,2048]{2,1,0:T(8,128)(2,1)}) custom-call(s32[1]{0:T(128)} %bitcast.3.mine_ref, bf16[1024,1536]{1,0:T(8,128)(2,1)S(1)} %copy-done.5, bf16[1024,2048]{1,0:T(8,128)(2,1)S(1)} %copy-done.26), custom_call_target="tpu_custom_call" | custom-call | flops 1000000 | bytes 1000000 | tf_op jit(solution)/shard_map/weight_halves/pallas_call | solution.py:388
  247.3 9.2 %weight_halves.8 = (bf16[8,96,2048]{2,1,0:T(8,128)(2,1)S(1)}, bf16[8,96,2048]{2,1,0:T(8,128)(2,1)}) custom-call(s32[1]{0:T(128)} %bitcast.3.mine_ref, bf16[1024,1536]{1,0:T(8,128)(2,1)S(1)} %copy-done.6, bf16[1024,2048]{1,0:T(8,128)(2,1)S(1)} %copy-done.24), custom_call_target="tpu_custom_call" | custom-call | flops 1000000 | bytes 1000000 | tf_op jit(solution)/shard_map/weight_halves/pallas_call | solution.py:388
  277.0 8.9 %fusion.49 = f32[1024,1536]{1,0:T(8,128)S(1)} fusion(bf16[1024,2048]{1,0:T(8,128)(2,1)S(1)} %copy-done.22, bf16[2048,1536]{1,0:T(8,128)(2,1)} %param.28), kind=kOutput, calls=%fused_computation.178 | convolution fusion | flops 6442450944 | bytes 16777216 | tf_op jit(solution)/shard_map/dot_general | solution.py:19
  292.1 9.8 %collective-permute-done.8 = bf16[512,1536]{1,0:T(8,128)(2,1)} collective-permute-done((bf16[512,1536]{1,0:T(8,128)(2,1)}, bf16[512,1536]{1,0:T(8,128)(2,1)}, u32[]{:S(2)}, u32[]{:S(2)}) %collective-permute-start.8) | collective-permute-done | bytes 1572896 | tf_op jit(solution)/shard_map/ppermute | solution.py:326
  309.3 36.1 %collective-permute-done.9 = bf16[2,2,96,2048]{3,2,1,0:T(8,128)(2,1)S(1)} collective-permute-done((bf16[2,2,96,2048]{3,2,1,0:T(8,128)(2,1)}, bf16[2,2,96,2048]{3,2,1,0:T(8,128)(2,1)S(1)}, u32[]{:S(2)}, u32[]{:S(2)}) %collective-permute-start.9) | collective-permute-done | bytes 1572896 | tf_op jit(solution)/shard_map/ppermute | solution.py:454
  353.5 26.6 %attention_backward.2 = (bf16[1024,1536]{1,0:T(8,128)(2,1)}, f32[3,1024,2]{2,1,0:T(8,128)}) custom-call(s32[3]{0:T(128)} %pad_add_fusion.refs_0_.where_ref, bf16[1024,3072]{1,0:T(8,128)(2,1)} %convolution_convert_fusion.refs_1_.qkvz_ref, bf16[1024,768]{1,0:T(8,128)(2,1)} %convolution_convert_fusion.3.gm_ref, f32[1024,768]{1,0:T(8,128)} %get-tuple-element.548.att_ref, ...), custom_call_target="tpu_custom_call" | custom-call | flops 7000000000 | bytes 10000000 | tf_op jit(solution)/shard_map/attention_backward/pallas_call | solution.py:277
  389.1 7.3 %weight_halves.10 = (bf16[8,96,1536]{2,1,0:T(8,128)(2,1)S(1)}, bf16[8,96,1536]{2,1,0:T(8,128)(2,1)}) custom-call(s32[1]{0:T(128)} %bitcast.3.mine_ref, bf16[1024,1536]{1,0:T(8,128)(2,1)S(1)} %copy-done.2, bf16[1024,1536]{1,0:T(8,128)(2,1)S(1)} %copy-done.27), custom_call_target="tpu_custom_call" | custom-call | flops 1000000 | bytes 1000000 | tf_op jit(solution)/shard_map/weight_halves/pallas_call | solution.py:388
  402.7 26.7 %attention_backward.3 = (bf16[1024,1536]{1,0:T(8,128)(2,1)}, f32[3,1024,2]{2,1,0:T(8,128)}) custom-call(s32[3]{0:T(128)} %pad_add_fusion.refs_0_.where_ref, bf16[1024,3072]{1,0:T(8,128)(2,1)} %convolution_convert_fusion.refs_1_.qkvz_ref, bf16[1024,768]{1,0:T(8,128)(2,1)} %convolution_convert_fusion.3.gm_ref, f32[1024,768]{1,0:T(8,128)} %get-tuple-element.548.att_ref, ...), custom_call_target="tpu_custom_call" | custom-call | flops 7000000000 | bytes 10000000 | tf_op jit(solution)/shard_map/attention_backward/pallas_call | solution.py:277
  436.1 6.5 %weight_halves.11 = (bf16[8,96,1536]{2,1,0:T(8,128)(2,1)S(1)}, bf16[8,96,1536]{2,1,0:T(8,128)(2,1)S(1)}) custom-call(s32[1]{0:T(128)} %bitcast.3.mine_ref, bf16[1024,1536]{1,0:T(8,128)(2,1)S(1)} %copy-done.3, bf16[1024,1536]{1,0:T(8,128)(2,1)S(1)} %copy-done.29), custom_call_target="tpu_custom_call" | custom-call | flops 1000000 | bytes 1000000 | tf_op jit(solution)/shard_map/weight_halves/pallas_call | solution.py:388
  480.8 19.7 %collective-permute-done.20 = bf16[2,96,2048]{2,1,0:T(8,128)(2,1)S(1)} collective-permute-done((bf16[2,96,2048]{2,1,0:T(8,128)(2,1)}, bf16[2,96,2048]{2,1,0:T(8,128)(2,1)S(1)}, u32[]{:S(2)}, u32[]{:S(2)}) %collective-permute-start.20) | collective-permute-done | bytes 786464 | tf_op jit(solution)/shard_map/ppermute | solution.py:454
  524.8 7.2 %collective-permute-done.25 = bf16[2,2,96,1536]{3,2,1,0:T(8,128)(2,1)} collective-permute-done((bf16[2,2,96,1536]{3,2,1,0:T(8,128)(2,1)}, bf16[2,2,96,1536]{3,2,1,0:T(8,128)(2,1)}, u32[]{:S(2)}, u32[]{:S(2)}) %collective-permute-start.25) | collective-permute-done | bytes 1179680 | tf_op jit(solution)/shard_map/ppermute | solution.py:454
  573.8 8.5 %collective-permute-done.34 = f32[15,1536]{1,0:T(8,128)S(1)} collective-permute-done((f32[15,1536]{1,0:T(8,128)S(1)}, f32[15,1536]{1,0:T(8,128)S(1)}, u32[]{:S(2)}, u32[]{:S(2)}) %collective-permute-start.34) | collective-permute-done | bytes 92192 | tf_op jit(solution)/shard_map/ppermute | solution.py:488
  (400 shorter events, 242.1 us)
Async XLA Ops:
  5.1 37.7 %collective-permute-start = (bf16[512,1536]{1,0:T(8,128)(2,1)}, bf16[512,1536]{1,0:T(8,128)(2,1)}, u32[]{:S(2)}, u32[]{:S(2)}) collective-permute-start(bf16[512,1536]{1,0:T(8,128)(2,1)} %multiply_convert_fusion.2), channel_id=1, source_target_pairs={{0,1},{1,0},{2,3},{3,2},{4,5},{5,4},{6,7},{7,6},{8,9},{9,8},{10,11... | collective-permute-start | bytes 4718600 | tf_op jit(solution)/shard_map/ppermute | solution.py:326
  47.6 40.8 %collective-permute-start.1 = (bf16[512,1536]{1,0:T(8,128)(2,1)}, bf16[512,1536]{1,0:T(8,128)(2,1)}, u32[]{:S(2)}, u32[]{:S(2)}) collective-permute-start(bf16[512,1536]{1,0:T(8,128)(2,1)} %convert_element_type.100), channel_id=1, source_target_pairs={{0,1},{1,0},{2,3},{3,2},{4,5},{5,4},{6,7},{7,6},{8,9},{9,8},{10,11... | collective-permute-start | bytes 4718600 | tf_op jit(solution)/shard_map/ppermute | solution.py:326
  92.8 35.2 %collective-permute-start.2 = (bf16[512,1536]{1,0:T(8,128)(2,1)}, bf16[512,1536]{1,0:T(8,128)(2,1)S(1)}, u32[]{:S(2)}, u32[]{:S(2)}) collective-permute-start(bf16[512,1536]{1,0:T(8,128)(2,1)} %convolution_convert_fusion.2), channel_id=1, source_target_pairs={{0,1},{1,0},{2,3},{3,2},{4,5},{5,4},{6,7},{7,6},{8,9},{9,8},{10,11... | collective-permute-start | bytes 4718600 | tf_op jit(solution)/shard_map/ppermute | solution.py:326
  131.0 34.2 %collective-permute-start.3 = (bf16[512,1536]{1,0:T(8,128)(2,1)S(1)}, bf16[512,1536]{1,0:T(8,128)(2,1)S(1)}, u32[]{:S(2)}, u32[]{:S(2)}) collective-permute-start(bf16[512,1536]{1,0:T(8,128)(2,1)S(1)} %multiply_convert_fusion.1), channel_id=1, source_target_pairs={{0,1},{1,0},{2,3},{3,2},{4,5},{5,4},{6,7},{7,6},{8,9},{9,8},{10,11... | collective-permute-start | bytes 4718600 | tf_op jit(solution)/shard_map/ppermute | solution.py:326
  217.1 39.4 %collective-permute-start.4 = (bf16[512,1536]{1,0:T(8,128)(2,1)}, bf16[512,1536]{1,0:T(8,128)(2,1)}, u32[]{:S(2)}, u32[]{:S(2)}) collective-permute-start(bf16[512,1536]{1,0:T(8,128)(2,1)} %slice.268), channel_id=1, source_target_pairs={{0,1},{1,0},{2,3},{3,2},{4,5},{5,4},{6,7},{7,6},{8,9},{9,8},{10,11... | collective-permute-start | bytes 4718600 | tf_op jit(solution)/shard_map/ppermute | solution.py:326
  230.9 35.4 %collective-permute-start.5 = (bf16[2,2,2,96,2048]{4,3,2,1,0:T(8,128)(2,1)}, bf16[2,2,2,96,2048]{4,3,2,1,0:T(8,128)(2,1)}, u32[]{:S(2)}, u32[]{:S(2)}) collective-permute-start(bf16[2,2,2,96,2048]{4,3,2,1,0:T(8,128)(2,1)} %bitcast.5), channel_id=1, source_target_pairs={{0,2},{2,0},{4,6},{6,4},{8,10},{10,8},{12,14},{14,12},{16,18},{18,... | collective-permute-start | bytes 9437192 | tf_op jit(solution)/shard_map/ppermute | solution.py:454
  256.5 30.9 %collective-permute-start.7 = (bf16[2,2,2,96,2048]{4,3,2,1,0:T(8,128)(2,1)}, bf16[2,2,2,96,2048]{4,3,2,1,0:T(8,128)(2,1)S(1)}, u32[]{:S(2)}, u32[]{:S(2)}) collective-permute-start(bf16[2,2,2,96,2048]{4,3,2,1,0:T(8,128)(2,1)} %bitcast.18), channel_id=1, source_target_pairs={{0,2},{2,0},{4,6},{6,4},{8,10},{10,8},{12,14},{14,12},{16,18},{18,... | collective-permute-start | bytes 9437192 | tf_op jit(solution)/shard_map/ppermute | solution.py:454
  264.8 37.1 %collective-permute-start.8 = (bf16[512,1536]{1,0:T(8,128)(2,1)}, bf16[512,1536]{1,0:T(8,128)(2,1)}, u32[]{:S(2)}, u32[]{:S(2)}) collective-permute-start(bf16[512,1536]{1,0:T(8,128)(2,1)} %get-tuple-element.525), channel_id=1, source_target_pairs={{0,1},{1,0},{2,3},{3,2},{4,5},{5,4},{6,7},{7,6},{8,9},{9,8},{10,11... | collective-permute-start | bytes 4718600 | tf_op jit(solution)/shard_map/ppermute | solution.py:326
  274.9 105.2 %collective-permute-start.11 = (bf16[2,2,96,2048]{3,2,1,0:T(8,128)(2,1)}, bf16[2,2,96,2048]{3,2,1,0:T(8,128)(2,1)}, u32[]{:S(2)}, u32[]{:S(2)}) collective-permute-start(bf16[2,2,96,2048]{3,2,1,0:T(8,128)(2,1)} %bitcast.16), channel_id=1, source_target_pairs={{0,4},{2,6},{4,0},{6,2},{8,12},{10,14},{12,8},{14,10},{16,20},{18,... | collective-permute-start | bytes 4718600 | tf_op jit(solution)/shard_map/ppermute | solution.py:454
  276.4 68.9 %collective-permute-start.9 = (bf16[2,2,96,2048]{3,2,1,0:T(8,128)(2,1)}, bf16[2,2,96,2048]{3,2,1,0:T(8,128)(2,1)S(1)}, u32[]{:S(2)}, u32[]{:S(2)}) collective-permute-start(bf16[2,2,96,2048]{3,2,1,0:T(8,128)(2,1)} %bitcast.198), channel_id=1, source_target_pairs={{0,4},{2,6},{4,0},{6,2},{8,12},{10,14},{12,8},{14,10},{16,20},{18,... | collective-permute-start | bytes 4718600 | tf_op jit(solution)/shard_map/ppermute | solution.py:454
  304.0 76.1 %collective-permute-start.10 = (bf16[512,1536]{1,0:T(8,128)(2,1)}, bf16[512,1536]{1,0:T(8,128)(2,1)}, u32[]{:S(2)}, u32[]{:S(2)}) collective-permute-start(bf16[512,1536]{1,0:T(8,128)(2,1)} %slice.267), channel_id=1, source_target_pairs={{0,1},{1,0},{2,3},{3,2},{4,5},{5,4},{6,7},{7,6},{8,9},{9,8},{10,11... | collective-permute-start | bytes 4718600 | tf_op jit(solution)/shard_map/ppermute | solution.py:326
  351.9 33.6 %collective-permute-start.13 = (bf16[2,2,2,96,768]{4,3,2,1,0:T(8,128)(2,1)}, bf16[2,2,2,96,768]{4,3,2,1,0:T(8,128)(2,1)}, u32[]{:S(2)}, u32[]{:S(2)}) collective-permute-start(bf16[2,2,2,96,768]{4,3,2,1,0:T(8,128)(2,1)} %bitcast.38), channel_id=1, source_target_pairs={{0,2},{2,0},{4,6},{6,4},{8,10},{10,8},{12,14},{14,12},{16,18},{18,... | collective-permute-start | bytes 3538952 | tf_op jit(solution)/shard_map/ppermute | solution.py:454
  396.4 33.1 %collective-permute-start.14 = (bf16[2,2,2,96,1536]{4,3,2,1,0:T(8,128)(2,1)}, bf16[2,2,2,96,1536]{4,3,2,1,0:T(8,128)(2,1)S(1)}, u32[]{:S(2)}, u32[]{:S(2)}) collective-permute-start(bf16[2,2,2,96,1536]{4,3,2,1,0:T(8,128)(2,1)} %bitcast.40), channel_id=1, source_target_pairs={{0,2},{2,0},{4,6},{6,4},{8,10},{10,8},{12,14},{14,12},{16,18},{18,... | collective-permute-start | bytes 7077896 | tf_op jit(solution)/shard_map/ppermute | solution.py:454
  396.6 46.0 %collective-permute-start.15 = (bf16[2,2,96,2048]{3,2,1,0:T(8,128)(2,1)}, bf16[2,2,96,2048]{3,2,1,0:T(8,128)(2,1)}, u32[]{:S(2)}, u32[]{:S(2)}) collective-permute-start(bf16[2,2,96,2048]{3,2,1,0:T(8,128)(2,1)} %bitcast.22), channel_id=1, source_target_pairs={{0,4},{2,6},{4,0},{6,2},{8,12},{10,14},{12,8},{14,10},{16,20},{18,... | collective-permute-start | bytes 4718600 | tf_op jit(solution)/shard_map/ppermute | solution.py:454
  398.1 48.4 %collective-permute-start.17 = (bf16[2,96,2048]{2,1,0:T(8,128)(2,1)}, bf16[2,96,2048]{2,1,0:T(8,128)(2,1)}, u32[]{:S(2)}, u32[]{:S(2)}) collective-permute-start(bf16[2,96,2048]{2,1,0:T(8,128)(2,1)} %bitcast.31), channel_id=1, source_target_pairs={{0,8},{2,10},{4,12},{6,14},{8,0},{10,2},{12,4},{14,6},{16,24},{18,... | collective-permute-start | bytes 2359304 | tf_op jit(solution)/shard_map/ppermute | solution.py:454
  398.6 47.9 %collective-permute-start.16 = (bf16[96,2048]{1,0:T(8,128)(2,1)}, bf16[96,2048]{1,0:T(8,128)(2,1)}, u32[]{:S(2)}, u32[]{:S(2)}) collective-permute-start(bf16[96,2048]{1,0:T(8,128)(2,1)} %bitcast.36), channel_id=1, source_target_pairs={{0,16},{2,18},{4,20},{6,22},{8,24},{10,26},{12,28},{14,30},{16,0},... | collective-permute-start | bytes 1179656 | tf_op jit(solution)/shard_map/ppermute | solution.py:454
  401.1 47.7 %collective-permute-start.18 = (bf16[2,2,96,768]{3,2,1,0:T(8,128)(2,1)}, bf16[2,2,96,768]{3,2,1,0:T(8,128)(2,1)}, u32[]{:S(2)}, u32[]{:S(2)}) collective-permute-start(bf16[2,2,96,768]{3,2,1,0:T(8,128)(2,1)} %get-tuple-element.625), channel_id=1, source_target_pairs={{0,8},{2,10},{4,12},{6,14},{8,0},{10,2},{12,4},{14,6},{16,24},{18,... | collective-permute-start | bytes 1769480 | tf_op jit(solution)/shard_map/ppermute | solution.py:454
  431.2 34.4 %collective-permute-start.19 = (bf16[2,2,96,1536]{3,2,1,0:T(8,128)(2,1)}, bf16[2,2,96,1536]{3,2,1,0:T(8,128)(2,1)}, u32[]{:S(2)}, u32[]{:S(2)}) collective-permute-start(bf16[2,2,96,1536]{3,2,1,0:T(8,128)(2,1)} %bitcast.44), channel_id=1, source_target_pairs={{0,4},{2,6},{4,0},{6,2},{8,12},{10,14},{12,8},{14,10},{16,20},{18,... | collective-permute-start | bytes 3538952 | tf_op jit(solution)/shard_map/ppermute | solution.py:454
  459.5 41.5 %collective-permute-start.22 = (bf16[2,2,2,96,1536]{4,3,2,1,0:T(8,128)(2,1)}, bf16[2,2,2,96,1536]{4,3,2,1,0:T(8,128)(2,1)S(1)}, u32[]{:S(2)}, u32[]{:S(2)}) collective-permute-start(bf16[2,2,2,96,1536]{4,3,2,1,0:T(8,128)(2,1)} %bitcast.197), channel_id=1, source_target_pairs={{0,2},{2,0},{4,6},{6,4},{8,10},{10,8},{12,14},{14,12},{16,18},{18,... | collective-permute-start | bytes 7077896 | tf_op jit(solution)/shard_map/ppermute | solution.py:454
  462.2 53.5 %collective-permute-start.23 = (bf16[2,96,768]{2,1,0:T(8,128)(2,1)}, bf16[2,96,768]{2,1,0:T(8,128)(2,1)S(1)}, u32[]{:S(2)}, u32[]{:S(2)}) collective-permute-start(bf16[2,96,768]{2,1,0:T(8,128)(2,1)} %bitcast.202), channel_id=1, source_target_pairs={{0,16},{2,18},{4,20},{6,22},{8,24},{10,26},{12,28},{14,30},{16,0},... | collective-permute-start | bytes 884744 | tf_op jit(solution)/shard_map/ppermute | solution.py:454
  462.6 37.9 %collective-permute-start.21 = (bf16[96,2048]{1,0:T(8,128)(2,1)}, bf16[96,2048]{1,0:T(8,128)(2,1)S(1)}, u32[]{:S(2)}, u32[]{:S(2)}) collective-permute-start(bf16[96,2048]{1,0:T(8,128)(2,1)} %bitcast.201), channel_id=1, source_target_pairs={{0,16},{2,18},{4,20},{6,22},{8,24},{10,26},{12,28},{14,30},{16,0},... | collective-permute-start | bytes 1179656 | tf_op jit(solution)/shard_map/ppermute | solution.py:454
  465.2 35.3 %collective-permute-start.20 = (bf16[2,96,2048]{2,1,0:T(8,128)(2,1)}, bf16[2,96,2048]{2,1,0:T(8,128)(2,1)S(1)}, u32[]{:S(2)}, u32[]{:S(2)}) collective-permute-start(bf16[2,96,2048]{2,1,0:T(8,128)(2,1)} %bitcast.199), channel_id=1, source_target_pairs={{0,8},{2,10},{4,12},{6,14},{8,0},{10,2},{12,4},{14,6},{16,24},{18,... | collective-permute-start | bytes 2359304 | tf_op jit(solution)/shard_map/ppermute | solution.py:454
  467.7 52.8 %collective-permute-start.24 = (bf16[2,96,1536]{2,1,0:T(8,128)(2,1)}, bf16[2,96,1536]{2,1,0:T(8,128)(2,1)}, u32[]{:S(2)}, u32[]{:S(2)}) collective-permute-start(bf16[2,96,1536]{2,1,0:T(8,128)(2,1)} %bitcast.61), channel_id=1, source_target_pairs={{0,8},{2,10},{4,12},{6,14},{8,0},{10,2},{12,4},{14,6},{16,24},{18,... | collective-permute-start | bytes 1769480 | tf_op jit(solution)/shard_map/ppermute | solution.py:454
  500.5 34.7 %collective-permute-start.26 = (bf16[512,1536]{1,0:T(8,128)(2,1)}, bf16[512,1536]{1,0:T(8,128)(2,1)}, u32[]{:S(2)}, u32[]{:S(2)}) collective-permute-start(bf16[512,1536]{1,0:T(8,128)(2,1)} %fusion.9), channel_id=1, source_target_pairs={{0,1},{1,0},{2,3},{3,2},{4,5},{5,4},{6,7},{7,6},{8,9},{9,8},{10,11... | collective-permute-start | bytes 4718600 | tf_op jit(solution)/shard_map/ppermute | solution.py:326
  (119 other events, 1301.4 us)

commit v4 on v3

--- a/solution.py
+++ b/solution.py
@@ -619,10 +619,10 @@
     grad_hidden, mlp_gain_part, mid_rows = line.run(middle_grads, own, arrived)
     grad_mid = gather_rows(mid_rows)
     down.step()
-    gate_sum.step()
     last_own, last_arrived = scatter_rows(
         line, lambda a, b, m, w: dot_nn(m[a:b], w), (active, down_weight), LEN
     )
+    gate_sum.step()
     up_sum.step()
 
     grad_mid, grad_mixed = line.run(
@@ -664,13 +664,13 @@
 
     grad_forget = line.run(forget_term, decay_a, decay_b)
     sum_a.step()
+    up_sum.arrive()
     values = (grads_a, grads_b, grad_forget)
     if two_devices():
         sent = line.run(lambda *v: normed_term(half, LEN, *v).astype(jnp.bfloat16), *values)
         arrived = swap(sent)
-    up_sum.arrive()
+    sum_b.step()
     gate_sum.arrive()
-    sum_b.step()
     if two_devices():
         own = line.run(lambda *v: normed_term(0, half, *v), *values)
     else:

time: 605 us -> 568 us (0.939)
  waiting for transfers between devices: 155 us -> 115 us
    ppermute x24, waiting for transfers between devices: 72.7 us -> 31.3 us  [exchange(): return lax.ppermute(sent, 'dp', [(i, i ^ mask) for i in range(self.size)])]
    unnamed x233 -> x241, local copies, waits for them, and re-layouts: 39.8 us -> 41.8 us
  transfers between devices with their start and end apart: 37 -> 37, of which waited for: 14 -> 13; matrix products, arithmetic and copies ran while one was open for 20% -> 22% of each run, Pallas kernels for 27% -> 29%
where the time goes in v4:
time: 568 us; the launch traced here: 561 us
  Pallas kernels  176 us (31%)
  waiting for transfers between devices  115 us (20%)
  matrix products  114 us (20%)
  local copies, waits for them, and re-layouts  70.5 us (12%)
  other arithmetic  47.9 us (8%)
  starting transfers between devices  35.7 us (6%)
    ppermute x9, waiting for transfers between devices, swap(): return lax.ppermute(rows, 'tensor', [(0, 1), (1, 0)])  72.1 us
    dot_general x9, matrix products, dot_nn(): lax.dot_general(left, right, (((1,), (0,)), ((), ())), preferred_element_...  56.6 us
    dot_general x10, matrix products, dot_nt(): lax.dot_general(left, right, (((1,), (1,)), ((), ())), preferred_element_...  54.5 us
    pallas_call x2, Pallas kernels, attention_backward(): pl.pallas_call(backward_kernel, grid_spec=pltpu.PrefetchScalarGridSpec(nu...  53.4 us
    pallas_call x6, Pallas kernels, weight_halves(): pl.pallas_call(halves_kernel, grid_spec=pltpu.PrefetchScalarGridSpec(num_...  46.2 us
    unnamed x241, local copies, waits for them, and re-layouts  41.8 us
    pallas_call x2, Pallas kernels, attention_forward(): pl.pallas_call(lambda *refs: forward_kernel(slot, *refs), grid_spec=pltpu...  40.2 us
    pallas_call x18, Pallas kernels, halve(): pl.pallas_call(halve_kernel, grid_spec=pltpu.PrefetchScalarGridSpec(num_s...  35.8 us
  transfers between devices with their start and end apart: 37, of which 13 were waited for; matrix products, arithmetic and copies ran while one was open for 22% of the time, Pallas kernels for 29%

profile of v4, /device:TPU:0, one launch (start us, length us, event | category | flops | bytes accessed | tf_op | source)
XLA Modules:
  0.0 561.2 jit_solution(3383304202496444914)
XLA Ops:
  23.9 18.9 %collective-permute-done = bf16[512,1536]{1,0:T(8,128)(2,1)} collective-permute-done((bf16[512,1536]{1,0:T(8,128)(2,1)}, bf16[512,1536]{1,0:T(8,128)(2,1)}, u32[]{:S(2)}, u32[]{:S(2)}) %collective-permute-start) | collective-permute-done | bytes 1572896 | tf_op jit(solution)/shard_map/ppermute | solution.py:326
  52.0 15.1 %convolution_convert_fusion.refs_1_.qkvz_ref = bf16[1024,3072]{1,0:T(8,128)(2,1)} fusion(bf16[1024,1536]{1,0:T(8,128)(2,1)} %copy-done.1, bf16[1536,3072]{1,0:T(8,128)(2,1)} %copy-done.96), kind=kOutput, calls=%fused_computation.9 | convolution fusion | flops 9666822144 | bytes 18874368 | tf_op jit(solution)/shard_map/dot_general | solution.py:19
  67.1 21.2 %attention_forward.2 = (bf16[1024,768]{1,0:T(8,128)(2,1)}, f32[1024,768]{1,0:T(8,128)}, f32[6,1024,2]{2,1,0:T(8,128)}) custom-call(s32[3]{0:T(128)} %pad_add_fusion.refs_0_.where_ref, bf16[1024,3072]{1,0:T(8,128)(2,1)} %convolution_convert_fusion.refs_1_.qkvz_ref, f32[6,1024,2]{2,1,0:T(8,128)} %bitcast.203), custom_call_target="tpu_custom_call" | custom-call | flops 1000000 | bytes 1000000 | tf_op jit(solution)/shard_map/attention_forward/pallas_call | solution.py:250
  92.8 19.0 %attention_forward.3 = (bf16[1024,768]{1,0:T(8,128)(2,1)}, f32[1024,768]{1,0:T(8,128)}, f32[6,1024,2]{2,1,0:T(8,128)}) custom-call(s32[3]{0:T(128)} %pad_add_fusion.refs_0_.where_ref, bf16[1024,3072]{1,0:T(8,128)(2,1)} %convolution_convert_fusion.refs_1_.qkvz_ref, ...), custom_call_target="tpu_custom_call", output_to_operand_aliasing={{0}: (3, {}), {1}: (4, {}), {2}: (5, {})} | custom-call | flops 1000000 | bytes 1000000 | tf_op jit(solution)/shard_map/attention_forward/pallas_call | solution.py:250
  114.3 13.7 %collective-permute-done.2 = bf16[512,1536]{1,0:T(8,128)(2,1)S(1)} collective-permute-done((bf16[512,1536]{1,0:T(8,128)(2,1)}, bf16[512,1536]{1,0:T(8,128)(2,1)S(1)}, u32[]{:S(2)}, u32[]{:S(2)}) %collective-permute-start.2) | collective-permute-done | bytes 1572896 | tf_op jit(solution)/shard_map/ppermute | solution.py:326
  132.2 8.3 %convolution_convert_fusion.1 = bf16[1024,2048]{1,0:T(8,128)(2,1)} fusion(bf16[1024,1536]{1,0:T(8,128)(2,1)S(1)} %pad_maximum_fusion.1.left_ref, bf16[2048,1536]{1,0:T(8,128)(2,1)S(1)} %bitcast.218), kind=kOutput, calls=%fused_computation.15 | convolution fusion | flops 6444548096 | bytes 13631488 | tf_op jit(solution)/shard_map/dot_general | solution.py:25
  140.6 24.7 %collective-permute-done.3 = bf16[512,1536]{1,0:T(8,128)(2,1)S(1)} collective-permute-done((bf16[512,1536]{1,0:T(8,128)(2,1)S(1)}, bf16[512,1536]{1,0:T(8,128)(2,1)S(1)}, u32[]{:S(2)}, u32[]{:S(2)}) %collective-permute-start.3) | collective-permute-done | bytes 1572896 | tf_op jit(solution)/shard_map/ppermute | solution.py:326
  165.4 8.8 %fusion.47 = f32[1024,2048]{1,0:T(8,128)} fusion(bf16[1024,1536]{1,0:T(8,128)(2,1)S(1)} %constant_dynamic-update-slice_fusion.left_ref, bf16[1536,2048]{1,0:T(8,128)(2,1)S(1)} %bitcast.216), kind=kOutput, calls=%fused_computation.176 | convolution fusion | flops 6442450944 | bytes 17825792 | tf_op jit(solution)/shard_map/dot_general | solution.py:19
  174.3 15.3 %fusion.2 = (bf16[1024,2048]{1,0:T(8,128)(2,1)S(1)}, bf16[1024,2048]{1,0:T(8,128)(2,1)}, bf16[1024,2048]{1,0:T(8,128)(2,1)S(1)}) fusion(bf16[1024,2048]{1,0:T(8,128)(2,1)} %convolution_convert_fusion.1, f32[1024,2048]{1,0:T(8,128)} %fusion.47, bf16[1024,1536]{1,0:T(8,128)(2,1)S(1)} %constant_dynamic-update-slice_fusion.left_ref, bf16[1536,2048]{1,0:T(8,128)(2,1)} %param.27), kind=kOutput, calls=%fused_computation.4 | convolution fusion | flops 6478102528 | bytes 34603008 | tf_op jit(solution)/shard_map/dot_general | solution.py:19
  189.6 13.0 %fusion.48 = f32[1024,1536]{1,0:T(8,128)} fusion(bf16[1024,2048]{1,0:T(8,128)(2,1)S(1)} %get-tuple-element.479.right_ref, bf16[1536,2048]{1,0:T(8,128)(2,1)} %param.26), kind=kOutput, calls=%fused_computation.177 | convolution fusion | flops 6442450944 | bytes 16777216 | tf_op jit(solution)/shard_map/dot_general | solution.py:25
  202.6 10.4 %convolution_add_fusion = f32[1024,1536]{1,0:T(8,128)S(1)} fusion(f32[1024,1536]{1,0:T(8,128)} %fusion.48, bf16[1024,2048]{1,0:T(8,128)(2,1)S(1)} %get-tuple-element.485.right_ref, bf16[1536,2048]{1,0:T(8,128)(2,1)} %param.27), kind=kOutput, calls=%fused_computation.10 | convolution fusion | flops 6444023808 | bytes 23068672 | tf_op jit(solution)/shard_map/dot_general | solution.py:25
  221.6 9.2 %weight_halves.6 = (bf16[8,96,2048]{2,1,0:T(8,128)(2,1)S(1)}, bf16[8,96,2048]{2,1,0:T(8,128)(2,1)}) custom-call(s32[1]{0:T(128)} %bitcast.3.mine_ref, bf16[1024,1536]{1,0:T(8,128)(2,1)S(1)} %copy-done.7, bf16[1024,2048]{1,0:T(8,128)(2,1)S(1)} %copy-done.22), custom_call_target="tpu_custom_call" | custom-call | flops 1000000 | bytes 1000000 | tf_op jit(solution)/shard_map/weight_halves/pallas_call | solution.py:388
  238.5 9.3 %weight_halves.7 = (bf16[8,96,2048]{2,1,0:T(8,128)(2,1)S(1)}, bf16[8,96,2048]{2,1,0:T(8,128)(2,1)}) custom-call(s32[1]{0:T(128)} %bitcast.3.mine_ref, bf16[1024,1536]{1,0:T(8,128)(2,1)S(1)} %copy-done.5, bf16[1024,2048]{1,0:T(8,128)(2,1)S(1)} %copy-done.27), custom_call_target="tpu_custom_call" | custom-call | flops 1000000 | bytes 1000000 | tf_op jit(solution)/shard_map/weight_halves/pallas_call | solution.py:388
  247.8 9.3 %weight_halves.8 = (bf16[8,96,2048]{2,1,0:T(8,128)(2,1)S(1)}, bf16[8,96,2048]{2,1,0:T(8,128)(2,1)}) custom-call(s32[1]{0:T(128)} %bitcast.3.mine_ref, bf16[1024,1536]{1,0:T(8,128)(2,1)S(1)} %copy-done.5, bf16[1024,2048]{1,0:T(8,128)(2,1)S(1)} %copy-done.25), custom_call_target="tpu_custom_call" | custom-call | flops 1000000 | bytes 1000000 | tf_op jit(solution)/shard_map/weight_halves/pallas_call | solution.py:388
  273.1 8.9 %fusion.49 = f32[1024,1536]{1,0:T(8,128)S(1)} fusion(bf16[1024,2048]{1,0:T(8,128)(2,1)S(1)} %copy-done.23, bf16[2048,1536]{1,0:T(8,128)(2,1)} %param.28), kind=kOutput, calls=%fused_computation.178 | convolution fusion | flops 6442450944 | bytes 16777216 | tf_op jit(solution)/shard_map/dot_general | solution.py:19
  293.6 9.7 %collective-permute-done.8 = bf16[512,1536]{1,0:T(8,128)(2,1)} collective-permute-done((bf16[512,1536]{1,0:T(8,128)(2,1)}, bf16[512,1536]{1,0:T(8,128)(2,1)}, u32[]{:S(2)}, u32[]{:S(2)}) %collective-permute-start.8) | collective-permute-done | bytes 1572896 | tf_op jit(solution)/shard_map/ppermute | solution.py:326
  322.7 26.7 %attention_backward.2 = (bf16[1024,1536]{1,0:T(8,128)(2,1)}, f32[3,1024,2]{2,1,0:T(8,128)}) custom-call(s32[3]{0:T(128)} %pad_add_fusion.refs_0_.where_ref, bf16[1024,3072]{1,0:T(8,128)(2,1)} %convolution_convert_fusion.refs_1_.qkvz_ref, bf16[1024,768]{1,0:T(8,128)(2,1)} %convolution_convert_fusion.3.gm_ref, f32[1024,768]{1,0:T(8,128)} %get-tuple-element.548.att_ref, ...), custom_call_target="tpu_custom_call" | custom-call | flops 7000000000 | bytes 10000000 | tf_op jit(solution)/shard_map/attention_backward/pallas_call | solution.py:277
  358.3 7.3 %weight_halves.10 = (bf16[8,96,1536]{2,1,0:T(8,128)(2,1)S(1)}, bf16[8,96,1536]{2,1,0:T(8,128)(2,1)}) custom-call(s32[1]{0:T(128)} %bitcast.3.mine_ref, bf16[1024,1536]{1,0:T(8,128)(2,1)S(1)} %copy-done.2, bf16[1024,1536]{1,0:T(8,128)(2,1)S(1)} %copy-done.28), custom_call_target="tpu_custom_call" | custom-call | flops 1000000 | bytes 1000000 | tf_op jit(solution)/shard_map/weight_halves/pallas_call | solution.py:388
  371.0 26.7 %attention_backward.3 = (bf16[1024,1536]{1,0:T(8,128)(2,1)}, f32[3,1024,2]{2,1,0:T(8,128)}) custom-call(s32[3]{0:T(128)} %pad_add_fusion.refs_0_.where_ref, bf16[1024,3072]{1,0:T(8,128)(2,1)} %convolution_convert_fusion.refs_1_.qkvz_ref, bf16[1024,768]{1,0:T(8,128)(2,1)} %convolution_convert_fusion.3.gm_ref, f32[1024,768]{1,0:T(8,128)} %get-tuple-element.548.att_ref, ...), custom_call_target="tpu_custom_call" | custom-call | flops 7000000000 | bytes 10000000 | tf_op jit(solution)/shard_map/attention_backward/pallas_call | solution.py:277
  405.3 6.5 %weight_halves.11 = (bf16[8,96,1536]{2,1,0:T(8,128)(2,1)S(1)}, bf16[8,96,1536]{2,1,0:T(8,128)(2,1)S(1)}) custom-call(s32[1]{0:T(128)} %bitcast.3.mine_ref, bf16[1024,1536]{1,0:T(8,128)(2,1)S(1)} %copy-done.3, bf16[1024,1536]{1,0:T(8,128)(2,1)S(1)} %copy-done.30), custom_call_target="tpu_custom_call" | custom-call | flops 1000000 | bytes 1000000 | tf_op jit(solution)/shard_map/weight_halves/pallas_call | solution.py:388
  438.4 16.2 %collective-permute-done.20 = bf16[2,96,2048]{2,1,0:T(8,128)(2,1)} collective-permute-done((bf16[2,96,2048]{2,1,0:T(8,128)(2,1)}, bf16[2,96,2048]{2,1,0:T(8,128)(2,1)}, u32[]{:S(2)}, u32[]{:S(2)}) %collective-permute-start.20) | collective-permute-done | bytes 786464 | tf_op jit(solution)/shard_map/ppermute | solution.py:454
  488.6 7.7 %collective-permute-done.25 = bf16[2,2,96,1536]{3,2,1,0:T(8,128)(2,1)} collective-permute-done((bf16[2,2,96,1536]{3,2,1,0:T(8,128)(2,1)}, bf16[2,2,96,1536]{3,2,1,0:T(8,128)(2,1)}, u32[]{:S(2)}, u32[]{:S(2)}) %collective-permute-start.25) | collective-permute-done | bytes 1179680 | tf_op jit(solution)/shard_map/ppermute | solution.py:454
  536.0 9.7 %collective-permute-done.34 = f32[15,1536]{1,0:T(8,128)S(1)} collective-permute-done((f32[15,1536]{1,0:T(8,128)S(1)}, f32[15,1536]{1,0:T(8,128)S(1)}, u32[]{:S(2)}, u32[]{:S(2)}) %collective-permute-start.34) | collective-permute-done | bytes 92192 | tf_op jit(solution)/shard_map/ppermute | solution.py:488
  553.1 6.1 %slice_reduce_fusion = (f32[96,6,128]{2,1,0:T(8,128)S(1)}, f32[96,6,128]{2,1,0:T(8,128)S(1)}, f32[96,6,128]{2,1,0:T(8,128)S(1)}, f32[96,6,128]{2,1,0:T(8,128)S(1)}) fusion(f32[96,6,4,128]{3,2,1,0:T(4,128)} %reshape.466), kind=kLoop, calls=%fused_computation.114 | loop fusion | bytes 2359296 | tf_op jit(solution)/shard_map/slice | solution.py:726
  (409 shorter events, 236.4 us)
Async XLA Ops:
  5.1 37.7 %collective-permute-start = (bf16[512,1536]{1,0:T(8,128)(2,1)}, bf16[512,1536]{1,0:T(8,128)(2,1)}, u32[]{:S(2)}, u32[]{:S(2)}) collective-permute-start(bf16[512,1536]{1,0:T(8,128)(2,1)} %multiply_convert_fusion.2), channel_id=1, source_target_pairs={{0,1},{1,0},{2,3},{3,2},{4,5},{5,4},{6,7},{7,6},{8,9},{9,8},{10,11... | collective-permute-start | bytes 4718600 | tf_op jit(solution)/shard_map/ppermute | solution.py:326
  47.6 40.8 %collective-permute-start.1 = (bf16[512,1536]{1,0:T(8,128)(2,1)}, bf16[512,1536]{1,0:T(8,128)(2,1)}, u32[]{:S(2)}, u32[]{:S(2)}) collective-permute-start(bf16[512,1536]{1,0:T(8,128)(2,1)} %convert_element_type.100), channel_id=1, source_target_pairs={{0,1},{1,0},{2,3},{3,2},{4,5},{5,4},{6,7},{7,6},{8,9},{9,8},{10,11... | collective-permute-start | bytes 4718600 | tf_op jit(solution)/shard_map/ppermute | solution.py:326
  92.8 35.2 %collective-permute-start.2 = (bf16[512,1536]{1,0:T(8,128)(2,1)}, bf16[512,1536]{1,0:T(8,128)(2,1)S(1)}, u32[]{:S(2)}, u32[]{:S(2)}) collective-permute-start(bf16[512,1536]{1,0:T(8,128)(2,1)} %convolution_convert_fusion.2), channel_id=1, source_target_pairs={{0,1},{1,0},{2,3},{3,2},{4,5},{5,4},{6,7},{7,6},{8,9},{9,8},{10,11... | collective-permute-start | bytes 4718600 | tf_op jit(solution)/shard_map/ppermute | solution.py:326
  131.1 34.2 %collective-permute-start.3 = (bf16[512,1536]{1,0:T(8,128)(2,1)S(1)}, bf16[512,1536]{1,0:T(8,128)(2,1)S(1)}, u32[]{:S(2)}, u32[]{:S(2)}) collective-permute-start(bf16[512,1536]{1,0:T(8,128)(2,1)S(1)} %multiply_convert_fusion.1), channel_id=1, source_target_pairs={{0,1},{1,0},{2,3},{3,2},{4,5},{5,4},{6,7},{7,6},{8,9},{9,8},{10,11... | collective-permute-start | bytes 4718600 | tf_op jit(solution)/shard_map/ppermute | solution.py:326
  216.9 40.8 %collective-permute-start.4 = (bf16[512,1536]{1,0:T(8,128)(2,1)}, bf16[512,1536]{1,0:T(8,128)(2,1)}, u32[]{:S(2)}, u32[]{:S(2)}) collective-permute-start(bf16[512,1536]{1,0:T(8,128)(2,1)} %slice.268), channel_id=1, source_target_pairs={{0,1},{1,0},{2,3},{3,2},{4,5},{5,4},{6,7},{7,6},{8,9},{9,8},{10,11... | collective-permute-start | bytes 4718600 | tf_op jit(solution)/shard_map/ppermute | solution.py:326
  232.4 35.8 %collective-permute-start.5 = (bf16[2,2,2,96,2048]{4,3,2,1,0:T(8,128)(2,1)}, bf16[2,2,2,96,2048]{4,3,2,1,0:T(8,128)(2,1)}, u32[]{:S(2)}, u32[]{:S(2)}) collective-permute-start(bf16[2,2,2,96,2048]{4,3,2,1,0:T(8,128)(2,1)} %bitcast.5), channel_id=1, source_target_pairs={{0,2},{2,0},{4,6},{6,4},{8,10},{10,8},{12,14},{14,12},{16,18},{18,... | collective-permute-start | bytes 9437192 | tf_op jit(solution)/shard_map/ppermute | solution.py:454
  257.1 33.1 %collective-permute-start.7 = (bf16[2,2,2,96,2048]{4,3,2,1,0:T(8,128)(2,1)}, bf16[2,2,2,96,2048]{4,3,2,1,0:T(8,128)(2,1)S(1)}, u32[]{:S(2)}, u32[]{:S(2)}) collective-permute-start(bf16[2,2,2,96,2048]{4,3,2,1,0:T(8,128)(2,1)} %bitcast.18), channel_id=1, source_target_pairs={{0,2},{2,0},{4,6},{6,4},{8,10},{10,8},{12,14},{14,12},{16,18},{18,... | collective-permute-start | bytes 9437192 | tf_op jit(solution)/shard_map/ppermute | solution.py:454
  266.7 36.6 %collective-permute-start.8 = (bf16[512,1536]{1,0:T(8,128)(2,1)}, bf16[512,1536]{1,0:T(8,128)(2,1)}, u32[]{:S(2)}, u32[]{:S(2)}) collective-permute-start(bf16[512,1536]{1,0:T(8,128)(2,1)} %get-tuple-element.525), channel_id=1, source_target_pairs={{0,1},{1,0},{2,3},{3,2},{4,5},{5,4},{6,7},{7,6},{8,9},{9,8},{10,11... | collective-permute-start | bytes 4718600 | tf_op jit(solution)/shard_map/ppermute | solution.py:326
  271.5 40.7 %collective-permute-start.9 = (bf16[2,2,96,2048]{3,2,1,0:T(8,128)(2,1)S(1)}, bf16[2,2,96,2048]{3,2,1,0:T(8,128)(2,1)S(1)}, u32[]{:S(2)}, u32[]{:S(2)}) collective-permute-start(bf16[2,2,96,2048]{3,2,1,0:T(8,128)(2,1)S(1)} %bitcast.196), channel_id=1, source_target_pairs={{0,4},{2,6},{4,0},{6,2},{8,12},{10,14},{12,8},{14,10},{16,20},{18,... | collective-permute-start | bytes 4718600 | tf_op jit(solution)/shard_map/ppermute | solution.py:454
  305.4 43.9 %collective-permute-start.11 = (bf16[2,2,96,2048]{3,2,1,0:T(8,128)(2,1)}, bf16[2,2,96,2048]{3,2,1,0:T(8,128)(2,1)}, u32[]{:S(2)}, u32[]{:S(2)}) collective-permute-start(bf16[2,2,96,2048]{3,2,1,0:T(8,128)(2,1)} %bitcast.16), channel_id=1, source_target_pairs={{0,4},{2,6},{4,0},{6,2},{8,12},{10,14},{12,8},{14,10},{16,20},{18,... | collective-permute-start | bytes 4718600 | tf_op jit(solution)/shard_map/ppermute | solution.py:454
  307.0 42.4 %collective-permute-start.10 = (bf16[512,1536]{1,0:T(8,128)(2,1)}, bf16[512,1536]{1,0:T(8,128)(2,1)}, u32[]{:S(2)}, u32[]{:S(2)}) collective-permute-start(bf16[512,1536]{1,0:T(8,128)(2,1)} %slice.267), channel_id=1, source_target_pairs={{0,1},{1,0},{2,3},{3,2},{4,5},{5,4},{6,7},{7,6},{8,9},{9,8},{10,11... | collective-permute-start | bytes 4718600 | tf_op jit(solution)/shard_map/ppermute | solution.py:326
  321.1 33.6 %collective-permute-start.13 = (bf16[2,2,2,96,768]{4,3,2,1,0:T(8,128)(2,1)}, bf16[2,2,2,96,768]{4,3,2,1,0:T(8,128)(2,1)}, u32[]{:S(2)}, u32[]{:S(2)}) collective-permute-start(bf16[2,2,2,96,768]{4,3,2,1,0:T(8,128)(2,1)} %bitcast.38), channel_id=1, source_target_pairs={{0,2},{2,0},{4,6},{6,4},{8,10},{10,8},{12,14},{14,12},{16,18},{18,... | collective-permute-start | bytes 3538952 | tf_op jit(solution)/shard_map/ppermute | solution.py:454
  321.1 30.6 %collective-permute-start.12 = (bf16[2,96,2048]{2,1,0:T(8,128)(2,1)}, bf16[2,96,2048]{2,1,0:T(8,128)(2,1)}, u32[]{:S(2)}, u32[]{:S(2)}) collective-permute-start(bf16[2,96,2048]{2,1,0:T(8,128)(2,1)} %bitcast.27), channel_id=1, source_target_pairs={{0,8},{2,10},{4,12},{6,14},{8,0},{10,2},{12,4},{14,6},{16,24},{18,... | collective-permute-start | bytes 2359304 | tf_op jit(solution)/shard_map/ppermute | solution.py:454
  365.6 32.1 %collective-permute-start.14 = (bf16[2,2,2,96,1536]{4,3,2,1,0:T(8,128)(2,1)}, bf16[2,2,2,96,1536]{4,3,2,1,0:T(8,128)(2,1)S(1)}, u32[]{:S(2)}, u32[]{:S(2)}) collective-permute-start(bf16[2,2,2,96,1536]{4,3,2,1,0:T(8,128)(2,1)} %bitcast.40), channel_id=1, source_target_pairs={{0,2},{2,0},{4,6},{6,4},{8,10},{10,8},{12,14},{14,12},{16,18},{18,... | collective-permute-start | bytes 7077896 | tf_op jit(solution)/shard_map/ppermute | solution.py:454
  365.8 46.0 %collective-permute-start.15 = (bf16[2,2,96,2048]{3,2,1,0:T(8,128)(2,1)}, bf16[2,2,96,2048]{3,2,1,0:T(8,128)(2,1)}, u32[]{:S(2)}, u32[]{:S(2)}) collective-permute-start(bf16[2,2,96,2048]{3,2,1,0:T(8,128)(2,1)} %bitcast.22), channel_id=1, source_target_pairs={{0,4},{2,6},{4,0},{6,2},{8,12},{10,14},{12,8},{14,10},{16,20},{18,... | collective-permute-start | bytes 4718600 | tf_op jit(solution)/shard_map/ppermute | solution.py:454
  366.4 49.3 %collective-permute-start.17 = (bf16[2,96,2048]{2,1,0:T(8,128)(2,1)}, bf16[2,96,2048]{2,1,0:T(8,128)(2,1)}, u32[]{:S(2)}, u32[]{:S(2)}) collective-permute-start(bf16[2,96,2048]{2,1,0:T(8,128)(2,1)} %bitcast.31), channel_id=1, source_target_pairs={{0,8},{2,10},{4,12},{6,14},{8,0},{10,2},{12,4},{14,6},{16,24},{18,... | collective-permute-start | bytes 2359304 | tf_op jit(solution)/shard_map/ppermute | solution.py:454
  366.8 48.8 %collective-permute-start.16 = (bf16[96,2048]{1,0:T(8,128)(2,1)}, bf16[96,2048]{1,0:T(8,128)(2,1)}, u32[]{:S(2)}, u32[]{:S(2)}) collective-permute-start(bf16[96,2048]{1,0:T(8,128)(2,1)} %bitcast.36), channel_id=1, source_target_pairs={{0,16},{2,18},{4,20},{6,22},{8,24},{10,26},{12,28},{14,30},{16,0},... | collective-permute-start | bytes 1179656 | tf_op jit(solution)/shard_map/ppermute | solution.py:454
  369.4 48.6 %collective-permute-start.18 = (bf16[2,2,96,768]{3,2,1,0:T(8,128)(2,1)}, bf16[2,2,96,768]{3,2,1,0:T(8,128)(2,1)}, u32[]{:S(2)}, u32[]{:S(2)}) collective-permute-start(bf16[2,2,96,768]{3,2,1,0:T(8,128)(2,1)} %get-tuple-element.625), channel_id=1, source_target_pairs={{0,8},{2,10},{4,12},{6,14},{8,0},{10,2},{12,4},{14,6},{16,24},{18,... | collective-permute-start | bytes 1769480 | tf_op jit(solution)/shard_map/ppermute | solution.py:454
  399.4 35.4 %collective-permute-start.19 = (bf16[2,2,96,1536]{3,2,1,0:T(8,128)(2,1)}, bf16[2,2,96,1536]{3,2,1,0:T(8,128)(2,1)}, u32[]{:S(2)}, u32[]{:S(2)}) collective-permute-start(bf16[2,2,96,1536]{3,2,1,0:T(8,128)(2,1)} %bitcast.44), channel_id=1, source_target_pairs={{0,4},{2,6},{4,0},{6,2},{8,12},{10,14},{12,8},{14,10},{16,20},{18,... | collective-permute-start | bytes 3538952 | tf_op jit(solution)/shard_map/ppermute | solution.py:454
  429.2 37.6 %collective-permute-start.21 = (bf16[2,2,2,96,1536]{4,3,2,1,0:T(8,128)(2,1)}, bf16[2,2,2,96,1536]{4,3,2,1,0:T(8,128)(2,1)S(1)}, u32[]{:S(2)}, u32[]{:S(2)}) collective-permute-start(bf16[2,2,2,96,1536]{4,3,2,1,0:T(8,128)(2,1)} %bitcast.195), channel_id=1, source_target_pairs={{0,2},{2,0},{4,6},{6,4},{8,10},{10,8},{12,14},{14,12},{16,18},{18,... | collective-permute-start | bytes 7077896 | tf_op jit(solution)/shard_map/ppermute | solution.py:454
  431.9 47.7 %collective-permute-start.23 = (bf16[2,96,768]{2,1,0:T(8,128)(2,1)}, bf16[2,96,768]{2,1,0:T(8,128)(2,1)S(1)}, u32[]{:S(2)}, u32[]{:S(2)}) collective-permute-start(bf16[2,96,768]{2,1,0:T(8,128)(2,1)} %bitcast.200), channel_id=1, source_target_pairs={{0,16},{2,18},{4,20},{6,22},{8,24},{10,26},{12,28},{14,30},{16,0},... | collective-permute-start | bytes 884744 | tf_op jit(solution)/shard_map/ppermute | solution.py:454
  432.3 36.2 %collective-permute-start.22 = (bf16[96,2048]{1,0:T(8,128)(2,1)}, bf16[96,2048]{1,0:T(8,128)(2,1)S(1)}, u32[]{:S(2)}, u32[]{:S(2)}) collective-permute-start(bf16[96,2048]{1,0:T(8,128)(2,1)} %bitcast.198), channel_id=1, source_target_pairs={{0,16},{2,18},{4,20},{6,22},{8,24},{10,26},{12,28},{14,30},{16,0},... | collective-permute-start | bytes 1179656 | tf_op jit(solution)/shard_map/ppermute | solution.py:454
  436.9 47.4 %collective-permute-start.24 = (bf16[2,96,1536]{2,1,0:T(8,128)(2,1)}, bf16[2,96,1536]{2,1,0:T(8,128)(2,1)}, u32[]{:S(2)}, u32[]{:S(2)}) collective-permute-start(bf16[2,96,1536]{2,1,0:T(8,128)(2,1)} %bitcast.61), channel_id=1, source_target_pairs={{0,8},{2,10},{4,12},{6,14},{8,0},{10,2},{12,4},{14,6},{16,24},{18,... | collective-permute-start | bytes 1769480 | tf_op jit(solution)/shard_map/ppermute | solution.py:454
  466.2 32.6 %collective-permute-start.26 = (bf16[512,1536]{1,0:T(8,128)(2,1)}, bf16[512,1536]{1,0:T(8,128)(2,1)}, u32[]{:S(2)}, u32[]{:S(2)}) collective-permute-start(bf16[512,1536]{1,0:T(8,128)(2,1)} %fusion.9), channel_id=1, source_target_pairs={{0,1},{1,0},{2,3},{3,2},{4,5},{5,4},{6,7},{7,6},{8,9},{9,8},{10,11... | collective-permute-start | bytes 4718600 | tf_op jit(solution)/shard_map/ppermute | solution.py:326
  (123 other events, 1252.9 us)
